TPU v7x, 32 devices: a whole 2x2x4 slice. The times are simulated.
32 devices in a mesh: seq: 8 (over z, x), tp: 4 (over y, core).
Axes of the slice: x: 2, y: 2, z: 4, core: 2. Of those that a mesh axis runs over, the one named last changes fastest.
Arguments:
- hidden_states: bfloat16 [2048, 3584], P('seq', 'tp'), may hold values from -6 to 6
- queries: bfloat16 [2048, 3584], P('seq', 'tp'), may hold values from -6 to 6
- key_weight: bfloat16 [3584, 512], P(None, 'tp'), may hold values from -0.09375 to 0.09375
- value_weight: bfloat16 [3584, 512], P(None, 'tp'), may hold values from -0.09375 to 0.09375
- output_weight: bfloat16 [3584, 3584], P('tp'), may hold values from -1.5 to 1.5
- prefix_keys: bfloat16 [2048, 512], P('seq', 'tp'), may hold values from -64 to 64
- prefix_values: bfloat16 [2048, 512], P('seq', 'tp'), may hold values from -6 to 6
- reads: int32 [8, 16], replicated, may hold values from 0 to 31, as said below
- out_grad: bfloat16 [2048, 3584], P('seq', 'tp'), may hold values from -6 to 6
Outputs:
- layer_output: bfloat16 [2048, 3584], P('seq', 'tp')
- prefix_key_grad: float32 [2048, 512], P('seq', 'tp')
- prefix_value_grad: float32 [2048, 512], P('seq', 'tp')
Inputs may be any that keep to these rules, and one draw needn't show every extreme that they name: Entry l of a row is the row's node at depth l of a prefix tree, one of the blocks l * (2) to (l + 1) * 2 - 1; two rows that share a node share all its ancestors, and all rows share the root. Block b is held by index b // 4 of seq; every row names exactly 2 blocks of each index that it reads from.
All inputs are finite; a program needn't handle non-finite values.
Results may differ from a plain program's by a relative error of at most 0.0095.
Values may be sent and summed in bfloat16 or wider, within the bound.
No kernel may reach another device: no remote copies, remote signals or barrier semaphores. Data moves between devices by JAX's collectives and lax.ppermute only.
A program may use at most 128 MiB of HBM per device.

v0:
```python
import functools

import jax
import jax.numpy as jnp
from jax import lax
from jax.experimental import pallas as pl
from jax.experimental.pallas import tpu as pltpu
from jax.sharding import PartitionSpec as P


HD = 128
PBLK = 64
LOG2E = 1.4426950408889634
F32 = jnp.float32
BF16 = jnp.bfloat16
VMEM = pl.BlockSpec(memory_space=pltpu.VMEM)
SMEM = pl.BlockSpec(memory_space=pltpu.SMEM)
ANY = pl.BlockSpec(memory_space=pl.ANY)


def dot(a, b, dims):
    return lax.dot_general(a, b, (dims, ((), ())), preferred_element_type=F32)


def cost(flops, nbytes, trans=0):
    return pl.CostEstimate(flops=int(flops), bytes_accessed=int(nbytes), transcendentals=int(trans))


def pick_kernel(n, cap, here, me_ref, reads_ref, keys_ref, values_ref, *outs):
    me = me_ref[0]
    for k in range(n):
        for r in range(cap):
            block = reads_ref[me ^ k, cap * me + r] - here * me
            rows = pl.ds(pl.multiple_of(block * PBLK, PBLK), PBLK)
            outs[k][r * PBLK:(r + 1) * PBLK, :HD] = keys_ref[rows, :]
            outs[k][r * PBLK:(r + 1) * PBLK, HD:] = values_ref[rows, :]


def place_kernel(n, cap, here, me_ref, reads_ref, *refs):
    parts, keys_ref, values_ref = refs[:n], refs[n], refs[n + 1]
    me = me_ref[0]
    keys_ref[...] = jnp.zeros_like(keys_ref)
    values_ref[...] = jnp.zeros_like(values_ref)
    for k in range(n):
        for r in range(cap):
            block = reads_ref[me ^ k, cap * me + r] - here * me
            rows = pl.ds(pl.multiple_of(block * PBLK, PBLK), PBLK)
            piece = parts[k][r * PBLK:(r + 1) * PBLK, :].astype(F32)
            keys_ref[rows, :] += piece[:, :HD]
            values_ref[rows, :] += piece[:, HD:]


def kv_kernel(n_tp, me_ref, *refs):
    hidden, (wk_ref, wv_ref, k_ref, v_ref) = refs[:n_tp], refs[n_tp:]
    me = me_ref[0]
    length, width = hidden[0].shape
    new_k = jnp.zeros((length, HD), F32)
    new_v = jnp.zeros((length, HD), F32)
    for i in range(n_tp):
        rows = pl.ds(pl.multiple_of((me ^ i) * width, width), width)
        piece = hidden[i][...]
        new_k += dot(piece, wk_ref[rows, :], ((1,), (0,)))
        new_v += dot(piece, wv_ref[rows, :], ((1,), (0,)))
    k_ref[...] = new_k.astype(BF16)
    v_ref[...] = new_v.astype(BF16)


def forward_kernel(n_pre, scaling, q_ref, newk_ref, newv_ref, *refs):
    prefix = refs[:n_pre]
    ctx_ref, exps_ref, row_ref, col_ref, vt_all, s_buf, sums = refs[n_pre:]
    length = q_ref.shape[0]
    heads = q_ref.shape[1] // HD
    factor = scaling * LOG2E
    chunks = []
    at = 0
    for ref in prefix:
        size = ref.shape[0]
        vt_all[:, at:at + size] = ref[:, HD:].astype(F32).T.astype(BF16)
        chunks.append((at, size, ref))
        at += size
    vt_all[:, at:] = newv_ref[...].astype(F32).T.astype(BF16)
    visible = lax.broadcasted_iota(jnp.int32, (length, length), 0) <= lax.broadcasted_iota(
        jnp.int32, (length, length), 1)
    sums[...] = jnp.ones_like(sums)

    def scores(h):
        qh = q_ref[:, h * HD:(h + 1) * HD]
        peak = None
        for start, size, ref in chunks:
            s = dot(ref[:, :HD], qh, ((1,), (1,)))
            s_buf[h % 2, start:start + size, :] = s
            top = jnp.max(s, axis=0, keepdims=True)
            peak = top if peak is None else jnp.maximum(peak, top)
        s = jnp.where(visible, dot(newk_ref[...], qh, ((1,), (1,))), -jnp.inf)
        s_buf[h % 2, at:, :] = s
        return jnp.maximum(peak, jnp.max(s, axis=0, keepdims=True))

    def finish(h, peak):
        lanes = slice(h * length, (h + 1) * length)
        total = jnp.zeros((1, length), F32)
        step = length // 2
        for start in range(0, at + length, step):
            e = jnp.exp2((s_buf[h % 2, start:start + step, :] - peak) * factor)
            total += jnp.sum(e, axis=0, keepdims=True)
            exps_ref[start:start + step, lanes] = e.astype(BF16)
        inverse = 1.0 / total
        sums[h:h + 1, :] = inverse
        ctx_t = dot(vt_all[...], exps_ref[:, lanes], ((1,), (0,))) * inverse
        ctx_ref[:, h * HD:(h + 1) * HD] = ctx_t.T.astype(BF16)

    peak = scores(0)
    for h in range(heads):
        later = scores(h + 1) if h + 1 < heads else None
        finish(h, peak)
        peak = later
    row_ref[...] = sums[:row_ref.shape[0], :]
    col_ref[...] = sums[...].T


def project_kernel(order, me_ref, ctx_ref, w_ref, *outs):
    me = me_ref[0]
    width = outs[0].shape[1]
    ctx = ctx_ref[...]
    for i, out in zip(order, outs):
        cols = pl.ds(pl.multiple_of((me ^ i) * width, 128), width)
        out[...] = dot(ctx, w_ref[:, cols], ((1,), (0,))).astype(BF16)


def near_kernel(order, me_ref, w_ref, *refs):
    grads, out = refs[:-1], refs[-1]
    me = me_ref[0]
    width = grads[0].shape[1]
    total = jnp.zeros(out.shape, F32)
    for i, grad in zip(order, grads):
        cols = pl.ds(pl.multiple_of((me ^ i) * width, 128), width)
        total += dot(grad[...], w_ref[:, cols], ((1,), (1,)))
    out[...] = total


def backward_kernel(order, n_pre, scaling, me_ref, w_ref, near_ref, q_ref, newv_ref, exps_ref, row_ref, col_ref, *refs):
    grads, prefix = refs[:len(order)], refs[len(order):len(order) + n_pre]
    outs = refs[len(order) + n_pre:len(order) + 2 * n_pre]
    g_all, q_all, dbuf, slopes = refs[len(order) + 2 * n_pre:]
    me = me_ref[0]
    length, width = grads[0].shape
    heads = q_ref.shape[1] // HD
    total = near_ref[...]
    for i, grad in zip(order, grads):
        cols = pl.ds(pl.multiple_of((me ^ i) * width, 128), width)
        total += dot(grad[...], w_ref[:, cols], ((1,), (1,)))
    for h in range(heads):
        rows = slice(h * length, (h + 1) * length)
        q_all[rows, :] = q_ref[:, h * HD:(h + 1) * HD]
        g_all[rows, :] = (total[:, h * HD:(h + 1) * HD] * col_ref[:, h:h + 1]).astype(BF16)
    n_rows = dbuf.shape[0]

    def slope(h):
        gh = g_all[h * length:(h + 1) * length, :]
        lanes = slice(h * length, (h + 1) * length)
        at = 0
        delta = None
        for ref in prefix:
            size = ref.shape[0]
            s = dot(ref[:, HD:], gh, ((1,), (1,)))
            slopes[h % 2, at:at + size, :] = s
            part = jnp.sum(exps_ref[at:at + size, lanes].astype(F32) * s, axis=0, keepdims=True)
            delta = part if delta is None else delta + part
            at += size
        s = dot(newv_ref[...], gh, ((1,), (1,)))
        delta += jnp.sum(exps_ref[at:, lanes].astype(F32) * s, axis=0, keepdims=True)
        return delta * row_ref[h:h + 1, :]

    def finish(h, delta):
        lanes = slice(h * length, (h + 1) * length)
        step = length // 2
        for start in range(0, n_rows, step):
            e = exps_ref[start:start + step, lanes].astype(F32)
            dbuf[start:start + step, lanes] = (e * (slopes[h % 2, start:start + step, :] - delta)).astype(BF16)

    delta = slope(0)
    for h in range(heads):
        later = slope(h + 1) if h + 1 < heads else None
        finish(h, delta)
        delta = later
    at = 0
    for out in outs:
        size = out.shape[0]
        out[:, HD:] = dot(exps_ref[at:at + size, :], g_all[...], ((1,), (0,))).astype(out.dtype)
        out[:, :HD] = (dot(dbuf[at:at + size, :], q_all[...], ((1,), (0,))) * scaling).astype(out.dtype)
        at += size


def local(hidden_states, queries, key_weight, value_weight, output_weight, prefix_keys, prefix_values, reads, out_grad):
    length, width = hidden_states.shape
    scaling = HD ** (-0.5)
    heads = queries.shape[1] // HD
    n_tp = lax.axis_size("tp")
    n_seq = lax.axis_size("seq")
    here = prefix_keys.shape[0] // PBLK
    read_count = reads.shape[1]
    cap = max(1, read_count // n_seq)
    dense = cap * n_seq == read_count and n_seq & (n_seq - 1) == 0 and here * n_seq % read_count == 0
    me_tp = lax.axis_index("tp").astype(jnp.int32).reshape(1)
    me_seq = lax.axis_index("seq").astype(jnp.int32).reshape(1)
    n_rows = read_count * PBLK
    keys = n_rows + length

    def hop(x, axis, k):
        n = n_tp if axis == "tp" else n_seq
        return lax.ppermute(x, axis, [(i, i ^ k) for i in range(n)])

    def grant(mib):
        return pltpu.CompilerParams(vmem_limit_bytes=mib * 2 ** 20)

    near_grad = hop(out_grad, "tp", 1)
    far_grad = hop(out_grad, "tp", 2)
    near_hidden = hop(hidden_states, "tp", 1)
    far_hidden = hop(hidden_states, "tp", 2)
    last_hidden = hop(far_hidden, "tp", 1)
    last_grad = hop(far_grad, "tp", 1)
    far_first = sorted(range(1, n_seq), key=lambda k: (-(k // 4), k & 1, -k))

    if dense:
        shape = jax.ShapeDtypeStruct((cap * PBLK, 2 * HD), BF16)
        picked = pl.pallas_call(
            functools.partial(pick_kernel, n_seq, cap, here),
            out_shape=[shape] * n_seq,
            in_specs=[SMEM, SMEM, VMEM, VMEM],
            out_specs=[VMEM] * n_seq,
            cost_estimate=cost(0, 2 ** 20),
            compiler_params=grant(4),
            name="pick",
        )(me_seq, reads, prefix_keys, prefix_values)
        moved = {k: hop(picked[k], "seq", k) for k in far_first}
        prefix = [picked[0]] + [moved[k] for k in range(1, n_seq)]
    else:
        flat = PBLK * 2 * HD
        local_cache = jnp.concatenate([prefix_keys, prefix_values], axis=1).reshape(here, flat)
        own = me_seq[0]
        owners = reads // here
        slot_here = reads % here
        earlier = jnp.arange(read_count)[None, :] < jnp.arange(read_count)[:, None]
        ranks = jnp.sum((owners[:, :, None] == owners[:, None, :]) & earlier[None], axis=2)
        slots = jnp.arange(cap, dtype=jnp.int32)
        picker = jnp.sum(
            ((owners == own)[:, :, None, None]
             & (ranks[:, :, None, None] == slots[None, None, :, None])
             & (slot_here[:, :, None, None] == jnp.arange(here, dtype=jnp.int32))).astype(F32), axis=1)
        outgoing = jnp.einsum("dcb,bf->dcf", picker.astype(BF16), local_cache, preferred_element_type=F32).astype(BF16)
        incoming = lax.all_to_all(outgoing, "seq", split_axis=0, concat_axis=0, tiled=True)
        my_owner, my_rank = owners[own], ranks[own]
        fetched = jnp.take(incoming.reshape(n_seq * cap, flat), my_owner * cap + my_rank, axis=0)
        prefix = [fetched.reshape(n_rows, 2 * HD)]
    n_pre = len(prefix)

    new_kv = jax.ShapeDtypeStruct((length, HD), BF16)
    new_k, new_v = pl.pallas_call(
        functools.partial(kv_kernel, n_tp),
        out_shape=[new_kv] * 2,
        in_specs=[SMEM] + [VMEM] * (n_tp + 2),
        out_specs=[VMEM] * 2,
        compiler_params=grant(8),
        cost_estimate=cost(5e8, 4e6),
        name="kv",
    )(me_tp, hidden_states, near_hidden, far_hidden, last_hidden, key_weight, value_weight)

    near = pl.pallas_call(
        functools.partial(near_kernel, (0, 1)),
        out_shape=jax.ShapeDtypeStruct((length, heads * HD), F32),
        in_specs=[SMEM] + [VMEM] * 3,
        out_specs=VMEM,
        compiler_params=grant(16),
        cost_estimate=cost(1e9, 8e6),
        name="near",
    )(me_tp, output_weight, out_grad, near_grad)

    ctx, exps, row, col = pl.pallas_call(
        functools.partial(forward_kernel, n_pre, scaling),
        out_shape=[
            jax.ShapeDtypeStruct((length, heads * HD), BF16),
            jax.ShapeDtypeStruct((keys, heads * length), BF16),
            jax.ShapeDtypeStruct((heads + (-heads) % 8, length), F32),
            jax.ShapeDtypeStruct((length, HD), F32),
        ],
        in_specs=[VMEM] * (3 + n_pre),
        out_specs=[VMEM] * 4,
        scratch_shapes=[
            pltpu.VMEM((HD, keys), BF16),
            pltpu.VMEM((2, keys, length), F32),
            pltpu.VMEM((HD, length), F32),
        ],
        compiler_params=grant(20),
        cost_estimate=cost(5e9, 1e7, 3e6),
        name="forward",
    )(queries, new_k, new_v, *prefix)

    def project(order):
        return pl.pallas_call(
            functools.partial(project_kernel, order),
            out_shape=[jax.ShapeDtypeStruct((length, width), BF16)] * len(order),
            in_specs=[SMEM, VMEM, VMEM],
            out_specs=[VMEM] * len(order),
            compiler_params=grant(16),
            cost_estimate=cost(5e8 * len(order), 2e6 * len(order)),
        )(me_tp, ctx, output_weight)

    share3, = project((3,))
    near3 = hop(share3, "tp", 1)
    share2, share1, share0 = project((2, 1, 0))
    near1 = hop(share1, "tp", 1)
    cross = (share2.astype(F32) + near3.astype(F32)).astype(BF16)
    across = hop(cross, "tp", 2)
    layer_output = (share0.astype(F32) + near1.astype(F32) + across.astype(F32)).astype(BF16)

    grad_type = BF16 if dense else F32
    parts = pl.pallas_call(
        functools.partial(backward_kernel, (2, 3), n_pre, scaling),
        out_shape=[jax.ShapeDtypeStruct(x.shape, grad_type) for x in prefix],
        in_specs=[SMEM] + [VMEM] * (9 + n_pre),
        out_specs=[VMEM] * n_pre,
        scratch_shapes=[
            pltpu.VMEM((heads * length, HD), BF16),
            pltpu.VMEM((heads * length, HD), BF16),
            pltpu.VMEM((n_rows, heads * length), BF16),
            pltpu.VMEM((2, n_rows, length), F32),
        ],
        compiler_params=grant(32),
        cost_estimate=cost(7e9, 1e7),
        name="backward",
    )(me_tp, output_weight, near, queries, new_v, exps, row, col, far_grad, last_grad, *prefix)

    if dense:
        back = {k: hop(parts[k], "seq", k) for k in far_first}
        returned = [parts[0]] + [back[k] for k in range(1, n_seq)]
        shape = jax.ShapeDtypeStruct(prefix_keys.shape, F32)
        key_grad, value_grad = pl.pallas_call(
            functools.partial(place_kernel, n_seq, cap, here),
            out_shape=[shape] * 2,
            in_specs=[SMEM, SMEM] + [VMEM] * n_seq,
            out_specs=[VMEM] * 2,
            cost_estimate=cost(0, 2 ** 20),
            compiler_params=grant(4),
            name="place",
        )(me_seq, reads, *returned)
    else:
        cache_grads = parts[0].reshape(read_count, flat)
        placer = ((my_owner[None, None, :] == jnp.arange(n_seq, dtype=jnp.int32)[:, None, None])
                  & (my_rank[None, None, :] == slots[None, :, None])).astype(F32)
        leaving = jnp.einsum("ocr,rf->ocf", placer, cache_grads, precision=lax.Precision.HIGHEST)
        back = lax.all_to_all(leaving.astype(BF16), "seq", split_axis=0, concat_axis=0, tiled=True).astype(F32)
        summed = jnp.einsum("dcb,dcf->bf", picker, back, precision=lax.Precision.HIGHEST).reshape(here * PBLK, 2 * HD)
        key_grad, value_grad = summed[:, :HD], summed[:, HD:]
    return layer_output, key_grad, value_grad


def solution(mesh):
    in_specs = (P("seq", "tp"), P("seq", "tp"), P(None, "tp"), P(None, "tp"), P("tp", None),
                P("seq", "tp"), P("seq", "tp"), P(), P("seq", "tp"))
    out_specs = (P("seq", "tp"), P("seq", "tp"), P("seq", "tp"))
    return jax.shard_map(local, mesh=mesh, in_specs=in_specs, out_specs=out_specs, check_vma=False)
```

profile of v0, /device:TPU:0, one launch (start us, length us, event | category | flops | bytes accessed | tf_op | source)
XLA Modules:
  0.0 81.7 jit_solution(10200574331218906235)
XLA Ops:
  0.6 3.1 %collective-permute-start.1 = (bf16[256,896]{1,0:T(8,128)(2,1)}, bf16[256,896]{1,0:T(8,128)(2,1)S(1)}, u32[]{:S(2)}, u32[]{:S(2)}) collective-permute-start(bf16[256,896]{1,0:T(8,128)(2,1)} %refs_0_.2), channel_id=1, source_target_pairs={{0,2},{1,3},{2,0},{3,1},{4,6},{5,7},{6,4},{7,5},{8,10},{9,11},{10,... | collective-permute-start | bytes 1376264 | tf_op jit(solution)/shard_map/ppermute | solution.py:210
  3.7 10.7 %collective-permute-done.1.refs_2_ = bf16[256,896]{1,0:T(8,128)(2,1)S(1)} collective-permute-done((bf16[256,896]{1,0:T(8,128)(2,1)}, bf16[256,896]{1,0:T(8,128)(2,1)S(1)}, u32[]{:S(2)}, u32[]{:S(2)}) %collective-permute-start.1) | collective-permute-done | bytes 458784 | tf_op jit(solution)/shard_map/ppermute | solution.py:210
  17.5 1.8 %collective-permute-start.3 = (bf16[128,256]{1,0:T(8,128)(2,1)S(1)}, bf16[128,256]{1,0:T(8,128)(2,1)S(1)}, u32[]{:S(2)}, u32[]{:S(2)}) collective-permute-start(bf16[128,256]{1,0:T(8,128)(2,1)S(1)} %get-tuple-element.33), channel_id=1, source_target_pairs={{0,4},{4,0},{8,12},{12,8},{16,20},{20,16},{24,28},{28,24},{1,5},{5... | collective-permute-start | bytes 196616 | tf_op jit(solution)/shard_map/ppermute | solution.py:210
  19.3 1.6 %collective-permute-start.4 = (bf16[128,256]{1,0:T(8,128)(2,1)S(1)}, bf16[128,256]{1,0:T(8,128)(2,1)S(1)}, u32[]{:S(2)}, u32[]{:S(2)}) collective-permute-start(bf16[128,256]{1,0:T(8,128)(2,1)S(1)} %get-tuple-element.34), channel_id=1, source_target_pairs={{0,8},{4,12},{8,0},{12,4},{16,24},{20,28},{24,16},{28,20},{1,9},{5... | collective-permute-start | bytes 196616 | tf_op jit(solution)/shard_map/ppermute | solution.py:210
  22.1 2.8 %collective-permute-start.6 = (bf16[128,256]{1,0:T(8,128)(2,1)S(1)}, bf16[128,256]{1,0:T(8,128)(2,1)S(1)}, u32[]{:S(2)}, u32[]{:S(2)}) collective-permute-start(bf16[128,256]{1,0:T(8,128)(2,1)S(1)} %get-tuple-element.36), channel_id=1, source_target_pairs={{0,16},{4,20},{8,24},{12,28},{16,0},{20,4},{24,8},{28,12},{1,17},{... | collective-permute-start | bytes 196616 | tf_op jit(solution)/shard_map/ppermute | solution.py:210
  24.9 1.3 %collective-permute-start.7 = (bf16[128,256]{1,0:T(8,128)(2,1)S(1)}, bf16[128,256]{1,0:T(8,128)(2,1)S(1)}, u32[]{:S(2)}, u32[]{:S(2)}) collective-permute-start(bf16[128,256]{1,0:T(8,128)(2,1)S(1)} %get-tuple-element.37), channel_id=1, source_target_pairs={{0,20},{4,16},{8,28},{12,24},{16,4},{20,0},{24,12},{28,8},{1,21},{... | collective-permute-start | bytes 196616 | tf_op jit(solution)/shard_map/ppermute | solution.py:210
  26.2 3.6 %collective-permute-start.8 = (bf16[128,256]{1,0:T(8,128)(2,1)S(1)}, bf16[128,256]{1,0:T(8,128)(2,1)S(1)}, u32[]{:S(2)}, u32[]{:S(2)}) collective-permute-start(bf16[128,256]{1,0:T(8,128)(2,1)S(1)} %get-tuple-element.38), channel_id=1, source_target_pairs={{0,24},{4,28},{8,16},{12,20},{16,8},{20,12},{24,0},{28,4},{1,25},{... | collective-permute-start | bytes 196616 | tf_op jit(solution)/shard_map/ppermute | solution.py:210
  29.8 1.3 %collective-permute-start.9 = (bf16[128,256]{1,0:T(8,128)(2,1)S(1)}, bf16[128,256]{1,0:T(8,128)(2,1)S(1)}, u32[]{:S(2)}, u32[]{:S(2)}) collective-permute-start(bf16[128,256]{1,0:T(8,128)(2,1)S(1)} %get-tuple-element.39), channel_id=1, source_target_pairs={{0,28},{4,24},{8,20},{12,16},{16,12},{20,8},{24,4},{28,0},{1,29},{... | collective-permute-start | bytes 196616 | tf_op jit(solution)/shard_map/ppermute | solution.py:210
  31.1 1.2 %copy-done = bf16[3584,128]{1,0:T(8,128)(2,1)S(1)} copy-done((bf16[3584,128]{1,0:T(8,128)(2,1)S(1)}, bf16[3584,128]{1,0:T(8,128)(2,1)}, u32[]{:S(2)}) %copy-start) | copy-done | bytes 917528
  32.2 1.2 %copy-done.1 = bf16[3584,128]{1,0:T(8,128)(2,1)S(1)} copy-done((bf16[3584,128]{1,0:T(8,128)(2,1)S(1)}, bf16[3584,128]{1,0:T(8,128)(2,1)}, u32[]{:S(2)}) %copy-start.1) | copy-done | bytes 917528
  35.7 1.6 %collective-permute-start.14 = (bf16[256,896]{1,0:T(8,128)(2,1)}, bf16[256,896]{1,0:T(8,128)(2,1)S(1)}, u32[]{:S(2)}, u32[]{:S(2)}) collective-permute-start(bf16[256,896]{1,0:T(8,128)(2,1)} %refs_0_.3), channel_id=1, source_target_pairs={{0,2},{1,3},{2,0},{3,1},{4,6},{5,7},{6,4},{7,5},{8,10},{9,11},{10,... | collective-permute-start | bytes 1376264 | tf_op jit(solution)/shard_map/ppermute | solution.py:210
  38.3 3.9 %forward.1 = (bf16[256,896]{1,0:T(8,128)(2,1)S(1)}, bf16[1280,1792]{1,0:T(8,128)(2,1)S(1)}, f32[8,256]{1,0:T(8,128)S(1)}, f32[256,128]{1,0:T(8,128)S(1)}) custom-call(bf16[256,896]{1,0:T(8,128)(2,1)S(1)} %copy-done.8, bf16[256,128]{1,0:T(8,128)(2,1)S(1)} %get-tuple-element.30.newk_ref, bf16[256,128]{1,0:T(8,128)(2,1)S(1)} %get-tuple-element.31.newv_ref, ...), custom_call_target="tpu_custom_call" | custom-call | flops 5000000000 | bytes 10000000 | tf_op jit(solution)/shard_map/forward/pallas_call | solution.py:277
  43.2 5.6 %collective-permute-done.14.refs_0_ = bf16[256,896]{1,0:T(8,128)(2,1)S(1)} collective-permute-done((bf16[256,896]{1,0:T(8,128)(2,1)}, bf16[256,896]{1,0:T(8,128)(2,1)S(1)}, u32[]{:S(2)}, u32[]{:S(2)}) %collective-permute-start.14) | collective-permute-done | bytes 458784 | tf_op jit(solution)/shard_map/ppermute | solution.py:210
  48.8 1.3 %near.1.near_ref = f32[256,896]{1,0:T(8,128)S(1)} custom-call(s32[1]{0:T(128)} %bitcast.me_ref, bf16[896,3584]{1,0:T(8,128)(2,1)S(1)} %bitcast.3, bf16[256,896]{1,0:T(8,128)(2,1)S(1)} %copy-done.3, bf16[256,896]{1,0:T(8,128)(2,1)S(1)} %collective-permute-done.13.refs_1_), custom_call_target="tpu_custom_call" | custom-call | flops 1000000000 | bytes 8000000 | tf_op jit(solution)/shard_map/near/pallas_call | solution.py:267
  50.1 1.8 %shard_map.112 = (bf16[256,896]{1,0:T(8,128)(2,1)S(1)}, bf16[256,896]{1,0:T(8,128)(2,1)S(1)}, bf16[256,896]{1,0:T(8,128)(2,1)S(1)}) custom-call(s32[1]{0:T(128)} %bitcast.me_ref, bf16[256,896]{1,0:T(8,128)(2,1)S(1)} %get-tuple-element.40.ctx_ref, bf16[896,3584]{1,0:T(8,128)(2,1)S(1)} %bitcast.3), custom_call_target="tpu_custom_call" | custom-call | flops 1500000000 | bytes 6000000 | tf_op jit(solution)/shard_map/pallas_call | solution.py:298
  52.6 1.6 %collective-permute-start.12 = (bf16[256,896]{1,0:T(8,128)(2,1)S(1)}, bf16[256,896]{1,0:T(8,128)(2,1)S(1)}, u32[]{:S(2)}, u32[]{:S(2)}) collective-permute-start(bf16[256,896]{1,0:T(8,128)(2,1)S(1)} %add_convert_fusion.1), channel_id=1, source_target_pairs={{0,2},{1,3},{2,0},{3,1},{4,6},{5,7},{6,4},{7,5},{8,10},{9,11},{10,... | collective-permute-start | bytes 1376264 | tf_op jit(solution)/shard_map/ppermute | solution.py:210
  54.2 6.1 %backward.1 = (bf16[128,256]{1,0:T(8,128)(2,1)S(1)}, bf16[128,256]{1,0:T(8,128)(2,1)S(1)}, bf16[128,256]{1,0:T(8,128)(2,1)S(1)}, bf16[128,256]{1,0:T(8,128)(2,1)...) custom-call(s32[1]{0:T(128)} %bitcast.me_ref, ...), custom_call_target="tpu_custom_call" | custom-call | flops 7000000000 | bytes 10000000 | tf_op jit(solution)/shard_map/backward/pallas_call | solution.py:316
  60.8 3.0 %collective-permute-start.18 = (bf16[128,256]{1,0:T(8,128)(2,1)S(1)}, bf16[128,256]{1,0:T(8,128)(2,1)S(1)}, u32[]{:S(2)}, u32[]{:S(2)}) collective-permute-start(bf16[128,256]{1,0:T(8,128)(2,1)S(1)} %get-tuple-element.50), channel_id=1, source_target_pairs={{0,12},{4,8},{8,4},{12,0},{16,28},{20,24},{24,20},{28,16},{1,13},{... | collective-permute-start | bytes 196616 | tf_op jit(solution)/shard_map/ppermute | solution.py:210
  65.3 2.1 %collective-permute-start.20 = (bf16[128,256]{1,0:T(8,128)(2,1)S(1)}, bf16[128,256]{1,0:T(8,128)(2,1)S(1)}, u32[]{:S(2)}, u32[]{:S(2)}) collective-permute-start(bf16[128,256]{1,0:T(8,128)(2,1)S(1)} %get-tuple-element.52), channel_id=1, source_target_pairs={{0,20},{4,16},{8,28},{12,24},{16,4},{20,0},{24,12},{28,8},{1,21},{... | collective-permute-start | bytes 196616 | tf_op jit(solution)/shard_map/ppermute | solution.py:210
  67.4 3.6 %collective-permute-start.21 = (bf16[128,256]{1,0:T(8,128)(2,1)S(1)}, bf16[128,256]{1,0:T(8,128)(2,1)S(1)}, u32[]{:S(2)}, u32[]{:S(2)}) collective-permute-start(bf16[128,256]{1,0:T(8,128)(2,1)S(1)} %get-tuple-element.53), channel_id=1, source_target_pairs={{0,24},{4,28},{8,16},{12,20},{16,8},{20,12},{24,0},{28,4},{1,25},{... | collective-permute-start | bytes 196616 | tf_op jit(solution)/shard_map/ppermute | solution.py:210
  71.0 1.4 %collective-permute-done.19.refs_4_ = bf16[128,256]{1,0:T(8,128)(2,1)S(1)} collective-permute-done((bf16[128,256]{1,0:T(8,128)(2,1)S(1)}, bf16[128,256]{1,0:T(8,128)(2,1)S(1)}, u32[]{:S(2)}, u32[]{:S(2)}) %collective-permute-start.19) | collective-permute-done | bytes 65568 | tf_op jit(solution)/shard_map/ppermute | solution.py:210
  72.4 3.8 %collective-permute-start.22 = (bf16[128,256]{1,0:T(8,128)(2,1)S(1)}, bf16[128,256]{1,0:T(8,128)(2,1)S(1)}, u32[]{:S(2)}, u32[]{:S(2)}) collective-permute-start(bf16[128,256]{1,0:T(8,128)(2,1)S(1)} %get-tuple-element.54), channel_id=1, source_target_pairs={{0,28},{4,24},{8,20},{12,16},{16,12},{20,8},{24,4},{28,0},{1,29},{... | collective-permute-start | bytes 196616 | tf_op jit(solution)/shard_map/ppermute | solution.py:210
  76.2 3.2 %collective-permute-done.22.refs_7_ = bf16[128,256]{1,0:T(8,128)(2,1)S(1)} collective-permute-done((bf16[128,256]{1,0:T(8,128)(2,1)S(1)}, bf16[128,256]{1,0:T(8,128)(2,1)S(1)}, u32[]{:S(2)}, u32[]{:S(2)}) %collective-permute-start.22) | collective-permute-done | bytes 65568 | tf_op jit(solution)/shard_map/ppermute | solution.py:210
  79.3 1.4 %place.1 = (f32[256,128]{1,0:T(8,128)}, f32[256,128]{1,0:T(8,128)}) custom-call(s32[1]{0:T(128)} %bitcast.1.me_ref, s32[8,16]{1,0:T(8,128)S(1)} %copy-done.7, bf16[128,256]{1,0:T(8,128)(2,1)S(1)} %get-tuple-element.47.refs_0_, bf16[128,256]{1,0:T(8,128)(2,1)S(1)} %collective-permute-done.16.refs_1_, bf16[128,256]{1,0:T(8,128)(2,1)S(1)} %collective-permute-done.17.refs_2_, ...), custom_call_target="tpu_custom_call" | custom-call | bytes 1048576 | tf_op jit(solution)/shard_map/place/pallas_call | solution.py:336
  (57 shorter events, 12.1 us)
Async XLA Ops:
  0.6 13.8 %collective-permute-start.1 = (bf16[256,896]{1,0:T(8,128)(2,1)}, bf16[256,896]{1,0:T(8,128)(2,1)S(1)}, u32[]{:S(2)}, u32[]{:S(2)}) collective-permute-start(bf16[256,896]{1,0:T(8,128)(2,1)} %refs_0_.2), channel_id=1, source_target_pairs={{0,2},{1,3},{2,0},{3,1},{4,6},{5,7},{6,4},{7,5},{8,10},{9,11},{10,... | collective-permute-start | bytes 1376264 | tf_op jit(solution)/shard_map/ppermute | solution.py:210
  3.7 22.5 %collective-permute-start = (bf16[256,896]{1,0:T(8,128)(2,1)}, bf16[256,896]{1,0:T(8,128)(2,1)S(1)}, u32[]{:S(2)}, u32[]{:S(2)}) collective-permute-start(bf16[256,896]{1,0:T(8,128)(2,1)} %refs_0_.2), channel_id=1, source_target_pairs={{0,1},{1,0},{2,3},{3,2},{4,5},{5,4},{6,7},{7,6},{8,9},{9,8},{10,11... | collective-permute-start | bytes 1376264 | tf_op jit(solution)/shard_map/ppermute | solution.py:210
  14.4 15.4 %collective-permute-start.2 = (bf16[256,896]{1,0:T(8,128)(2,1)S(1)}, bf16[256,896]{1,0:T(8,128)(2,1)S(1)}, u32[]{:S(2)}, u32[]{:S(2)}) collective-permute-start(bf16[256,896]{1,0:T(8,128)(2,1)S(1)} %collective-permute-done.1.refs_2_), channel_id=1, source_target_pairs={{0,1},{1,0},{2,3},{3,2},{4,5},{5,4},{6,7},{7,6},{8,9},{9,8},{10,11... | collective-permute-start | bytes 1376264 | tf_op jit(solution)/shard_map/ppermute | solution.py:210
  17.5 4.6 %collective-permute-start.3 = (bf16[128,256]{1,0:T(8,128)(2,1)S(1)}, bf16[128,256]{1,0:T(8,128)(2,1)S(1)}, u32[]{:S(2)}, u32[]{:S(2)}) collective-permute-start(bf16[128,256]{1,0:T(8,128)(2,1)S(1)} %get-tuple-element.33), channel_id=1, source_target_pairs={{0,4},{4,0},{8,12},{12,8},{16,20},{20,16},{24,28},{28,24},{1,5},{5... | collective-permute-start | bytes 196616 | tf_op jit(solution)/shard_map/ppermute | solution.py:210
  19.3 5.6 %collective-permute-start.4 = (bf16[128,256]{1,0:T(8,128)(2,1)S(1)}, bf16[128,256]{1,0:T(8,128)(2,1)S(1)}, u32[]{:S(2)}, u32[]{:S(2)}) collective-permute-start(bf16[128,256]{1,0:T(8,128)(2,1)S(1)} %get-tuple-element.34), channel_id=1, source_target_pairs={{0,8},{4,12},{8,0},{12,4},{16,24},{20,28},{24,16},{28,20},{1,9},{5... | collective-permute-start | bytes 196616 | tf_op jit(solution)/shard_map/ppermute | solution.py:210
  20.9 14.7 %collective-permute-start.5 = (bf16[128,256]{1,0:T(8,128)(2,1)S(1)}, bf16[128,256]{1,0:T(8,128)(2,1)S(1)}, u32[]{:S(2)}, u32[]{:S(2)}) collective-permute-start(bf16[128,256]{1,0:T(8,128)(2,1)S(1)} %get-tuple-element.35), channel_id=1, source_target_pairs={{0,12},{4,8},{8,4},{12,0},{16,28},{20,24},{24,20},{28,16},{1,13},{... | collective-permute-start | bytes 196616 | tf_op jit(solution)/shard_map/ppermute | solution.py:210
  22.1 13.6 %collective-permute-start.6 = (bf16[128,256]{1,0:T(8,128)(2,1)S(1)}, bf16[128,256]{1,0:T(8,128)(2,1)S(1)}, u32[]{:S(2)}, u32[]{:S(2)}) collective-permute-start(bf16[128,256]{1,0:T(8,128)(2,1)S(1)} %get-tuple-element.36), channel_id=1, source_target_pairs={{0,16},{4,20},{8,24},{12,28},{16,0},{20,4},{24,8},{28,12},{1,17},{... | collective-permute-start | bytes 196616 | tf_op jit(solution)/shard_map/ppermute | solution.py:210
  24.9 12.4 %collective-permute-start.7 = (bf16[128,256]{1,0:T(8,128)(2,1)S(1)}, bf16[128,256]{1,0:T(8,128)(2,1)S(1)}, u32[]{:S(2)}, u32[]{:S(2)}) collective-permute-start(bf16[128,256]{1,0:T(8,128)(2,1)S(1)} %get-tuple-element.37), channel_id=1, source_target_pairs={{0,20},{4,16},{8,28},{12,24},{16,4},{20,0},{24,12},{28,8},{1,21},{... | collective-permute-start | bytes 196616 | tf_op jit(solution)/shard_map/ppermute | solution.py:210
  26.2 11.1 %collective-permute-start.8 = (bf16[128,256]{1,0:T(8,128)(2,1)S(1)}, bf16[128,256]{1,0:T(8,128)(2,1)S(1)}, u32[]{:S(2)}, u32[]{:S(2)}) collective-permute-start(bf16[128,256]{1,0:T(8,128)(2,1)S(1)} %get-tuple-element.38), channel_id=1, source_target_pairs={{0,24},{4,28},{8,16},{12,20},{16,8},{20,12},{24,0},{28,4},{1,25},{... | collective-permute-start | bytes 196616 | tf_op jit(solution)/shard_map/ppermute | solution.py:210
  29.8 7.5 %collective-permute-start.9 = (bf16[128,256]{1,0:T(8,128)(2,1)S(1)}, bf16[128,256]{1,0:T(8,128)(2,1)S(1)}, u32[]{:S(2)}, u32[]{:S(2)}) collective-permute-start(bf16[128,256]{1,0:T(8,128)(2,1)S(1)} %get-tuple-element.39), channel_id=1, source_target_pairs={{0,28},{4,24},{8,20},{12,16},{16,12},{20,8},{24,4},{28,0},{1,29},{... | collective-permute-start | bytes 196616 | tf_op jit(solution)/shard_map/ppermute | solution.py:210
  35.6 13.2 %collective-permute-start.13 = (bf16[256,896]{1,0:T(8,128)(2,1)}, bf16[256,896]{1,0:T(8,128)(2,1)S(1)}, u32[]{:S(2)}, u32[]{:S(2)}) collective-permute-start(bf16[256,896]{1,0:T(8,128)(2,1)} %refs_0_.3), channel_id=1, source_target_pairs={{0,1},{1,0},{2,3},{3,2},{4,5},{5,4},{6,7},{7,6},{8,9},{9,8},{10,11... | collective-permute-start | bytes 1376264 | tf_op jit(solution)/shard_map/ppermute | solution.py:210
  35.7 13.1 %collective-permute-start.14 = (bf16[256,896]{1,0:T(8,128)(2,1)}, bf16[256,896]{1,0:T(8,128)(2,1)S(1)}, u32[]{:S(2)}, u32[]{:S(2)}) collective-permute-start(bf16[256,896]{1,0:T(8,128)(2,1)} %refs_0_.3), channel_id=1, source_target_pairs={{0,2},{1,3},{2,0},{3,1},{4,6},{5,7},{6,4},{7,5},{8,10},{9,11},{10,... | collective-permute-start | bytes 1376264 | tf_op jit(solution)/shard_map/ppermute | solution.py:210
  43.0 9.5 %collective-permute-start.11 = (bf16[256,896]{1,0:T(8,128)(2,1)S(1)}, bf16[256,896]{1,0:T(8,128)(2,1)S(1)}, u32[]{:S(2)}, u32[]{:S(2)}) collective-permute-start(bf16[256,896]{1,0:T(8,128)(2,1)S(1)} %shard_map.113), channel_id=1, source_target_pairs={{0,1},{1,0},{2,3},{3,2},{4,5},{5,4},{6,7},{7,6},{8,9},{9,8},{10,11... | collective-permute-start | bytes 1376264 | tf_op jit(solution)/shard_map/ppermute | solution.py:210
  48.8 5.3 %collective-permute-start.15 = (bf16[256,896]{1,0:T(8,128)(2,1)S(1)}, bf16[256,896]{1,0:T(8,128)(2,1)S(1)}, u32[]{:S(2)}, u32[]{:S(2)}) collective-permute-start(bf16[256,896]{1,0:T(8,128)(2,1)S(1)} %collective-permute-done.14.refs_0_), channel_id=1, source_target_pairs={{0,1},{1,0},{2,3},{3,2},{4,5},{5,4},{6,7},{7,6},{8,9},{9,8},{10,11... | collective-permute-start | bytes 1376264 | tf_op jit(solution)/shard_map/ppermute | solution.py:210
  51.9 28.9 %collective-permute-start.10 = (bf16[256,896]{1,0:T(8,128)(2,1)S(1)}, bf16[256,896]{1,0:T(8,128)(2,1)S(1)}, u32[]{:S(2)}, u32[]{:S(2)}) collective-permute-start(bf16[256,896]{1,0:T(8,128)(2,1)S(1)} %get-tuple-element.42), channel_id=1, source_target_pairs={{0,1},{1,0},{2,3},{3,2},{4,5},{5,4},{6,7},{7,6},{8,9},{9,8},{10,11... | collective-permute-start | bytes 1376264 | tf_op jit(solution)/shard_map/ppermute | solution.py:210
  52.6 28.2 %collective-permute-start.12 = (bf16[256,896]{1,0:T(8,128)(2,1)S(1)}, bf16[256,896]{1,0:T(8,128)(2,1)S(1)}, u32[]{:S(2)}, u32[]{:S(2)}) collective-permute-start(bf16[256,896]{1,0:T(8,128)(2,1)S(1)} %add_convert_fusion.1), channel_id=1, source_target_pairs={{0,2},{1,3},{2,0},{3,1},{4,6},{5,7},{6,4},{7,5},{8,10},{9,11},{10,... | collective-permute-start | bytes 1376264 | tf_op jit(solution)/shard_map/ppermute | solution.py:210
  54.1 25.2 %copy-start.7 = (s32[8,16]{1,0:T(8,128)S(1)}, s32[8,16]{1,0:T(8,128)}, u32[]{:S(2)}) copy-start(s32[8,16]{1,0:T(8,128)} %reads_ref.3) | copy-start | bytes 1540
  60.3 4.3 %collective-permute-start.16 = (bf16[128,256]{1,0:T(8,128)(2,1)S(1)}, bf16[128,256]{1,0:T(8,128)(2,1)S(1)}, u32[]{:S(2)}, u32[]{:S(2)}) collective-permute-start(bf16[128,256]{1,0:T(8,128)(2,1)S(1)} %get-tuple-element.48), channel_id=1, source_target_pairs={{0,4},{4,0},{8,12},{12,8},{16,20},{20,16},{24,28},{28,24},{1,5},{5... | collective-permute-start | bytes 196616 | tf_op jit(solution)/shard_map/ppermute | solution.py:210
  60.7 4.5 %collective-permute-start.17 = (bf16[128,256]{1,0:T(8,128)(2,1)S(1)}, bf16[128,256]{1,0:T(8,128)(2,1)S(1)}, u32[]{:S(2)}, u32[]{:S(2)}) collective-permute-start(bf16[128,256]{1,0:T(8,128)(2,1)S(1)} %get-tuple-element.49), channel_id=1, source_target_pairs={{0,8},{4,12},{8,0},{12,4},{16,24},{20,28},{24,16},{28,20},{1,9},{5... | collective-permute-start | bytes 196616 | tf_op jit(solution)/shard_map/ppermute | solution.py:210
  60.8 6.5 %collective-permute-start.18 = (bf16[128,256]{1,0:T(8,128)(2,1)S(1)}, bf16[128,256]{1,0:T(8,128)(2,1)S(1)}, u32[]{:S(2)}, u32[]{:S(2)}) collective-permute-start(bf16[128,256]{1,0:T(8,128)(2,1)S(1)} %get-tuple-element.50), channel_id=1, source_target_pairs={{0,12},{4,8},{8,4},{12,0},{16,28},{20,24},{24,20},{28,16},{1,13},{... | collective-permute-start | bytes 196616 | tf_op jit(solution)/shard_map/ppermute | solution.py:210
  64.6 7.8 %collective-permute-start.19 = (bf16[128,256]{1,0:T(8,128)(2,1)S(1)}, bf16[128,256]{1,0:T(8,128)(2,1)S(1)}, u32[]{:S(2)}, u32[]{:S(2)}) collective-permute-start(bf16[128,256]{1,0:T(8,128)(2,1)S(1)} %get-tuple-element.51), channel_id=1, source_target_pairs={{0,16},{4,20},{8,24},{12,28},{16,0},{20,4},{24,8},{28,12},{1,17},{... | collective-permute-start | bytes 196616 | tf_op jit(solution)/shard_map/ppermute | solution.py:210
  65.3 10.9 %collective-permute-start.20 = (bf16[128,256]{1,0:T(8,128)(2,1)S(1)}, bf16[128,256]{1,0:T(8,128)(2,1)S(1)}, u32[]{:S(2)}, u32[]{:S(2)}) collective-permute-start(bf16[128,256]{1,0:T(8,128)(2,1)S(1)} %get-tuple-element.52), channel_id=1, source_target_pairs={{0,20},{4,16},{8,28},{12,24},{16,4},{20,0},{24,12},{28,8},{1,21},{... | collective-permute-start | bytes 196616 | tf_op jit(solution)/shard_map/ppermute | solution.py:210
  67.4 8.8 %collective-permute-start.21 = (bf16[128,256]{1,0:T(8,128)(2,1)S(1)}, bf16[128,256]{1,0:T(8,128)(2,1)S(1)}, u32[]{:S(2)}, u32[]{:S(2)}) collective-permute-start(bf16[128,256]{1,0:T(8,128)(2,1)S(1)} %get-tuple-element.53), channel_id=1, source_target_pairs={{0,24},{4,28},{8,16},{12,20},{16,8},{20,12},{24,0},{28,4},{1,25},{... | collective-permute-start | bytes 196616 | tf_op jit(solution)/shard_map/ppermute | solution.py:210
  72.4 7.0 %collective-permute-start.22 = (bf16[128,256]{1,0:T(8,128)(2,1)S(1)}, bf16[128,256]{1,0:T(8,128)(2,1)S(1)}, u32[]{:S(2)}, u32[]{:S(2)}) collective-permute-start(bf16[128,256]{1,0:T(8,128)(2,1)S(1)} %get-tuple-element.54), channel_id=1, source_target_pairs={{0,28},{4,24},{8,20},{12,16},{16,12},{20,8},{24,4},{28,0},{1,29},{... | collective-permute-start | bytes 196616 | tf_op jit(solution)/shard_map/ppermute | solution.py:210
  (11 other events, 36.3 us)
where the time goes:
time: 82.1 us; the launch traced here: 81.7 us
  starting transfers between devices  33 us (40%)
  waiting for transfers between devices  23 us (28%)
  Pallas kernels  17.1 us (21%)
  local copies, waits for them, and re-layouts  6.78 us (8%)
  other arithmetic  1.05 us (1%)
    ppermute x23, starting transfers between devices, hop(): return lax.ppermute(x, axis, [(i, i ^ k) for i in range(n)])  33 us
    ppermute x23, waiting for transfers between devices, hop(): return lax.ppermute(x, axis, [(i, i ^ k) for i in range(n)])  23 us
    unnamed x24, local copies, waits for them, and re-layouts  6.78 us
    pallas_call x1, Pallas kernels, local(): pl.pallas_call(functools.partial(backward_kernel, (2, 3), n_pre, scaling)...  6.1 us
    pallas_call x1, Pallas kernels, local(): pl.pallas_call(functools.partial(forward_kernel, n_pre, scaling), out_sha...  3.94 us
    pallas_call x2, Pallas kernels, project(): pl.pallas_call(functools.partial(project_kernel, order), out_shape=[jax.S...  2.47 us
  transfers between devices with their start and end apart: 23, of which 7 were waited for; matrix products, arithmetic and copies ran while one was open for 0% of the time, Pallas kernels for 21%

commit v1 on v0

--- a/solution.py
+++ b/solution.py
@@ -15,25 +15,39 @@
 BF16 = jnp.bfloat16
 VMEM = pl.BlockSpec(memory_space=pltpu.VMEM)
 SMEM = pl.BlockSpec(memory_space=pltpu.SMEM)
-ANY = pl.BlockSpec(memory_space=pl.ANY)
+HBM = pl.BlockSpec(memory_space=pltpu.HBM)
 
 
 def dot(a, b, dims):
     return lax.dot_general(a, b, (dims, ((), ())), preferred_element_type=F32)
 
 
+def hbm(x):
+    return pltpu.with_memory_space_constraint(x, pltpu.HBM)
+
+
 def cost(flops, nbytes, trans=0):
     return pl.CostEstimate(flops=int(flops), bytes_accessed=int(nbytes), transcendentals=int(trans))
 
 
-def pick_kernel(n, cap, here, me_ref, reads_ref, keys_ref, values_ref, *outs):
-    me = me_ref[0]
+def pick_kernel(n, cap, here, me_ref, reads_hbm, keys_hbm, values_hbm, *refs):
+    outs, reads_ref, read_sem, sem = refs[:n], refs[n], refs[n + 1], refs[n + 2]
+    me = me_ref[0]
+    fetch = pltpu.make_async_copy(reads_hbm, reads_ref, read_sem)
+    fetch.start()
+    fetch.wait()
+    copies = []
     for k in range(n):
         for r in range(cap):
             block = reads_ref[me ^ k, cap * me + r] - here * me
             rows = pl.ds(pl.multiple_of(block * PBLK, PBLK), PBLK)
-            outs[k][r * PBLK:(r + 1) * PBLK, :HD] = keys_ref[rows, :]
-            outs[k][r * PBLK:(r + 1) * PBLK, HD:] = values_ref[rows, :]
+            at = pl.ds(r * PBLK, PBLK)
+            copies.append(pltpu.make_async_copy(keys_hbm.at[rows], outs[k].at[at, pl.ds(0, HD)], sem))
+            copies.append(pltpu.make_async_copy(values_hbm.at[rows], outs[k].at[at, pl.ds(HD, HD)], sem))
+    for copy in copies:
+        copy.start()
+    for copy in copies:
+        copy.wait()
 
 
 def place_kernel(n, cap, here, me_ref, reads_ref, *refs):
@@ -50,17 +64,32 @@
             values_ref[rows, :] += piece[:, HD:]
 
 
-def kv_kernel(n_tp, me_ref, *refs):
-    hidden, (wk_ref, wv_ref, k_ref, v_ref) = refs[:n_tp], refs[n_tp:]
-    me = me_ref[0]
-    length, width = hidden[0].shape
+def kv_kernel(n_tp, me_ref, own_hbm, *refs):
+    hidden, (wk_hbm, wv_hbm, k_ref, v_ref, own_ref, wk_ref, wv_ref, sems, own_sem) = refs[:n_tp - 1], refs[n_tp - 1:]
+    me = me_ref[0]
+    length, width = own_ref.shape
+
+    def fetch(i):
+        rows = pl.ds(pl.multiple_of((me ^ i) * width, width), width)
+        return (pltpu.make_async_copy(wk_hbm.at[rows], wk_ref.at[i], sems.at[0, i]),
+                pltpu.make_async_copy(wv_hbm.at[rows], wv_ref.at[i], sems.at[1, i]))
+
+    order = list(range(1, n_tp)) + [0]
+    for i in order:
+        for copy in fetch(i):
+            copy.start()
+    own = pltpu.make_async_copy(own_hbm, own_ref, own_sem)
+    own.start()
     new_k = jnp.zeros((length, HD), F32)
     new_v = jnp.zeros((length, HD), F32)
-    for i in range(n_tp):
-        rows = pl.ds(pl.multiple_of((me ^ i) * width, width), width)
-        piece = hidden[i][...]
-        new_k += dot(piece, wk_ref[rows, :], ((1,), (0,)))
-        new_v += dot(piece, wv_ref[rows, :], ((1,), (0,)))
+    for i in order:
+        for copy in fetch(i):
+            copy.wait()
+        if i == 0:
+            own.wait()
+        piece = hidden[i - 1][...] if i else own_ref[...]
+        new_k += dot(piece, wk_ref[i], ((1,), (0,)))
+        new_v += dot(piece, wv_ref[i], ((1,), (0,)))
     k_ref[...] = new_k.astype(BF16)
     v_ref[...] = new_v.astype(BF16)
 
@@ -126,15 +155,23 @@
         out[...] = dot(ctx, w_ref[:, cols], ((1,), (0,))).astype(BF16)
 
 
-def near_kernel(order, me_ref, w_ref, *refs):
-    grads, out = refs[:-1], refs[-1]
-    me = me_ref[0]
-    width = grads[0].shape[1]
-    total = jnp.zeros(out.shape, F32)
-    for i, grad in zip(order, grads):
+def near_kernel(me_ref, w_hbm, own_hbm, near_ref, out, w_buf, own_ref, sems, own_sem):
+    me = me_ref[0]
+    width = near_ref.shape[1]
+
+    def fetch(i):
         cols = pl.ds(pl.multiple_of((me ^ i) * width, 128), width)
-        total += dot(grad[...], w_ref[:, cols], ((1,), (1,)))
-    out[...] = total
+        return pltpu.make_async_copy(w_hbm.at[:, cols], w_buf.at[i], sems.at[i])
+
+    fetch(1).start()
+    fetch(0).start()
+    own = pltpu.make_async_copy(own_hbm, own_ref, own_sem)
+    own.start()
+    fetch(1).wait()
+    total = dot(near_ref[...], w_buf[1], ((1,), (1,)))
+    fetch(0).wait()
+    own.wait()
+    out[...] = total + dot(own_ref[...], w_buf[0], ((1,), (1,)))
 
 
 def backward_kernel(order, n_pre, scaling, me_ref, w_ref, near_ref, q_ref, newv_ref, exps_ref, row_ref, col_ref, *refs):
@@ -225,12 +262,13 @@
         picked = pl.pallas_call(
             functools.partial(pick_kernel, n_seq, cap, here),
             out_shape=[shape] * n_seq,
-            in_specs=[SMEM, SMEM, VMEM, VMEM],
+            in_specs=[SMEM, HBM, HBM, HBM],
             out_specs=[VMEM] * n_seq,
+            scratch_shapes=[pltpu.SMEM(reads.shape, jnp.int32), pltpu.SemaphoreType.DMA, pltpu.SemaphoreType.DMA],
             cost_estimate=cost(0, 2 ** 20),
             compiler_params=grant(4),
             name="pick",
-        )(me_seq, reads, prefix_keys, prefix_values)
+        )(me_seq, hbm(reads), hbm(prefix_keys), hbm(prefix_values))
         moved = {k: hop(picked[k], "seq", k) for k in far_first}
         prefix = [picked[0]] + [moved[k] for k in range(1, n_seq)]
     else:
@@ -257,22 +295,35 @@
     new_k, new_v = pl.pallas_call(
         functools.partial(kv_kernel, n_tp),
         out_shape=[new_kv] * 2,
-        in_specs=[SMEM] + [VMEM] * (n_tp + 2),
+        in_specs=[SMEM, HBM] + [VMEM] * (n_tp - 1) + [HBM] * 2,
         out_specs=[VMEM] * 2,
+        scratch_shapes=[
+            pltpu.VMEM((length, width), BF16),
+            pltpu.VMEM((n_tp, width, HD), BF16),
+            pltpu.VMEM((n_tp, width, HD), BF16),
+            pltpu.SemaphoreType.DMA((2, n_tp)),
+            pltpu.SemaphoreType.DMA,
+        ],
         compiler_params=grant(8),
         cost_estimate=cost(5e8, 4e6),
         name="kv",
-    )(me_tp, hidden_states, near_hidden, far_hidden, last_hidden, key_weight, value_weight)
+    )(me_tp, hbm(hidden_states), near_hidden, far_hidden, last_hidden, hbm(key_weight), hbm(value_weight))
 
     near = pl.pallas_call(
-        functools.partial(near_kernel, (0, 1)),
+        near_kernel,
         out_shape=jax.ShapeDtypeStruct((length, heads * HD), F32),
-        in_specs=[SMEM] + [VMEM] * 3,
+        in_specs=[SMEM, HBM, HBM, VMEM],
         out_specs=VMEM,
+        scratch_shapes=[
+            pltpu.VMEM((2, heads * HD, width), BF16),
+            pltpu.VMEM((length, width), BF16),
+            pltpu.SemaphoreType.DMA((2,)),
+            pltpu.SemaphoreType.DMA,
+        ],
         compiler_params=grant(16),
         cost_estimate=cost(1e9, 8e6),
         name="near",
-    )(me_tp, output_weight, out_grad, near_grad)
+    )(me_tp, hbm(output_weight), hbm(out_grad), near_grad)
 
     ctx, exps, row, col = pl.pallas_call(
         functools.partial(forward_kernel, n_pre, scaling),

time: 82.1 us -> 81.3 us (level)
  local copies, waits for them, and re-layouts: 6.78 us -> 1.05 us
  Pallas kernels: 17.1 us -> 22.2 us
    unnamed x24 -> x14, local copies, waits for them, and re-layouts: 6.78 us -> 1.05 us
    pallas_call x1, Pallas kernels: 1.3 us -> 3.31 us  [local(): pl.pallas_call(near_kernel, out_shape=jax.ShapeDtypeStruct((length, heads...]
    pallas_call x1, Pallas kernels: 1.13 us -> 2.9 us  [local(): pl.pallas_call(functools.partial(kv_kernel, n_tp), out_shape=[new_kv] * 2...]
    pallas_call x1, Pallas kernels: 0.72 us -> 2.11 us  [local(): pl.pallas_call(functools.partial(pick_kernel, n_seq, cap, here), out_shap...]
  transfers between devices with their start and end apart: 23 -> 23, of which waited for: 7 -> 8; matrix products, arithmetic and copies ran while one was open for 0% -> 0% of each run, Pallas kernels for 21% -> 27%
where the time goes in v1:
time: 81.3 us; the launch traced here: 81 us
  starting transfers between devices  32.6 us (40%)
  waiting for transfers between devices  23.2 us (29%)
  Pallas kernels  22.2 us (27%)
  other arithmetic  1.06 us (1%)
  local copies, waits for them, and re-layouts  1.05 us (1%)
    ppermute x23, starting transfers between devices, hop(): return lax.ppermute(x, axis, [(i, i ^ k) for i in range(n)])  32.6 us
    ppermute x23, waiting for transfers between devices, hop(): return lax.ppermute(x, axis, [(i, i ^ k) for i in range(n)])  23.2 us
    pallas_call x1, Pallas kernels, local(): pl.pallas_call(functools.partial(backward_kernel, (2, 3), n_pre, scaling)...  6.09 us
    pallas_call x1, Pallas kernels, local(): pl.pallas_call(functools.partial(forward_kernel, n_pre, scaling), out_sha...  3.94 us
    pallas_call x1, Pallas kernels, local(): pl.pallas_call(near_kernel, out_shape=jax.ShapeDtypeStruct((length, heads...  3.31 us
    pallas_call x1, Pallas kernels, local(): pl.pallas_call(functools.partial(kv_kernel, n_tp), out_shape=[new_kv] * 2...  2.9 us
    pallas_call x2, Pallas kernels, project(): pl.pallas_call(functools.partial(project_kernel, order), out_shape=[jax.S...  2.47 us
    pallas_call x1, Pallas kernels, local(): pl.pallas_call(functools.partial(pick_kernel, n_seq, cap, here), out_shap...  2.11 us
  transfers between devices with their start and end apart: 23, of which 8 were waited for; matrix products, arithmetic and copies ran while one was open for 0% of the time, Pallas kernels for 27%

profile of v1, /device:TPU:0, one launch (start us, length us, event | category | flops | bytes accessed | tf_op | source)
XLA Modules:
  0.0 81.0 jit_solution(6522734912564960796)
XLA Ops:
  0.6 3.1 %collective-permute-start.1 = (bf16[256,896]{1,0:T(8,128)(2,1)}, bf16[256,896]{1,0:T(8,128)(2,1)S(1)}, u32[]{:S(2)}, u32[]{:S(2)}) collective-permute-start(bf16[256,896]{1,0:T(8,128)(2,1)} %own_hbm.2), channel_id=1, source_target_pairs={{0,2},{1,3},{2,0},{3,1},{4,6},{5,7},{6,4},{7,5},{8,10},{9,11},{10,... | collective-permute-start | bytes 1376264 | tf_op jit(solution)/shard_map/ppermute | solution.py:247
  3.7 10.7 %collective-permute-done.1.refs_1_ = bf16[256,896]{1,0:T(8,128)(2,1)S(1)} collective-permute-done((bf16[256,896]{1,0:T(8,128)(2,1)}, bf16[256,896]{1,0:T(8,128)(2,1)S(1)}, u32[]{:S(2)}, u32[]{:S(2)}) %collective-permute-start.1) | collective-permute-done | bytes 458784 | tf_op jit(solution)/shard_map/ppermute | solution.py:247
  14.4 2.1 %pick.1 = (bf16[128,256]{1,0:T(8,128)(2,1)S(1)}, bf16[128,256]{1,0:T(8,128)(2,1)S(1)}, bf16[128,256]{1,0:T(8,128)(2,1)S(1)}, bf16[128,256]{1,0:T(8,128)(2,1)S(1)...) custom-call(s32[1]{0:T(128)} %bitcast.1.me_ref, ...), custom_call_target="tpu_custom_call" | custom-call | bytes 1048576 | tf_op jit(solution)/shard_map/pick/pallas_call | solution.py:262
  16.5 1.5 %collective-permute-start.3 = (bf16[128,256]{1,0:T(8,128)(2,1)S(1)}, bf16[128,256]{1,0:T(8,128)(2,1)S(1)}, u32[]{:S(2)}, u32[]{:S(2)}) collective-permute-start(bf16[128,256]{1,0:T(8,128)(2,1)S(1)} %get-tuple-element.33), channel_id=1, source_target_pairs={{0,4},{4,0},{8,12},{12,8},{16,20},{20,16},{24,28},{28,24},{1,5},{5... | collective-permute-start | bytes 196616 | tf_op jit(solution)/shard_map/ppermute | solution.py:247
  18.1 1.6 %collective-permute-start.4 = (bf16[128,256]{1,0:T(8,128)(2,1)S(1)}, bf16[128,256]{1,0:T(8,128)(2,1)S(1)}, u32[]{:S(2)}, u32[]{:S(2)}) collective-permute-start(bf16[128,256]{1,0:T(8,128)(2,1)S(1)} %get-tuple-element.34), channel_id=1, source_target_pairs={{0,8},{4,12},{8,0},{12,4},{16,24},{20,28},{24,16},{28,20},{1,9},{5... | collective-permute-start | bytes 196616 | tf_op jit(solution)/shard_map/ppermute | solution.py:247
  21.1 2.6 %collective-permute-start.6 = (bf16[128,256]{1,0:T(8,128)(2,1)S(1)}, bf16[128,256]{1,0:T(8,128)(2,1)S(1)}, u32[]{:S(2)}, u32[]{:S(2)}) collective-permute-start(bf16[128,256]{1,0:T(8,128)(2,1)S(1)} %get-tuple-element.36), channel_id=1, source_target_pairs={{0,16},{4,20},{8,24},{12,28},{16,0},{20,4},{24,8},{28,12},{1,17},{... | collective-permute-start | bytes 196616 | tf_op jit(solution)/shard_map/ppermute | solution.py:247
  23.7 1.3 %collective-permute-start.7 = (bf16[128,256]{1,0:T(8,128)(2,1)S(1)}, bf16[128,256]{1,0:T(8,128)(2,1)S(1)}, u32[]{:S(2)}, u32[]{:S(2)}) collective-permute-start(bf16[128,256]{1,0:T(8,128)(2,1)S(1)} %get-tuple-element.37), channel_id=1, source_target_pairs={{0,20},{4,16},{8,28},{12,24},{16,4},{20,0},{24,12},{28,8},{1,21},{... | collective-permute-start | bytes 196616 | tf_op jit(solution)/shard_map/ppermute | solution.py:247
  24.9 3.6 %collective-permute-start.8 = (bf16[128,256]{1,0:T(8,128)(2,1)S(1)}, bf16[128,256]{1,0:T(8,128)(2,1)S(1)}, u32[]{:S(2)}, u32[]{:S(2)}) collective-permute-start(bf16[128,256]{1,0:T(8,128)(2,1)S(1)} %get-tuple-element.38), channel_id=1, source_target_pairs={{0,24},{4,28},{8,16},{12,20},{16,8},{20,12},{24,0},{28,4},{1,25},{... | collective-permute-start | bytes 196616 | tf_op jit(solution)/shard_map/ppermute | solution.py:247
  28.6 1.3 %collective-permute-start.9 = (bf16[128,256]{1,0:T(8,128)(2,1)S(1)}, bf16[128,256]{1,0:T(8,128)(2,1)S(1)}, u32[]{:S(2)}, u32[]{:S(2)}) collective-permute-start(bf16[128,256]{1,0:T(8,128)(2,1)S(1)} %get-tuple-element.39), channel_id=1, source_target_pairs={{0,28},{4,24},{8,20},{12,16},{16,12},{20,8},{24,4},{28,0},{1,29},{... | collective-permute-start | bytes 196616 | tf_op jit(solution)/shard_map/ppermute | solution.py:247
  29.9 2.9 %kv.1 = (bf16[256,128]{1,0:T(8,128)(2,1)S(1)}, bf16[256,128]{1,0:T(8,128)(2,1)S(1)}) custom-call(s32[1]{0:T(128)} %bitcast.me_ref, bf16[256,896]{1,0:T(8,128)(2,1)} %own_hbm.2, bf16[256,896]{1,0:T(8,128)(2,1)S(1)} %collective-permute-done.refs_0_, bf16[256,896]{1,0:T(8,128)(2,1)S(1)} %collective-permute-done.1.refs_1_, ...), custom_call_target="tpu_custom_call" | custom-call | flops 500000000 | bytes 4000000 | tf_op jit(solution)/shard_map/kv/pallas_call | solution.py:295
  32.9 1.6 %collective-permute-start.14 = (bf16[256,896]{1,0:T(8,128)(2,1)}, bf16[256,896]{1,0:T(8,128)(2,1)S(1)}, u32[]{:S(2)}, u32[]{:S(2)}) collective-permute-start(bf16[256,896]{1,0:T(8,128)(2,1)} %own_hbm.3), channel_id=1, source_target_pairs={{0,2},{1,3},{2,0},{3,1},{4,6},{5,7},{6,4},{7,5},{8,10},{9,11},{10,... | collective-permute-start | bytes 1376264 | tf_op jit(solution)/shard_map/ppermute | solution.py:247
  36.7 3.9 %forward.1 = (bf16[256,896]{1,0:T(8,128)(2,1)S(1)}, bf16[1280,1792]{1,0:T(8,128)(2,1)S(1)}, f32[8,256]{1,0:T(8,128)S(1)}, f32[256,128]{1,0:T(8,128)S(1)}) custom-call(bf16[256,896]{1,0:T(8,128)(2,1)S(1)} %copy-done.1, bf16[256,128]{1,0:T(8,128)(2,1)S(1)} %get-tuple-element.30.newk_ref, bf16[256,128]{1,0:T(8,128)(2,1)S(1)} %get-tuple-element.31.newv_ref, ...), custom_call_target="tpu_custom_call" | custom-call | flops 5000000000 | bytes 10000000 | tf_op jit(solution)/shard_map/forward/pallas_call | solution.py:328
  41.5 4.5 %collective-permute-done.14.refs_0_ = bf16[256,896]{1,0:T(8,128)(2,1)S(1)} collective-permute-done((bf16[256,896]{1,0:T(8,128)(2,1)}, bf16[256,896]{1,0:T(8,128)(2,1)S(1)}, u32[]{:S(2)}, u32[]{:S(2)}) %collective-permute-start.14) | collective-permute-done | bytes 458784 | tf_op jit(solution)/shard_map/ppermute | solution.py:247
  46.0 3.3 %near.1.near_ref = f32[256,896]{1,0:T(8,128)S(1)} custom-call(s32[1]{0:T(128)} %bitcast.me_ref, bf16[896,3584]{1,0:T(8,128)(2,1)} %w_ref.5, bf16[256,896]{1,0:T(8,128)(2,1)} %own_hbm.3, bf16[256,896]{1,0:T(8,128)(2,1)S(1)} %collective-permute-done.13.near_ref), custom_call_target="tpu_custom_call" | custom-call | flops 1000000000 | bytes 8000000 | tf_op jit(solution)/shard_map/near/pallas_call | solution.py:312
  49.3 1.8 %shard_map.112 = (bf16[256,896]{1,0:T(8,128)(2,1)S(1)}, bf16[256,896]{1,0:T(8,128)(2,1)S(1)}, bf16[256,896]{1,0:T(8,128)(2,1)S(1)}) custom-call(s32[1]{0:T(128)} %bitcast.me_ref, bf16[256,896]{1,0:T(8,128)(2,1)S(1)} %get-tuple-element.40.ctx_ref, bf16[896,3584]{1,0:T(8,128)(2,1)S(1)} %bitcast.5), custom_call_target="tpu_custom_call" | custom-call | flops 1500000000 | bytes 6000000 | tf_op jit(solution)/shard_map/pallas_call | solution.py:349
  51.8 1.6 %collective-permute-start.12 = (bf16[256,896]{1,0:T(8,128)(2,1)S(1)}, bf16[256,896]{1,0:T(8,128)(2,1)S(1)}, u32[]{:S(2)}, u32[]{:S(2)}) collective-permute-start(bf16[256,896]{1,0:T(8,128)(2,1)S(1)} %add_convert_fusion.1), channel_id=1, source_target_pairs={{0,2},{1,3},{2,0},{3,1},{4,6},{5,7},{6,4},{7,5},{8,10},{9,11},{10,... | collective-permute-start | bytes 1376264 | tf_op jit(solution)/shard_map/ppermute | solution.py:247
  53.4 6.1 %backward.1 = (bf16[128,256]{1,0:T(8,128)(2,1)S(1)}, bf16[128,256]{1,0:T(8,128)(2,1)S(1)}, bf16[128,256]{1,0:T(8,128)(2,1)S(1)}, bf16[128,256]{1,0:T(8,128)(2,1)...) custom-call(s32[1]{0:T(128)} %bitcast.me_ref, ...), custom_call_target="tpu_custom_call" | custom-call | flops 7000000000 | bytes 10000000 | tf_op jit(solution)/shard_map/backward/pallas_call | solution.py:367
  60.0 3.1 %collective-permute-start.18 = (bf16[128,256]{1,0:T(8,128)(2,1)S(1)}, bf16[128,256]{1,0:T(8,128)(2,1)S(1)}, u32[]{:S(2)}, u32[]{:S(2)}) collective-permute-start(bf16[128,256]{1,0:T(8,128)(2,1)S(1)} %get-tuple-element.50), channel_id=1, source_target_pairs={{0,12},{4,8},{8,4},{12,0},{16,28},{20,24},{24,20},{28,16},{1,13},{... | collective-permute-start | bytes 196616 | tf_op jit(solution)/shard_map/ppermute | solution.py:247
  64.5 2.1 %collective-permute-start.20 = (bf16[128,256]{1,0:T(8,128)(2,1)S(1)}, bf16[128,256]{1,0:T(8,128)(2,1)S(1)}, u32[]{:S(2)}, u32[]{:S(2)}) collective-permute-start(bf16[128,256]{1,0:T(8,128)(2,1)S(1)} %get-tuple-element.52), channel_id=1, source_target_pairs={{0,20},{4,16},{8,28},{12,24},{16,4},{20,0},{24,12},{28,8},{1,21},{... | collective-permute-start | bytes 196616 | tf_op jit(solution)/shard_map/ppermute | solution.py:247
  66.6 3.7 %collective-permute-start.21 = (bf16[128,256]{1,0:T(8,128)(2,1)S(1)}, bf16[128,256]{1,0:T(8,128)(2,1)S(1)}, u32[]{:S(2)}, u32[]{:S(2)}) collective-permute-start(bf16[128,256]{1,0:T(8,128)(2,1)S(1)} %get-tuple-element.53), channel_id=1, source_target_pairs={{0,24},{4,28},{8,16},{12,20},{16,8},{20,12},{24,0},{28,4},{1,25},{... | collective-permute-start | bytes 196616 | tf_op jit(solution)/shard_map/ppermute | solution.py:247
  70.2 1.4 %collective-permute-done.19.refs_4_ = bf16[128,256]{1,0:T(8,128)(2,1)S(1)} collective-permute-done((bf16[128,256]{1,0:T(8,128)(2,1)S(1)}, bf16[128,256]{1,0:T(8,128)(2,1)S(1)}, u32[]{:S(2)}, u32[]{:S(2)}) %collective-permute-start.19) | collective-permute-done | bytes 65568 | tf_op jit(solution)/shard_map/ppermute | solution.py:247
  71.6 3.8 %collective-permute-start.22 = (bf16[128,256]{1,0:T(8,128)(2,1)S(1)}, bf16[128,256]{1,0:T(8,128)(2,1)S(1)}, u32[]{:S(2)}, u32[]{:S(2)}) collective-permute-start(bf16[128,256]{1,0:T(8,128)(2,1)S(1)} %get-tuple-element.54), channel_id=1, source_target_pairs={{0,28},{4,24},{8,20},{12,16},{16,12},{20,8},{24,4},{28,0},{1,29},{... | collective-permute-start | bytes 196616 | tf_op jit(solution)/shard_map/ppermute | solution.py:247
  75.4 3.2 %collective-permute-done.22.refs_7_ = bf16[128,256]{1,0:T(8,128)(2,1)S(1)} collective-permute-done((bf16[128,256]{1,0:T(8,128)(2,1)S(1)}, bf16[128,256]{1,0:T(8,128)(2,1)S(1)}, u32[]{:S(2)}, u32[]{:S(2)}) %collective-permute-start.22) | collective-permute-done | bytes 65568 | tf_op jit(solution)/shard_map/ppermute | solution.py:247
  78.6 1.4 %place.1 = (f32[256,128]{1,0:T(8,128)}, f32[256,128]{1,0:T(8,128)}) custom-call(s32[1]{0:T(128)} %bitcast.1.me_ref, s32[8,16]{1,0:T(8,128)S(1)} %copy-done, bf16[128,256]{1,0:T(8,128)(2,1)S(1)} %get-tuple-element.47.refs_0_, bf16[128,256]{1,0:T(8,128)(2,1)S(1)} %collective-permute-done.16.refs_1_, bf16[128,256]{1,0:T(8,128)(2,1)S(1)} %collective-permute-done.17.refs_2_, ...), custom_call_target="tpu_custom_call" | custom-call | bytes 1048576 | tf_op jit(solution)/shard_map/place/pallas_call | solution.py:387
  (48 shorter events, 8.1 us)
Async XLA Ops:
  0.6 13.8 %collective-permute-start.1 = (bf16[256,896]{1,0:T(8,128)(2,1)}, bf16[256,896]{1,0:T(8,128)(2,1)S(1)}, u32[]{:S(2)}, u32[]{:S(2)}) collective-permute-start(bf16[256,896]{1,0:T(8,128)(2,1)} %own_hbm.2), channel_id=1, source_target_pairs={{0,2},{1,3},{2,0},{3,1},{4,6},{5,7},{6,4},{7,5},{8,10},{9,11},{10,... | collective-permute-start | bytes 1376264 | tf_op jit(solution)/shard_map/ppermute | solution.py:247
  3.7 21.2 %collective-permute-start = (bf16[256,896]{1,0:T(8,128)(2,1)}, bf16[256,896]{1,0:T(8,128)(2,1)S(1)}, u32[]{:S(2)}, u32[]{:S(2)}) collective-permute-start(bf16[256,896]{1,0:T(8,128)(2,1)} %own_hbm.2), channel_id=1, source_target_pairs={{0,1},{1,0},{2,3},{3,2},{4,5},{5,4},{6,7},{7,6},{8,9},{9,8},{10,11... | collective-permute-start | bytes 1376264 | tf_op jit(solution)/shard_map/ppermute | solution.py:247
  14.4 14.2 %collective-permute-start.2 = (bf16[256,896]{1,0:T(8,128)(2,1)S(1)}, bf16[256,896]{1,0:T(8,128)(2,1)S(1)}, u32[]{:S(2)}, u32[]{:S(2)}) collective-permute-start(bf16[256,896]{1,0:T(8,128)(2,1)S(1)} %collective-permute-done.1.refs_1_), channel_id=1, source_target_pairs={{0,1},{1,0},{2,3},{3,2},{4,5},{5,4},{6,7},{7,6},{8,9},{9,8},{10,11... | collective-permute-start | bytes 1376264 | tf_op jit(solution)/shard_map/ppermute | solution.py:247
  16.5 4.6 %collective-permute-start.3 = (bf16[128,256]{1,0:T(8,128)(2,1)S(1)}, bf16[128,256]{1,0:T(8,128)(2,1)S(1)}, u32[]{:S(2)}, u32[]{:S(2)}) collective-permute-start(bf16[128,256]{1,0:T(8,128)(2,1)S(1)} %get-tuple-element.33), channel_id=1, source_target_pairs={{0,4},{4,0},{8,12},{12,8},{16,20},{20,16},{24,28},{28,24},{1,5},{5... | collective-permute-start | bytes 196616 | tf_op jit(solution)/shard_map/ppermute | solution.py:247
  18.1 5.6 %collective-permute-start.4 = (bf16[128,256]{1,0:T(8,128)(2,1)S(1)}, bf16[128,256]{1,0:T(8,128)(2,1)S(1)}, u32[]{:S(2)}, u32[]{:S(2)}) collective-permute-start(bf16[128,256]{1,0:T(8,128)(2,1)S(1)} %get-tuple-element.34), channel_id=1, source_target_pairs={{0,8},{4,12},{8,0},{12,4},{16,24},{20,28},{24,16},{28,20},{1,9},{5... | collective-permute-start | bytes 196616 | tf_op jit(solution)/shard_map/ppermute | solution.py:247
  19.7 13.1 %collective-permute-start.5 = (bf16[128,256]{1,0:T(8,128)(2,1)S(1)}, bf16[128,256]{1,0:T(8,128)(2,1)S(1)}, u32[]{:S(2)}, u32[]{:S(2)}) collective-permute-start(bf16[128,256]{1,0:T(8,128)(2,1)S(1)} %get-tuple-element.35), channel_id=1, source_target_pairs={{0,12},{4,8},{8,4},{12,0},{16,28},{20,24},{24,20},{28,16},{1,13},{... | collective-permute-start | bytes 196616 | tf_op jit(solution)/shard_map/ppermute | solution.py:247
  21.1 11.7 %collective-permute-start.6 = (bf16[128,256]{1,0:T(8,128)(2,1)S(1)}, bf16[128,256]{1,0:T(8,128)(2,1)S(1)}, u32[]{:S(2)}, u32[]{:S(2)}) collective-permute-start(bf16[128,256]{1,0:T(8,128)(2,1)S(1)} %get-tuple-element.36), channel_id=1, source_target_pairs={{0,16},{4,20},{8,24},{12,28},{16,0},{20,4},{24,8},{28,12},{1,17},{... | collective-permute-start | bytes 196616 | tf_op jit(solution)/shard_map/ppermute | solution.py:247
  23.7 10.8 %collective-permute-start.7 = (bf16[128,256]{1,0:T(8,128)(2,1)S(1)}, bf16[128,256]{1,0:T(8,128)(2,1)S(1)}, u32[]{:S(2)}, u32[]{:S(2)}) collective-permute-start(bf16[128,256]{1,0:T(8,128)(2,1)S(1)} %get-tuple-element.37), channel_id=1, source_target_pairs={{0,20},{4,16},{8,28},{12,24},{16,4},{20,0},{24,12},{28,8},{1,21},{... | collective-permute-start | bytes 196616 | tf_op jit(solution)/shard_map/ppermute | solution.py:247
  24.9 9.5 %collective-permute-start.8 = (bf16[128,256]{1,0:T(8,128)(2,1)S(1)}, bf16[128,256]{1,0:T(8,128)(2,1)S(1)}, u32[]{:S(2)}, u32[]{:S(2)}) collective-permute-start(bf16[128,256]{1,0:T(8,128)(2,1)S(1)} %get-tuple-element.38), channel_id=1, source_target_pairs={{0,24},{4,28},{8,16},{12,20},{16,8},{20,12},{24,0},{28,4},{1,25},{... | collective-permute-start | bytes 196616 | tf_op jit(solution)/shard_map/ppermute | solution.py:247
  28.6 7.1 %collective-permute-start.9 = (bf16[128,256]{1,0:T(8,128)(2,1)S(1)}, bf16[128,256]{1,0:T(8,128)(2,1)S(1)}, u32[]{:S(2)}, u32[]{:S(2)}) collective-permute-start(bf16[128,256]{1,0:T(8,128)(2,1)S(1)} %get-tuple-element.39), channel_id=1, source_target_pairs={{0,28},{4,24},{8,20},{12,16},{16,12},{20,8},{24,4},{28,0},{1,29},{... | collective-permute-start | bytes 196616 | tf_op jit(solution)/shard_map/ppermute | solution.py:247
  32.8 13.2 %collective-permute-start.13 = (bf16[256,896]{1,0:T(8,128)(2,1)}, bf16[256,896]{1,0:T(8,128)(2,1)S(1)}, u32[]{:S(2)}, u32[]{:S(2)}) collective-permute-start(bf16[256,896]{1,0:T(8,128)(2,1)} %own_hbm.3), channel_id=1, source_target_pairs={{0,1},{1,0},{2,3},{3,2},{4,5},{5,4},{6,7},{7,6},{8,9},{9,8},{10,11... | collective-permute-start | bytes 1376264 | tf_op jit(solution)/shard_map/ppermute | solution.py:247
  32.9 13.1 %collective-permute-start.14 = (bf16[256,896]{1,0:T(8,128)(2,1)}, bf16[256,896]{1,0:T(8,128)(2,1)S(1)}, u32[]{:S(2)}, u32[]{:S(2)}) collective-permute-start(bf16[256,896]{1,0:T(8,128)(2,1)} %own_hbm.3), channel_id=1, source_target_pairs={{0,2},{1,3},{2,0},{3,1},{4,6},{5,7},{6,4},{7,5},{8,10},{9,11},{10,... | collective-permute-start | bytes 1376264 | tf_op jit(solution)/shard_map/ppermute | solution.py:247
  41.4 10.3 %collective-permute-start.11 = (bf16[256,896]{1,0:T(8,128)(2,1)S(1)}, bf16[256,896]{1,0:T(8,128)(2,1)S(1)}, u32[]{:S(2)}, u32[]{:S(2)}) collective-permute-start(bf16[256,896]{1,0:T(8,128)(2,1)S(1)} %shard_map.113), channel_id=1, source_target_pairs={{0,1},{1,0},{2,3},{3,2},{4,5},{5,4},{6,7},{7,6},{8,9},{9,8},{10,11... | collective-permute-start | bytes 1376264 | tf_op jit(solution)/shard_map/ppermute | solution.py:247
  46.0 7.4 %collective-permute-start.15 = (bf16[256,896]{1,0:T(8,128)(2,1)S(1)}, bf16[256,896]{1,0:T(8,128)(2,1)S(1)}, u32[]{:S(2)}, u32[]{:S(2)}) collective-permute-start(bf16[256,896]{1,0:T(8,128)(2,1)S(1)} %collective-permute-done.14.refs_0_), channel_id=1, source_target_pairs={{0,1},{1,0},{2,3},{3,2},{4,5},{5,4},{6,7},{7,6},{8,9},{9,8},{10,11... | collective-permute-start | bytes 1376264 | tf_op jit(solution)/shard_map/ppermute | solution.py:247
  51.1 28.9 %collective-permute-start.10 = (bf16[256,896]{1,0:T(8,128)(2,1)S(1)}, bf16[256,896]{1,0:T(8,128)(2,1)S(1)}, u32[]{:S(2)}, u32[]{:S(2)}) collective-permute-start(bf16[256,896]{1,0:T(8,128)(2,1)S(1)} %get-tuple-element.42), channel_id=1, source_target_pairs={{0,1},{1,0},{2,3},{3,2},{4,5},{5,4},{6,7},{7,6},{8,9},{9,8},{10,11... | collective-permute-start | bytes 1376264 | tf_op jit(solution)/shard_map/ppermute | solution.py:247
  51.8 28.2 %collective-permute-start.12 = (bf16[256,896]{1,0:T(8,128)(2,1)S(1)}, bf16[256,896]{1,0:T(8,128)(2,1)S(1)}, u32[]{:S(2)}, u32[]{:S(2)}) collective-permute-start(bf16[256,896]{1,0:T(8,128)(2,1)S(1)} %add_convert_fusion.1), channel_id=1, source_target_pairs={{0,2},{1,3},{2,0},{3,1},{4,6},{5,7},{6,4},{7,5},{8,10},{9,11},{10,... | collective-permute-start | bytes 1376264 | tf_op jit(solution)/shard_map/ppermute | solution.py:247
  53.4 25.2 %copy-start = (s32[8,16]{1,0:T(8,128)S(1)}, s32[8,16]{1,0:T(8,128)}, u32[]{:S(2)}) copy-start(s32[8,16]{1,0:T(8,128)} %reads_ref.1) | copy-start | bytes 1540
  59.5 4.3 %collective-permute-start.16 = (bf16[128,256]{1,0:T(8,128)(2,1)S(1)}, bf16[128,256]{1,0:T(8,128)(2,1)S(1)}, u32[]{:S(2)}, u32[]{:S(2)}) collective-permute-start(bf16[128,256]{1,0:T(8,128)(2,1)S(1)} %get-tuple-element.48), channel_id=1, source_target_pairs={{0,4},{4,0},{8,12},{12,8},{16,20},{20,16},{24,28},{28,24},{1,5},{5... | collective-permute-start | bytes 196616 | tf_op jit(solution)/shard_map/ppermute | solution.py:247
  59.9 4.6 %collective-permute-start.17 = (bf16[128,256]{1,0:T(8,128)(2,1)S(1)}, bf16[128,256]{1,0:T(8,128)(2,1)S(1)}, u32[]{:S(2)}, u32[]{:S(2)}) collective-permute-start(bf16[128,256]{1,0:T(8,128)(2,1)S(1)} %get-tuple-element.49), channel_id=1, source_target_pairs={{0,8},{4,12},{8,0},{12,4},{16,24},{20,28},{24,16},{28,20},{1,9},{5... | collective-permute-start | bytes 196616 | tf_op jit(solution)/shard_map/ppermute | solution.py:247
  60.0 6.6 %collective-permute-start.18 = (bf16[128,256]{1,0:T(8,128)(2,1)S(1)}, bf16[128,256]{1,0:T(8,128)(2,1)S(1)}, u32[]{:S(2)}, u32[]{:S(2)}) collective-permute-start(bf16[128,256]{1,0:T(8,128)(2,1)S(1)} %get-tuple-element.50), channel_id=1, source_target_pairs={{0,12},{4,8},{8,4},{12,0},{16,28},{20,24},{24,20},{28,16},{1,13},{... | collective-permute-start | bytes 196616 | tf_op jit(solution)/shard_map/ppermute | solution.py:247
  63.8 7.8 %collective-permute-start.19 = (bf16[128,256]{1,0:T(8,128)(2,1)S(1)}, bf16[128,256]{1,0:T(8,128)(2,1)S(1)}, u32[]{:S(2)}, u32[]{:S(2)}) collective-permute-start(bf16[128,256]{1,0:T(8,128)(2,1)S(1)} %get-tuple-element.51), channel_id=1, source_target_pairs={{0,16},{4,20},{8,24},{12,28},{16,0},{20,4},{24,8},{28,12},{1,17},{... | collective-permute-start | bytes 196616 | tf_op jit(solution)/shard_map/ppermute | solution.py:247
  64.5 10.9 %collective-permute-start.20 = (bf16[128,256]{1,0:T(8,128)(2,1)S(1)}, bf16[128,256]{1,0:T(8,128)(2,1)S(1)}, u32[]{:S(2)}, u32[]{:S(2)}) collective-permute-start(bf16[128,256]{1,0:T(8,128)(2,1)S(1)} %get-tuple-element.52), channel_id=1, source_target_pairs={{0,20},{4,16},{8,28},{12,24},{16,4},{20,0},{24,12},{28,8},{1,21},{... | collective-permute-start | bytes 196616 | tf_op jit(solution)/shard_map/ppermute | solution.py:247
  66.6 8.8 %collective-permute-start.21 = (bf16[128,256]{1,0:T(8,128)(2,1)S(1)}, bf16[128,256]{1,0:T(8,128)(2,1)S(1)}, u32[]{:S(2)}, u32[]{:S(2)}) collective-permute-start(bf16[128,256]{1,0:T(8,128)(2,1)S(1)} %get-tuple-element.53), channel_id=1, source_target_pairs={{0,24},{4,28},{8,16},{12,20},{16,8},{20,12},{24,0},{28,4},{1,25},{... | collective-permute-start | bytes 196616 | tf_op jit(solution)/shard_map/ppermute | solution.py:247
  71.6 7.0 %collective-permute-start.22 = (bf16[128,256]{1,0:T(8,128)(2,1)S(1)}, bf16[128,256]{1,0:T(8,128)(2,1)S(1)}, u32[]{:S(2)}, u32[]{:S(2)}) collective-permute-start(bf16[128,256]{1,0:T(8,128)(2,1)S(1)} %get-tuple-element.54), channel_id=1, source_target_pairs={{0,28},{4,24},{8,20},{12,16},{16,12},{20,8},{24,4},{28,0},{1,29},{... | collective-permute-start | bytes 196616 | tf_op jit(solution)/shard_map/ppermute | solution.py:247
  (6 other events, 44.4 us)

commit v2 on v0

--- a/solution.py
+++ b/solution.py
@@ -15,19 +15,33 @@
 BF16 = jnp.bfloat16
 VMEM = pl.BlockSpec(memory_space=pltpu.VMEM)
 SMEM = pl.BlockSpec(memory_space=pltpu.SMEM)
-ANY = pl.BlockSpec(memory_space=pl.ANY)
+HBM = pl.BlockSpec(memory_space=pltpu.HBM)
 
 
 def dot(a, b, dims):
     return lax.dot_general(a, b, (dims, ((), ())), preferred_element_type=F32)
 
 
+def hbm(x):
+    return pltpu.with_memory_space_constraint(x, pltpu.HBM)
+
+
 def cost(flops, nbytes, trans=0):
     return pl.CostEstimate(flops=int(flops), bytes_accessed=int(nbytes), transcendentals=int(trans))
 
 
-def pick_kernel(n, cap, here, me_ref, reads_ref, keys_ref, values_ref, *outs):
-    me = me_ref[0]
+def pick_kernel(n, cap, here, me_ref, reads_hbm, keys_hbm, values_hbm, *refs):
+    outs, (reads_ref, keys_ref, values_ref, sems) = refs[:n], refs[n:]
+    me = me_ref[0]
+    copies = [
+        pltpu.make_async_copy(src, dst, sems.at[i])
+        for i, (src, dst) in enumerate(
+            ((reads_hbm, reads_ref), (keys_hbm, keys_ref), (values_hbm, values_ref)))
+    ]
+    for copy in copies:
+        copy.start()
+    for copy in copies:
+        copy.wait()
     for k in range(n):
         for r in range(cap):
             block = reads_ref[me ^ k, cap * me + r] - here * me
@@ -50,25 +64,45 @@
             values_ref[rows, :] += piece[:, HD:]
 
 
-def kv_kernel(n_tp, me_ref, *refs):
-    hidden, (wk_ref, wv_ref, k_ref, v_ref) = refs[:n_tp], refs[n_tp:]
-    me = me_ref[0]
-    length, width = hidden[0].shape
-    new_k = jnp.zeros((length, HD), F32)
-    new_v = jnp.zeros((length, HD), F32)
-    for i in range(n_tp):
-        rows = pl.ds(pl.multiple_of((me ^ i) * width, width), width)
-        piece = hidden[i][...]
-        new_k += dot(piece, wk_ref[rows, :], ((1,), (0,)))
-        new_v += dot(piece, wv_ref[rows, :], ((1,), (0,)))
-    k_ref[...] = new_k.astype(BF16)
-    v_ref[...] = new_v.astype(BF16)
-
-
-def forward_kernel(n_pre, scaling, q_ref, newk_ref, newv_ref, *refs):
+def weight_copies(i, me, width, hbms, bufs, slot, sems):
+    rows = pl.ds(pl.multiple_of((me ^ i) * width, width), width)
+    return [pltpu.make_async_copy(w.at[rows], buf.at[slot], sems.at[j, slot]) for j, (w, buf) in enumerate(zip(hbms, bufs))]
+
+
+def kv_kernel(order, me_ref, own_hbm, *refs):
+    hidden, (wk_hbm, wv_hbm, k_ref, v_ref, own_ref, wk_ref, wv_ref, sems, own_sem) = refs[:-9], refs[-9:]
+    me = me_ref[0]
+    width = own_ref.shape[1]
+
+    def fetch(slot, i):
+        return weight_copies(i, me, width, (wk_hbm, wv_hbm), (wk_ref, wv_ref), slot, sems)
+
+    for slot, i in enumerate(order):
+        for copy in fetch(slot, i):
+            copy.start()
+    own = pltpu.make_async_copy(own_hbm, own_ref, own_sem)
+    own.start()
+    new_k = jnp.zeros(k_ref.shape, F32)
+    new_v = jnp.zeros(k_ref.shape, F32)
+    for slot, i in enumerate(order):
+        for copy in fetch(slot, i):
+            copy.wait()
+        if i == 0:
+            own.wait()
+        piece = hidden[i - 1][...] if i else own_ref[...]
+        new_k += dot(piece, wk_ref[slot], ((1,), (0,)))
+        new_v += dot(piece, wv_ref[slot], ((1,), (0,)))
+    k_ref[...] = new_k
+    v_ref[...] = new_v
+
+
+def forward_kernel(n_pre, scaling, last, me_ref, wk_hbm, wv_hbm, hidden_ref, q_ref, partk_ref, partv_ref, *refs):
     prefix = refs[:n_pre]
-    ctx_ref, exps_ref, row_ref, col_ref, vt_all, s_buf, sums = refs[n_pre:]
-    length = q_ref.shape[0]
+    ctx_ref, exps_ref, row_ref, col_ref, newv_ref, newk_ref, wk_ref, wv_ref, vt_all, s_buf, sums, sems = refs[n_pre:]
+    length, width = hidden_ref.shape
+    copies = weight_copies(last, me_ref[0], width, (wk_hbm, wv_hbm), (wk_ref, wv_ref), 0, sems)
+    for copy in copies:
+        copy.start()
     heads = q_ref.shape[1] // HD
     factor = scaling * LOG2E
     chunks = []
@@ -78,6 +112,11 @@
         vt_all[:, at:at + size] = ref[:, HD:].astype(F32).T.astype(BF16)
         chunks.append((at, size, ref))
         at += size
+    for copy in copies:
+        copy.wait()
+    piece = hidden_ref[...]
+    newk_ref[...] = (partk_ref[...] + dot(piece, wk_ref[0], ((1,), (0,)))).astype(BF16)
+    newv_ref[...] = (partv_ref[...] + dot(piece, wv_ref[0], ((1,), (0,)))).astype(BF16)
     vt_all[:, at:] = newv_ref[...].astype(F32).T.astype(BF16)
     visible = lax.broadcasted_iota(jnp.int32, (length, length), 0) <= lax.broadcasted_iota(
         jnp.int32, (length, length), 1)
@@ -126,25 +165,14 @@
         out[...] = dot(ctx, w_ref[:, cols], ((1,), (0,))).astype(BF16)
 
 
-def near_kernel(order, me_ref, w_ref, *refs):
-    grads, out = refs[:-1], refs[-1]
-    me = me_ref[0]
-    width = grads[0].shape[1]
-    total = jnp.zeros(out.shape, F32)
-    for i, grad in zip(order, grads):
-        cols = pl.ds(pl.multiple_of((me ^ i) * width, 128), width)
-        total += dot(grad[...], w_ref[:, cols], ((1,), (1,)))
-    out[...] = total
-
-
-def backward_kernel(order, n_pre, scaling, me_ref, w_ref, near_ref, q_ref, newv_ref, exps_ref, row_ref, col_ref, *refs):
+def backward_kernel(order, n_pre, scaling, me_ref, w_ref, q_ref, newv_ref, exps_ref, row_ref, col_ref, *refs):
     grads, prefix = refs[:len(order)], refs[len(order):len(order) + n_pre]
     outs = refs[len(order) + n_pre:len(order) + 2 * n_pre]
     g_all, q_all, dbuf, slopes = refs[len(order) + 2 * n_pre:]
     me = me_ref[0]
     length, width = grads[0].shape
     heads = q_ref.shape[1] // HD
-    total = near_ref[...]
+    total = jnp.zeros((length, heads * HD), F32)
     for i, grad in zip(order, grads):
         cols = pl.ds(pl.multiple_of((me ^ i) * width, 128), width)
         total += dot(grad[...], w_ref[:, cols], ((1,), (1,)))
@@ -225,12 +253,18 @@
         picked = pl.pallas_call(
             functools.partial(pick_kernel, n_seq, cap, here),
             out_shape=[shape] * n_seq,
-            in_specs=[SMEM, SMEM, VMEM, VMEM],
+            in_specs=[SMEM, HBM, HBM, HBM],
             out_specs=[VMEM] * n_seq,
+            scratch_shapes=[
+                pltpu.SMEM(reads.shape, jnp.int32),
+                pltpu.VMEM(prefix_keys.shape, BF16),
+                pltpu.VMEM(prefix_keys.shape, BF16),
+                pltpu.SemaphoreType.DMA((3,)),
+            ],
             cost_estimate=cost(0, 2 ** 20),
             compiler_params=grant(4),
             name="pick",
-        )(me_seq, reads, prefix_keys, prefix_values)
+        )(me_seq, hbm(reads), hbm(prefix_keys), hbm(prefix_values))
         moved = {k: hop(picked[k], "seq", k) for k in far_first}
         prefix = [picked[0]] + [moved[k] for k in range(1, n_seq)]
     else:
@@ -253,46 +287,47 @@
         prefix = [fetched.reshape(n_rows, 2 * HD)]
     n_pre = len(prefix)
 
-    new_kv = jax.ShapeDtypeStruct((length, HD), BF16)
-    new_k, new_v = pl.pallas_call(
-        functools.partial(kv_kernel, n_tp),
-        out_shape=[new_kv] * 2,
-        in_specs=[SMEM] + [VMEM] * (n_tp + 2),
+    weight_bufs = [pltpu.VMEM((n_tp - 1, width, HD), BF16)] * 2
+    part_k, part_v = pl.pallas_call(
+        functools.partial(kv_kernel, (1, 0, 2)),
+        out_shape=[jax.ShapeDtypeStruct((length, HD), F32)] * 2,
+        in_specs=[SMEM, HBM] + [VMEM] * (n_tp - 2) + [HBM] * 2,
         out_specs=[VMEM] * 2,
+        scratch_shapes=[
+            pltpu.VMEM((length, width), BF16),
+            *weight_bufs,
+            pltpu.SemaphoreType.DMA((2, n_tp - 1)),
+            pltpu.SemaphoreType.DMA,
+        ],
         compiler_params=grant(8),
-        cost_estimate=cost(5e8, 4e6),
+        cost_estimate=cost(4e8, 3e6),
         name="kv",
-    )(me_tp, hidden_states, near_hidden, far_hidden, last_hidden, key_weight, value_weight)
-
-    near = pl.pallas_call(
-        functools.partial(near_kernel, (0, 1)),
-        out_shape=jax.ShapeDtypeStruct((length, heads * HD), F32),
-        in_specs=[SMEM] + [VMEM] * 3,
-        out_specs=VMEM,
-        compiler_params=grant(16),
-        cost_estimate=cost(1e9, 8e6),
-        name="near",
-    )(me_tp, output_weight, out_grad, near_grad)
-
-    ctx, exps, row, col = pl.pallas_call(
-        functools.partial(forward_kernel, n_pre, scaling),
+    )(me_tp, hbm(hidden_states), near_hidden, far_hidden, hbm(key_weight), hbm(value_weight))
+
+    ctx, exps, row, col, new_v = pl.pallas_call(
+        functools.partial(forward_kernel, n_pre, scaling, n_tp - 1),
         out_shape=[
             jax.ShapeDtypeStruct((length, heads * HD), BF16),
             jax.ShapeDtypeStruct((keys, heads * length), BF16),
             jax.ShapeDtypeStruct((heads + (-heads) % 8, length), F32),
             jax.ShapeDtypeStruct((length, HD), F32),
+            jax.ShapeDtypeStruct((length, HD), BF16),
         ],
-        in_specs=[VMEM] * (3 + n_pre),
-        out_specs=[VMEM] * 4,
+        in_specs=[SMEM, HBM, HBM] + [VMEM] * (4 + n_pre),
+        out_specs=[VMEM] * 5,
         scratch_shapes=[
+            pltpu.VMEM((length, HD), BF16),
+            pltpu.VMEM((1, width, HD), BF16),
+            pltpu.VMEM((1, width, HD), BF16),
             pltpu.VMEM((HD, keys), BF16),
             pltpu.VMEM((2, keys, length), F32),
             pltpu.VMEM((HD, length), F32),
+            pltpu.SemaphoreType.DMA((2, 1)),
         ],
         compiler_params=grant(20),
         cost_estimate=cost(5e9, 1e7, 3e6),
         name="forward",
-    )(queries, new_k, new_v, *prefix)
+    )(me_tp, hbm(key_weight), hbm(value_weight), last_hidden, queries, part_k, part_v, *prefix)
 
     def project(order):
         return pl.pallas_call(
@@ -314,9 +349,9 @@
 
     grad_type = BF16 if dense else F32
     parts = pl.pallas_call(
-        functools.partial(backward_kernel, (2, 3), n_pre, scaling),
+        functools.partial(backward_kernel, (0, 1, 2, 3), n_pre, scaling),
         out_shape=[jax.ShapeDtypeStruct(x.shape, grad_type) for x in prefix],
-        in_specs=[SMEM] + [VMEM] * (9 + n_pre),
+        in_specs=[SMEM] + [VMEM] * (10 + n_pre),
         out_specs=[VMEM] * n_pre,
         scratch_shapes=[
             pltpu.VMEM((heads * length, HD), BF16),
@@ -327,7 +362,7 @@
         compiler_params=grant(32),
         cost_estimate=cost(7e9, 1e7),
         name="backward",
-    )(me_tp, output_weight, near, queries, new_v, exps, row, col, far_grad, last_grad, *prefix)
+    )(me_tp, output_weight, queries, new_v, exps, row, col, out_grad, near_grad, far_grad, last_grad, *prefix)
 
     if dense:
         back = {k: hop(parts[k], "seq", k) for k in far_first}

time: 82.1 us -> 75.8 us (0.923)
  waiting for transfers between devices: 23 us -> 16.3 us
  local copies, waits for them, and re-layouts: 6.78 us -> 1.23 us
  Pallas kernels: 17.1 us -> 20.2 us
  starting transfers between devices: 33 us -> 36 us
    ppermute x23, waiting for transfers between devices: 23 us -> 16.3 us  [hop(): return lax.ppermute(x, axis, [(i, i ^ k) for i in range(n)])]
    unnamed x24 -> x12, local copies, waits for them, and re-layouts: 6.78 us -> 1.23 us
    ppermute x23, starting transfers between devices: 33 us -> 36 us  [hop(): return lax.ppermute(x, axis, [(i, i ^ k) for i in range(n)])]
    pallas_call x4 -> x3, Pallas kernels: 12.5 us -> 15.3 us  [the longest x1 7.11 us: local(): pl.pallas_call(functools.partial(backward_kernel, (0, 1, 2, 3), n_pre, sc...]
  transfers between devices with their start and end apart: 23 -> 23, of which waited for: 7 -> 6; matrix products, arithmetic and copies ran while one was open for 0% -> 0% of each run, Pallas kernels for 21% -> 27%
where the time goes in v2:
time: 75.8 us; the launch traced here: 75.6 us
  starting transfers between devices  36 us (47%)
  Pallas kernels  20.2 us (27%)
  waiting for transfers between devices  16.3 us (22%)
  local copies, waits for them, and re-layouts  1.23 us (2%)
  other arithmetic  1.06 us (1%)
  between operations  0.77 us (1%)
    ppermute x23, starting transfers between devices, hop(): return lax.ppermute(x, axis, [(i, i ^ k) for i in range(n)])  36 us
    ppermute x23, waiting for transfers between devices, hop(): return lax.ppermute(x, axis, [(i, i ^ k) for i in range(n)])  16.3 us
    pallas_call x1, Pallas kernels, local(): pl.pallas_call(functools.partial(backward_kernel, (0, 1, 2, 3), n_pre, sc...  7.11 us
    pallas_call x1, Pallas kernels, local(): pl.pallas_call(functools.partial(forward_kernel, n_pre, scaling, n_tp - 1...  5.42 us
    pallas_call x1, Pallas kernels, local(): pl.pallas_call(functools.partial(kv_kernel, (1, 0, 2)), out_shape=[jax.Sh...  2.78 us
    pallas_call x2, Pallas kernels, project(): pl.pallas_call(functools.partial(project_kernel, order), out_shape=[jax.S...  2.45 us
  transfers between devices with their start and end apart: 23, of which 6 were waited for; matrix products, arithmetic and copies ran while one was open for 0% of the time, Pallas kernels for 27%

profile of v2, /device:TPU:0, one launch (start us, length us, event | category | flops | bytes accessed | tf_op | source)
XLA Modules:
  0.0 75.6 jit_solution(17474953550300465492)
XLA Ops:
  0.6 3.1 %collective-permute-start = (bf16[256,896]{1,0:T(8,128)(2,1)}, bf16[256,896]{1,0:T(8,128)(2,1)S(1)}, u32[]{:S(2)}, u32[]{:S(2)}) collective-permute-start(bf16[256,896]{1,0:T(8,128)(2,1)} %own_hbm.1), channel_id=1, source_target_pairs={{0,2},{1,3},{2,0},{3,1},{4,6},{5,7},{6,4},{7,5},{8,10},{9,11},{10,... | collective-permute-start | bytes 1376264 | tf_op jit(solution)/shard_map/ppermute | solution.py:238
  3.7 10.7 %collective-permute-done.refs_1_ = bf16[256,896]{1,0:T(8,128)(2,1)S(1)} collective-permute-done((bf16[256,896]{1,0:T(8,128)(2,1)}, bf16[256,896]{1,0:T(8,128)(2,1)S(1)}, u32[]{:S(2)}, u32[]{:S(2)}) %collective-permute-start) | collective-permute-done | bytes 458784 | tf_op jit(solution)/shard_map/ppermute | solution.py:238
  15.4 1.8 %collective-permute-start.3 = (bf16[128,256]{1,0:T(8,128)(2,1)S(1)}, bf16[128,256]{1,0:T(8,128)(2,1)S(1)}, u32[]{:S(2)}, u32[]{:S(2)}) collective-permute-start(bf16[128,256]{1,0:T(8,128)(2,1)S(1)} %get-tuple-element.34), channel_id=1, source_target_pairs={{0,4},{4,0},{8,12},{12,8},{16,20},{20,16},{24,28},{28,24},{1,5},{5... | collective-permute-start | bytes 196616 | tf_op jit(solution)/shard_map/ppermute | solution.py:238
  17.2 1.6 %collective-permute-start.4 = (bf16[128,256]{1,0:T(8,128)(2,1)S(1)}, bf16[128,256]{1,0:T(8,128)(2,1)S(1)}, u32[]{:S(2)}, u32[]{:S(2)}) collective-permute-start(bf16[128,256]{1,0:T(8,128)(2,1)S(1)} %get-tuple-element.35), channel_id=1, source_target_pairs={{0,8},{4,12},{8,0},{12,4},{16,24},{20,28},{24,16},{28,20},{1,9},{5... | collective-permute-start | bytes 196616 | tf_op jit(solution)/shard_map/ppermute | solution.py:238
  20.0 2.8 %collective-permute-start.6 = (bf16[128,256]{1,0:T(8,128)(2,1)S(1)}, bf16[128,256]{1,0:T(8,128)(2,1)S(1)}, u32[]{:S(2)}, u32[]{:S(2)}) collective-permute-start(bf16[128,256]{1,0:T(8,128)(2,1)S(1)} %get-tuple-element.37), channel_id=1, source_target_pairs={{0,16},{4,20},{8,24},{12,28},{16,0},{20,4},{24,8},{28,12},{1,17},{... | collective-permute-start | bytes 196616 | tf_op jit(solution)/shard_map/ppermute | solution.py:238
  22.8 1.3 %collective-permute-start.7 = (bf16[128,256]{1,0:T(8,128)(2,1)S(1)}, bf16[128,256]{1,0:T(8,128)(2,1)S(1)}, u32[]{:S(2)}, u32[]{:S(2)}) collective-permute-start(bf16[128,256]{1,0:T(8,128)(2,1)S(1)} %get-tuple-element.38), channel_id=1, source_target_pairs={{0,20},{4,16},{8,28},{12,24},{16,4},{20,0},{24,12},{28,8},{1,21},{... | collective-permute-start | bytes 196616 | tf_op jit(solution)/shard_map/ppermute | solution.py:238
  24.1 3.6 %collective-permute-start.8 = (bf16[128,256]{1,0:T(8,128)(2,1)S(1)}, bf16[128,256]{1,0:T(8,128)(2,1)S(1)}, u32[]{:S(2)}, u32[]{:S(2)}) collective-permute-start(bf16[128,256]{1,0:T(8,128)(2,1)S(1)} %get-tuple-element.39), channel_id=1, source_target_pairs={{0,24},{4,28},{8,16},{12,20},{16,8},{20,12},{24,0},{28,4},{1,25},{... | collective-permute-start | bytes 196616 | tf_op jit(solution)/shard_map/ppermute | solution.py:238
  27.7 1.3 %collective-permute-start.9 = (bf16[128,256]{1,0:T(8,128)(2,1)S(1)}, bf16[128,256]{1,0:T(8,128)(2,1)S(1)}, u32[]{:S(2)}, u32[]{:S(2)}) collective-permute-start(bf16[128,256]{1,0:T(8,128)(2,1)S(1)} %get-tuple-element.40), channel_id=1, source_target_pairs={{0,28},{4,24},{8,20},{12,16},{16,12},{20,8},{24,4},{28,0},{1,29},{... | collective-permute-start | bytes 196616 | tf_op jit(solution)/shard_map/ppermute | solution.py:238
  29.0 2.8 %kv.1 = (f32[256,128]{1,0:T(8,128)S(1)}, f32[256,128]{1,0:T(8,128)S(1)}) custom-call(s32[1]{0:T(128)} %bitcast.me_ref, bf16[256,896]{1,0:T(8,128)(2,1)} %own_hbm.1, bf16[256,896]{1,0:T(8,128)(2,1)S(1)} %collective-permute-done.2.refs_0_, bf16[256,896]{1,0:T(8,128)(2,1)S(1)} %collective-permute-done.refs_1_, bf16[3584,128]{1,0:T(8,128)(2,1)} %wk_hbm.1, ...), custom_call_target="tpu_custom_call" | custom-call | flops 400000000 | bytes 3000000 | tf_op jit(solution)/shard_map/kv/pallas_call | solution.py:291
  31.8 1.6 %collective-permute-start.14 = (bf16[256,896]{1,0:T(8,128)(2,1)}, bf16[256,896]{1,0:T(8,128)(2,1)S(1)}, u32[]{:S(2)}, u32[]{:S(2)}) collective-permute-start(bf16[256,896]{1,0:T(8,128)(2,1)} %refs_0_.1), channel_id=1, source_target_pairs={{0,2},{1,3},{2,0},{3,1},{4,6},{5,7},{6,4},{7,5},{8,10},{9,11},{10,... | collective-permute-start | bytes 1376264 | tf_op jit(solution)/shard_map/ppermute | solution.py:238
  33.4 1.4 %collective-permute-done.9.refs_7_.refs_11_ = bf16[128,256]{1,0:T(8,128)(2,1)S(1)} collective-permute-done((bf16[128,256]{1,0:T(8,128)(2,1)S(1)}, bf16[128,256]{1,0:T(8,128)(2,1)S(1)}, u32[]{:S(2)}, u32[]{:S(2)}) %collective-permute-start.9) | collective-permute-done | bytes 65568 | tf_op jit(solution)/shard_map/ppermute | solution.py:238
  35.8 5.4 %forward.1 = (bf16[256,896]{1,0:T(8,128)(2,1)S(1)}, bf16[1280,1792]{1,0:T(8,128)(2,1)S(1)}, f32[8,256]{1,0:T(8,128)S(1)}, f32[256,128]{1,0:T(8,128)S(1)}, bf16[256,128]{1,0:T(8,128)(2,1)S(1)}) custom-call(s32[1]{0:T(128)} %bitcast.me_ref, bf16[3584,128]{1,0:T(8,128)(2,1)} %wk_hbm.1, bf16[3584,128]{1,0:T(8,128)(2,1)} %wv_hbm.1, ...), custom_call_target="tpu_custom_call" | custom-call | flops 5000000000 | bytes 10000000 | tf_op jit(solution)/shard_map/forward/pallas_call | solution.py:307
  42.8 1.8 %shard_map.112 = (bf16[256,896]{1,0:T(8,128)(2,1)S(1)}, bf16[256,896]{1,0:T(8,128)(2,1)S(1)}, bf16[256,896]{1,0:T(8,128)(2,1)S(1)}) custom-call(s32[1]{0:T(128)} %bitcast.me_ref, bf16[256,896]{1,0:T(8,128)(2,1)S(1)} %get-tuple-element.41.ctx_ref, bf16[896,3584]{1,0:T(8,128)(2,1)S(1)} %bitcast.3), custom_call_target="tpu_custom_call" | custom-call | flops 1500000000 | bytes 6000000 | tf_op jit(solution)/shard_map/pallas_call | solution.py:333
  45.0 1.6 %collective-permute-start.12 = (bf16[256,896]{1,0:T(8,128)(2,1)S(1)}, bf16[256,896]{1,0:T(8,128)(2,1)S(1)}, u32[]{:S(2)}, u32[]{:S(2)}) collective-permute-start(bf16[256,896]{1,0:T(8,128)(2,1)S(1)} %add_convert_fusion.1), channel_id=1, source_target_pairs={{0,2},{1,3},{2,0},{3,1},{4,6},{5,7},{6,4},{7,5},{8,10},{9,11},{10,... | collective-permute-start | bytes 1376264 | tf_op jit(solution)/shard_map/ppermute | solution.py:238
  46.6 7.1 %backward.1 = (bf16[128,256]{1,0:T(8,128)(2,1)S(1)}, bf16[128,256]{1,0:T(8,128)(2,1)S(1)}, bf16[128,256]{1,0:T(8,128)(2,1)S(1)}, bf16[128,256]{1,0:T(8,128)(2,1)...) custom-call(s32[1]{0:T(128)} %bitcast.me_ref, ...), custom_call_target="tpu_custom_call" | custom-call | flops 7000000000 | bytes 10000000 | tf_op jit(solution)/shard_map/backward/pallas_call | solution.py:351
  53.8 1.1 %collective-permute-start.16 = (bf16[128,256]{1,0:T(8,128)(2,1)S(1)}, bf16[128,256]{1,0:T(8,128)(2,1)S(1)}, u32[]{:S(2)}, u32[]{:S(2)}) collective-permute-start(bf16[128,256]{1,0:T(8,128)(2,1)S(1)} %get-tuple-element.50), channel_id=1, source_target_pairs={{0,4},{4,0},{8,12},{12,8},{16,20},{20,16},{24,28},{28,24},{1,5},{5... | collective-permute-start | bytes 196616 | tf_op jit(solution)/shard_map/ppermute | solution.py:238
  54.8 1.3 %collective-permute-start.17 = (bf16[128,256]{1,0:T(8,128)(2,1)S(1)}, bf16[128,256]{1,0:T(8,128)(2,1)S(1)}, u32[]{:S(2)}, u32[]{:S(2)}) collective-permute-start(bf16[128,256]{1,0:T(8,128)(2,1)S(1)} %get-tuple-element.51), channel_id=1, source_target_pairs={{0,8},{4,12},{8,0},{12,4},{16,24},{20,28},{24,16},{28,20},{1,9},{5... | collective-permute-start | bytes 196616 | tf_op jit(solution)/shard_map/ppermute | solution.py:238
  56.2 1.1 %collective-permute-start.18 = (bf16[128,256]{1,0:T(8,128)(2,1)S(1)}, bf16[128,256]{1,0:T(8,128)(2,1)S(1)}, u32[]{:S(2)}, u32[]{:S(2)}) collective-permute-start(bf16[128,256]{1,0:T(8,128)(2,1)S(1)} %get-tuple-element.52), channel_id=1, source_target_pairs={{0,12},{4,8},{8,4},{12,0},{16,28},{20,24},{24,20},{28,16},{1,13},{... | collective-permute-start | bytes 196616 | tf_op jit(solution)/shard_map/ppermute | solution.py:238
  58.1 3.4 %collective-permute-start.19 = (bf16[128,256]{1,0:T(8,128)(2,1)S(1)}, bf16[128,256]{1,0:T(8,128)(2,1)S(1)}, u32[]{:S(2)}, u32[]{:S(2)}) collective-permute-start(bf16[128,256]{1,0:T(8,128)(2,1)S(1)} %get-tuple-element.53), channel_id=1, source_target_pairs={{0,16},{4,20},{8,24},{12,28},{16,0},{20,4},{24,8},{28,12},{1,17},{... | collective-permute-start | bytes 196616 | tf_op jit(solution)/shard_map/ppermute | solution.py:238
  61.5 2.2 %collective-permute-start.20 = (bf16[128,256]{1,0:T(8,128)(2,1)S(1)}, bf16[128,256]{1,0:T(8,128)(2,1)S(1)}, u32[]{:S(2)}, u32[]{:S(2)}) collective-permute-start(bf16[128,256]{1,0:T(8,128)(2,1)S(1)} %get-tuple-element.54), channel_id=1, source_target_pairs={{0,20},{4,16},{8,28},{12,24},{16,4},{20,0},{24,12},{28,8},{1,21},{... | collective-permute-start | bytes 196616 | tf_op jit(solution)/shard_map/ppermute | solution.py:238
  63.6 1.6 %collective-permute-start.21 = (bf16[128,256]{1,0:T(8,128)(2,1)S(1)}, bf16[128,256]{1,0:T(8,128)(2,1)S(1)}, u32[]{:S(2)}, u32[]{:S(2)}) collective-permute-start(bf16[128,256]{1,0:T(8,128)(2,1)S(1)} %get-tuple-element.55), channel_id=1, source_target_pairs={{0,24},{4,28},{8,16},{12,20},{16,8},{20,12},{24,0},{28,4},{1,25},{... | collective-permute-start | bytes 196616 | tf_op jit(solution)/shard_map/ppermute | solution.py:238
  65.4 5.6 %collective-permute-start.22 = (bf16[128,256]{1,0:T(8,128)(2,1)S(1)}, bf16[128,256]{1,0:T(8,128)(2,1)S(1)}, u32[]{:S(2)}, u32[]{:S(2)}) collective-permute-start(bf16[128,256]{1,0:T(8,128)(2,1)S(1)} %get-tuple-element.56), channel_id=1, source_target_pairs={{0,28},{4,24},{8,20},{12,16},{16,12},{20,8},{24,4},{28,0},{1,29},{... | collective-permute-start | bytes 196616 | tf_op jit(solution)/shard_map/ppermute | solution.py:238
  71.0 2.2 %collective-permute-done.22.refs_7_ = bf16[128,256]{1,0:T(8,128)(2,1)S(1)} collective-permute-done((bf16[128,256]{1,0:T(8,128)(2,1)S(1)}, bf16[128,256]{1,0:T(8,128)(2,1)S(1)}, u32[]{:S(2)}, u32[]{:S(2)}) %collective-permute-start.22) | collective-permute-done | bytes 65568 | tf_op jit(solution)/shard_map/ppermute | solution.py:238
  73.2 1.4 %place.1 = (f32[256,128]{1,0:T(8,128)}, f32[256,128]{1,0:T(8,128)}) custom-call(s32[1]{0:T(128)} %bitcast.1.me_ref, s32[8,16]{1,0:T(8,128)S(1)} %copy-done, bf16[128,256]{1,0:T(8,128)(2,1)S(1)} %get-tuple-element.49.refs_0_, bf16[128,256]{1,0:T(8,128)(2,1)S(1)} %collective-permute-done.16.refs_1_, bf16[128,256]{1,0:T(8,128)(2,1)S(1)} %collective-permute-done.17.refs_2_, ...), custom_call_target="tpu_custom_call" | custom-call | bytes 1048576 | tf_op jit(solution)/shard_map/place/pallas_call | solution.py:371
  (44 shorter events, 7.2 us)
Async XLA Ops:
  0.6 13.8 %collective-permute-start = (bf16[256,896]{1,0:T(8,128)(2,1)}, bf16[256,896]{1,0:T(8,128)(2,1)S(1)}, u32[]{:S(2)}, u32[]{:S(2)}) collective-permute-start(bf16[256,896]{1,0:T(8,128)(2,1)} %own_hbm.1), channel_id=1, source_target_pairs={{0,2},{1,3},{2,0},{3,1},{4,6},{5,7},{6,4},{7,5},{8,10},{9,11},{10,... | collective-permute-start | bytes 1376264 | tf_op jit(solution)/shard_map/ppermute | solution.py:238
  3.7 24.0 %collective-permute-start.2 = (bf16[256,896]{1,0:T(8,128)(2,1)}, bf16[256,896]{1,0:T(8,128)(2,1)S(1)}, u32[]{:S(2)}, u32[]{:S(2)}) collective-permute-start(bf16[256,896]{1,0:T(8,128)(2,1)} %own_hbm.1), channel_id=1, source_target_pairs={{0,1},{1,0},{2,3},{3,2},{4,5},{5,4},{6,7},{7,6},{8,9},{9,8},{10,11... | collective-permute-start | bytes 1376264 | tf_op jit(solution)/shard_map/ppermute | solution.py:238
  14.4 20.3 %collective-permute-start.1 = (bf16[256,896]{1,0:T(8,128)(2,1)S(1)}, bf16[256,896]{1,0:T(8,128)(2,1)S(1)}, u32[]{:S(2)}, u32[]{:S(2)}) collective-permute-start(bf16[256,896]{1,0:T(8,128)(2,1)S(1)} %collective-permute-done.refs_1_), channel_id=1, source_target_pairs={{0,1},{1,0},{2,3},{3,2},{4,5},{5,4},{6,7},{7,6},{8,9},{9,8},{10,11... | collective-permute-start | bytes 1376264 | tf_op jit(solution)/shard_map/ppermute | solution.py:238
  15.4 4.6 %collective-permute-start.3 = (bf16[128,256]{1,0:T(8,128)(2,1)S(1)}, bf16[128,256]{1,0:T(8,128)(2,1)S(1)}, u32[]{:S(2)}, u32[]{:S(2)}) collective-permute-start(bf16[128,256]{1,0:T(8,128)(2,1)S(1)} %get-tuple-element.34), channel_id=1, source_target_pairs={{0,4},{4,0},{8,12},{12,8},{16,20},{20,16},{24,28},{28,24},{1,5},{5... | collective-permute-start | bytes 196616 | tf_op jit(solution)/shard_map/ppermute | solution.py:238
  17.2 5.6 %collective-permute-start.4 = (bf16[128,256]{1,0:T(8,128)(2,1)S(1)}, bf16[128,256]{1,0:T(8,128)(2,1)S(1)}, u32[]{:S(2)}, u32[]{:S(2)}) collective-permute-start(bf16[128,256]{1,0:T(8,128)(2,1)S(1)} %get-tuple-element.35), channel_id=1, source_target_pairs={{0,8},{4,12},{8,0},{12,4},{16,24},{20,28},{24,16},{28,20},{1,9},{5... | collective-permute-start | bytes 196616 | tf_op jit(solution)/shard_map/ppermute | solution.py:238
  18.8 5.3 %collective-permute-start.5 = (bf16[128,256]{1,0:T(8,128)(2,1)S(1)}, bf16[128,256]{1,0:T(8,128)(2,1)S(1)}, u32[]{:S(2)}, u32[]{:S(2)}) collective-permute-start(bf16[128,256]{1,0:T(8,128)(2,1)S(1)} %get-tuple-element.36), channel_id=1, source_target_pairs={{0,12},{4,8},{8,4},{12,0},{16,28},{20,24},{24,20},{28,16},{1,13},{... | collective-permute-start | bytes 196616 | tf_op jit(solution)/shard_map/ppermute | solution.py:238
  20.0 11.8 %collective-permute-start.6 = (bf16[128,256]{1,0:T(8,128)(2,1)S(1)}, bf16[128,256]{1,0:T(8,128)(2,1)S(1)}, u32[]{:S(2)}, u32[]{:S(2)}) collective-permute-start(bf16[128,256]{1,0:T(8,128)(2,1)S(1)} %get-tuple-element.37), channel_id=1, source_target_pairs={{0,16},{4,20},{8,24},{12,28},{16,0},{20,4},{24,8},{28,12},{1,17},{... | collective-permute-start | bytes 196616 | tf_op jit(solution)/shard_map/ppermute | solution.py:238
  22.8 10.5 %collective-permute-start.7 = (bf16[128,256]{1,0:T(8,128)(2,1)S(1)}, bf16[128,256]{1,0:T(8,128)(2,1)S(1)}, u32[]{:S(2)}, u32[]{:S(2)}) collective-permute-start(bf16[128,256]{1,0:T(8,128)(2,1)S(1)} %get-tuple-element.38), channel_id=1, source_target_pairs={{0,20},{4,16},{8,28},{12,24},{16,4},{20,0},{24,12},{28,8},{1,21},{... | collective-permute-start | bytes 196616 | tf_op jit(solution)/shard_map/ppermute | solution.py:238
  24.1 9.3 %collective-permute-start.8 = (bf16[128,256]{1,0:T(8,128)(2,1)S(1)}, bf16[128,256]{1,0:T(8,128)(2,1)S(1)}, u32[]{:S(2)}, u32[]{:S(2)}) collective-permute-start(bf16[128,256]{1,0:T(8,128)(2,1)S(1)} %get-tuple-element.39), channel_id=1, source_target_pairs={{0,24},{4,28},{8,16},{12,20},{16,8},{20,12},{24,0},{28,4},{1,25},{... | collective-permute-start | bytes 196616 | tf_op jit(solution)/shard_map/ppermute | solution.py:238
  27.7 7.1 %collective-permute-start.9 = (bf16[128,256]{1,0:T(8,128)(2,1)S(1)}, bf16[128,256]{1,0:T(8,128)(2,1)S(1)}, u32[]{:S(2)}, u32[]{:S(2)}) collective-permute-start(bf16[128,256]{1,0:T(8,128)(2,1)S(1)} %get-tuple-element.40), channel_id=1, source_target_pairs={{0,28},{4,24},{8,20},{12,16},{16,12},{20,8},{24,4},{28,0},{1,29},{... | collective-permute-start | bytes 196616 | tf_op jit(solution)/shard_map/ppermute | solution.py:238
  31.8 10.8 %collective-permute-start.14 = (bf16[256,896]{1,0:T(8,128)(2,1)}, bf16[256,896]{1,0:T(8,128)(2,1)S(1)}, u32[]{:S(2)}, u32[]{:S(2)}) collective-permute-start(bf16[256,896]{1,0:T(8,128)(2,1)} %refs_0_.1), channel_id=1, source_target_pairs={{0,2},{1,3},{2,0},{3,1},{4,6},{5,7},{6,4},{7,5},{8,10},{9,11},{10,... | collective-permute-start | bytes 1376264 | tf_op jit(solution)/shard_map/ppermute | solution.py:238
  42.0 2.9 %collective-permute-start.11 = (bf16[256,896]{1,0:T(8,128)(2,1)S(1)}, bf16[256,896]{1,0:T(8,128)(2,1)S(1)}, u32[]{:S(2)}, u32[]{:S(2)}) collective-permute-start(bf16[256,896]{1,0:T(8,128)(2,1)S(1)} %shard_map.113), channel_id=1, source_target_pairs={{0,1},{1,0},{2,3},{3,2},{4,5},{5,4},{6,7},{7,6},{8,9},{9,8},{10,11... | collective-permute-start | bytes 1376264 | tf_op jit(solution)/shard_map/ppermute | solution.py:238
  42.2 4.4 %collective-permute-start.13 = (bf16[256,896]{1,0:T(8,128)(2,1)S(1)}, bf16[256,896]{1,0:T(8,128)(2,1)S(1)}, u32[]{:S(2)}, u32[]{:S(2)}) collective-permute-start(bf16[256,896]{1,0:T(8,128)(2,1)S(1)} %copy-done.3), channel_id=1, source_target_pairs={{0,1},{1,0},{2,3},{3,2},{4,5},{5,4},{6,7},{7,6},{8,9},{9,8},{10,11... | collective-permute-start | bytes 1376264 | tf_op jit(solution)/shard_map/ppermute | solution.py:238
  42.6 4.1 %collective-permute-start.15 = (bf16[256,896]{1,0:T(8,128)(2,1)S(1)}, bf16[256,896]{1,0:T(8,128)(2,1)S(1)}, u32[]{:S(2)}, u32[]{:S(2)}) collective-permute-start(bf16[256,896]{1,0:T(8,128)(2,1)S(1)} %collective-permute-done.14.refs_2_), channel_id=1, source_target_pairs={{0,1},{1,0},{2,3},{3,2},{4,5},{5,4},{6,7},{7,6},{8,9},{9,8},{10,11... | collective-permute-start | bytes 1376264 | tf_op jit(solution)/shard_map/ppermute | solution.py:238
  44.5 30.1 %collective-permute-start.10 = (bf16[256,896]{1,0:T(8,128)(2,1)S(1)}, bf16[256,896]{1,0:T(8,128)(2,1)S(1)}, u32[]{:S(2)}, u32[]{:S(2)}) collective-permute-start(bf16[256,896]{1,0:T(8,128)(2,1)S(1)} %get-tuple-element.43), channel_id=1, source_target_pairs={{0,1},{1,0},{2,3},{3,2},{4,5},{5,4},{6,7},{7,6},{8,9},{9,8},{10,11... | collective-permute-start | bytes 1376264 | tf_op jit(solution)/shard_map/ppermute | solution.py:238
  45.0 29.6 %collective-permute-start.12 = (bf16[256,896]{1,0:T(8,128)(2,1)S(1)}, bf16[256,896]{1,0:T(8,128)(2,1)S(1)}, u32[]{:S(2)}, u32[]{:S(2)}) collective-permute-start(bf16[256,896]{1,0:T(8,128)(2,1)S(1)} %add_convert_fusion.1), channel_id=1, source_target_pairs={{0,2},{1,3},{2,0},{3,1},{4,6},{5,7},{6,4},{7,5},{8,10},{9,11},{10,... | collective-permute-start | bytes 1376264 | tf_op jit(solution)/shard_map/ppermute | solution.py:238
  46.6 26.6 %copy-start = (s32[8,16]{1,0:T(8,128)S(1)}, s32[8,16]{1,0:T(8,128)}, u32[]{:S(2)}) copy-start(s32[8,16]{1,0:T(8,128)} %reads_ref.1) | copy-start | bytes 1540
  53.8 4.3 %collective-permute-start.16 = (bf16[128,256]{1,0:T(8,128)(2,1)S(1)}, bf16[128,256]{1,0:T(8,128)(2,1)S(1)}, u32[]{:S(2)}, u32[]{:S(2)}) collective-permute-start(bf16[128,256]{1,0:T(8,128)(2,1)S(1)} %get-tuple-element.50), channel_id=1, source_target_pairs={{0,4},{4,0},{8,12},{12,8},{16,20},{20,16},{24,28},{28,24},{1,5},{5... | collective-permute-start | bytes 196616 | tf_op jit(solution)/shard_map/ppermute | solution.py:238
  54.8 6.6 %collective-permute-start.17 = (bf16[128,256]{1,0:T(8,128)(2,1)S(1)}, bf16[128,256]{1,0:T(8,128)(2,1)S(1)}, u32[]{:S(2)}, u32[]{:S(2)}) collective-permute-start(bf16[128,256]{1,0:T(8,128)(2,1)S(1)} %get-tuple-element.51), channel_id=1, source_target_pairs={{0,8},{4,12},{8,0},{12,4},{16,24},{20,28},{24,16},{28,20},{1,9},{5... | collective-permute-start | bytes 196616 | tf_op jit(solution)/shard_map/ppermute | solution.py:238
  56.2 7.5 %collective-permute-start.18 = (bf16[128,256]{1,0:T(8,128)(2,1)S(1)}, bf16[128,256]{1,0:T(8,128)(2,1)S(1)}, u32[]{:S(2)}, u32[]{:S(2)}) collective-permute-start(bf16[128,256]{1,0:T(8,128)(2,1)S(1)} %get-tuple-element.52), channel_id=1, source_target_pairs={{0,12},{4,8},{8,4},{12,0},{16,28},{20,24},{24,20},{28,16},{1,13},{... | collective-permute-start | bytes 196616 | tf_op jit(solution)/shard_map/ppermute | solution.py:238
  58.1 7.3 %collective-permute-start.19 = (bf16[128,256]{1,0:T(8,128)(2,1)S(1)}, bf16[128,256]{1,0:T(8,128)(2,1)S(1)}, u32[]{:S(2)}, u32[]{:S(2)}) collective-permute-start(bf16[128,256]{1,0:T(8,128)(2,1)S(1)} %get-tuple-element.53), channel_id=1, source_target_pairs={{0,16},{4,20},{8,24},{12,28},{16,0},{20,4},{24,8},{28,12},{1,17},{... | collective-permute-start | bytes 196616 | tf_op jit(solution)/shard_map/ppermute | solution.py:238
  61.5 9.5 %collective-permute-start.20 = (bf16[128,256]{1,0:T(8,128)(2,1)S(1)}, bf16[128,256]{1,0:T(8,128)(2,1)S(1)}, u32[]{:S(2)}, u32[]{:S(2)}) collective-permute-start(bf16[128,256]{1,0:T(8,128)(2,1)S(1)} %get-tuple-element.54), channel_id=1, source_target_pairs={{0,20},{4,16},{8,28},{12,24},{16,4},{20,0},{24,12},{28,8},{1,21},{... | collective-permute-start | bytes 196616 | tf_op jit(solution)/shard_map/ppermute | solution.py:238
  63.6 7.4 %collective-permute-start.21 = (bf16[128,256]{1,0:T(8,128)(2,1)S(1)}, bf16[128,256]{1,0:T(8,128)(2,1)S(1)}, u32[]{:S(2)}, u32[]{:S(2)}) collective-permute-start(bf16[128,256]{1,0:T(8,128)(2,1)S(1)} %get-tuple-element.55), channel_id=1, source_target_pairs={{0,24},{4,28},{8,16},{12,20},{16,8},{20,12},{24,0},{28,4},{1,25},{... | collective-permute-start | bytes 196616 | tf_op jit(solution)/shard_map/ppermute | solution.py:238
  65.4 7.8 %collective-permute-start.22 = (bf16[128,256]{1,0:T(8,128)(2,1)S(1)}, bf16[128,256]{1,0:T(8,128)(2,1)S(1)}, u32[]{:S(2)}, u32[]{:S(2)}) collective-permute-start(bf16[128,256]{1,0:T(8,128)(2,1)S(1)} %get-tuple-element.56), channel_id=1, source_target_pairs={{0,28},{4,24},{8,20},{12,16},{16,12},{20,8},{24,4},{28,0},{1,29},{... | collective-permute-start | bytes 196616 | tf_op jit(solution)/shard_map/ppermute | solution.py:238
  (5 other events, 25.1 us)

commit v3 on v2

--- a/solution.py
+++ b/solution.py
@@ -69,8 +69,9 @@
     return [pltpu.make_async_copy(w.at[rows], buf.at[slot], sems.at[j, slot]) for j, (w, buf) in enumerate(zip(hbms, bufs))]
 
 
-def kv_kernel(order, me_ref, own_hbm, *refs):
-    hidden, (wk_hbm, wv_hbm, k_ref, v_ref, own_ref, wk_ref, wv_ref, sems, own_sem) = refs[:-9], refs[-9:]
+def kv_kernel(order, last, me_ref, own_hbm, *refs):
+    hidden, (wk_hbm, wv_hbm, q_hbm, k_ref, v_ref, q_ref, lastk_ref, lastv_ref) = refs[:-13], refs[-13:-5]
+    own_ref, wk_ref, wv_ref, sems, far_sems = refs[-5:]
     me = me_ref[0]
     width = own_ref.shape[1]
 
@@ -80,8 +81,16 @@
     for slot, i in enumerate(order):
         for copy in fetch(slot, i):
             copy.start()
-    own = pltpu.make_async_copy(own_hbm, own_ref, own_sem)
+    own = pltpu.make_async_copy(own_hbm, own_ref, far_sems.at[0])
     own.start()
+    rows = pl.ds(pl.multiple_of((me ^ last) * width, width), width)
+    later = [
+        pltpu.make_async_copy(q_hbm, q_ref, far_sems.at[1]),
+        pltpu.make_async_copy(wk_hbm.at[rows], lastk_ref, far_sems.at[2]),
+        pltpu.make_async_copy(wv_hbm.at[rows], lastv_ref, far_sems.at[3]),
+    ]
+    for copy in later:
+        copy.start()
     new_k = jnp.zeros(k_ref.shape, F32)
     new_v = jnp.zeros(k_ref.shape, F32)
     for slot, i in enumerate(order):
@@ -94,43 +103,35 @@
         new_v += dot(piece, wv_ref[slot], ((1,), (0,)))
     k_ref[...] = new_k
     v_ref[...] = new_v
-
-
-def forward_kernel(n_pre, scaling, last, me_ref, wk_hbm, wv_hbm, hidden_ref, q_ref, partk_ref, partv_ref, *refs):
+    for copy in later:
+        copy.wait()
+
+
+def forward_kernel(n_pre, scaling, wk_ref, wv_ref, hidden_ref, q_ref, partk_ref, partv_ref, *refs):
     prefix = refs[:n_pre]
-    ctx_ref, exps_ref, row_ref, col_ref, newv_ref, newk_ref, wk_ref, wv_ref, vt_all, s_buf, sums, sems = refs[n_pre:]
-    length, width = hidden_ref.shape
-    copies = weight_copies(last, me_ref[0], width, (wk_hbm, wv_hbm), (wk_ref, wv_ref), 0, sems)
-    for copy in copies:
-        copy.start()
+    ctx_ref, exps_ref, row_ref, v_all, k_all, vt_all, s_buf, sums = refs[n_pre:]
+    length = hidden_ref.shape[0]
     heads = q_ref.shape[1] // HD
     factor = scaling * LOG2E
-    chunks = []
     at = 0
     for ref in prefix:
         size = ref.shape[0]
-        vt_all[:, at:at + size] = ref[:, HD:].astype(F32).T.astype(BF16)
-        chunks.append((at, size, ref))
+        k_all[at:at + size, :] = ref[:, :HD]
+        v_all[at:at + size, :] = ref[:, HD:]
         at += size
-    for copy in copies:
-        copy.wait()
     piece = hidden_ref[...]
-    newk_ref[...] = (partk_ref[...] + dot(piece, wk_ref[0], ((1,), (0,)))).astype(BF16)
-    newv_ref[...] = (partv_ref[...] + dot(piece, wv_ref[0], ((1,), (0,)))).astype(BF16)
-    vt_all[:, at:] = newv_ref[...].astype(F32).T.astype(BF16)
+    k_all[at:, :] = (partk_ref[...] + dot(piece, wk_ref[...], ((1,), (0,)))).astype(BF16)
+    v_all[at:, :] = (partv_ref[...] + dot(piece, wv_ref[...], ((1,), (0,)))).astype(BF16)
+    vt_all[...] = v_all[...].astype(F32).T.astype(BF16)
     visible = lax.broadcasted_iota(jnp.int32, (length, length), 0) <= lax.broadcasted_iota(
         jnp.int32, (length, length), 1)
-    sums[...] = jnp.ones_like(sums)
 
     def scores(h):
         qh = q_ref[:, h * HD:(h + 1) * HD]
-        peak = None
-        for start, size, ref in chunks:
-            s = dot(ref[:, :HD], qh, ((1,), (1,)))
-            s_buf[h % 2, start:start + size, :] = s
-            top = jnp.max(s, axis=0, keepdims=True)
-            peak = top if peak is None else jnp.maximum(peak, top)
-        s = jnp.where(visible, dot(newk_ref[...], qh, ((1,), (1,))), -jnp.inf)
+        s = dot(k_all[:at, :], qh, ((1,), (1,)))
+        s_buf[h % 2, :at, :] = s
+        peak = jnp.max(s, axis=0, keepdims=True)
+        s = jnp.where(visible, dot(k_all[at:, :], qh, ((1,), (1,))), -jnp.inf)
         s_buf[h % 2, at:, :] = s
         return jnp.maximum(peak, jnp.max(s, axis=0, keepdims=True))
 
@@ -152,8 +153,7 @@
         later = scores(h + 1) if h + 1 < heads else None
         finish(h, peak)
         peak = later
-    row_ref[...] = sums[:row_ref.shape[0], :]
-    col_ref[...] = sums[...].T
+    row_ref[:heads, :] = sums[:heads, :]
 
 
 def project_kernel(order, me_ref, ctx_ref, w_ref, *outs):
@@ -165,37 +165,36 @@
         out[...] = dot(ctx, w_ref[:, cols], ((1,), (0,))).astype(BF16)
 
 
-def backward_kernel(order, n_pre, scaling, me_ref, w_ref, q_ref, newv_ref, exps_ref, row_ref, col_ref, *refs):
-    grads, prefix = refs[:len(order)], refs[len(order):len(order) + n_pre]
-    outs = refs[len(order) + n_pre:len(order) + 2 * n_pre]
-    g_all, q_all, dbuf, slopes = refs[len(order) + 2 * n_pre:]
-    me = me_ref[0]
-    length, width = grads[0].shape
-    heads = q_ref.shape[1] // HD
-    total = jnp.zeros((length, heads * HD), F32)
+def grad_kernel(order, me_ref, w_ref, *refs):
+    grads, out = refs[:-1], refs[-1]
+    me = me_ref[0]
+    width = grads[0].shape[1]
+    total = jnp.zeros(out.shape, F32)
     for i, grad in zip(order, grads):
         cols = pl.ds(pl.multiple_of((me ^ i) * width, 128), width)
-        total += dot(grad[...], w_ref[:, cols], ((1,), (1,)))
+        total += dot(w_ref[:, cols], grad[...], ((1,), (1,)))
+    out[...] = total
+
+
+def backward_kernel(last, n_pre, scaling, me_ref, w_ref, part_ref, grad_ref, q_ref, v_all, exps_ref, row_ref, *refs):
+    outs = refs[:n_pre]
+    gt_all, q_all, dbuf, slopes = refs[n_pre:]
+    me = me_ref[0]
+    length, width = grad_ref.shape
+    heads = q_ref.shape[1] // HD
+    cols = pl.ds(pl.multiple_of((me ^ last) * width, 128), width)
+    total = part_ref[...] + dot(w_ref[:, cols], grad_ref[...], ((1,), (1,)))
     for h in range(heads):
-        rows = slice(h * length, (h + 1) * length)
-        q_all[rows, :] = q_ref[:, h * HD:(h + 1) * HD]
-        g_all[rows, :] = (total[:, h * HD:(h + 1) * HD] * col_ref[:, h:h + 1]).astype(BF16)
+        lanes = slice(h * length, (h + 1) * length)
+        q_all[lanes, :] = q_ref[:, h * HD:(h + 1) * HD]
+        gt_all[:, lanes] = (total[h * HD:(h + 1) * HD, :] * row_ref[h:h + 1, :]).astype(BF16)
     n_rows = dbuf.shape[0]
 
     def slope(h):
-        gh = g_all[h * length:(h + 1) * length, :]
         lanes = slice(h * length, (h + 1) * length)
-        at = 0
-        delta = None
-        for ref in prefix:
-            size = ref.shape[0]
-            s = dot(ref[:, HD:], gh, ((1,), (1,)))
-            slopes[h % 2, at:at + size, :] = s
-            part = jnp.sum(exps_ref[at:at + size, lanes].astype(F32) * s, axis=0, keepdims=True)
-            delta = part if delta is None else delta + part
-            at += size
-        s = dot(newv_ref[...], gh, ((1,), (1,)))
-        delta += jnp.sum(exps_ref[at:, lanes].astype(F32) * s, axis=0, keepdims=True)
+        s = dot(v_all[...], gt_all[:, lanes], ((1,), (0,)))
+        slopes[h % 2] = s[:n_rows]
+        delta = jnp.sum(exps_ref[:, lanes].astype(F32) * s, axis=0, keepdims=True)
         return delta * row_ref[h:h + 1, :]
 
     def finish(h, delta):
@@ -210,11 +209,13 @@
         later = slope(h + 1) if h + 1 < heads else None
         finish(h, delta)
         delta = later
+    value_grad = dot(exps_ref[:n_rows, :], gt_all[...], ((1,), (1,)))
+    key_grad = dot(dbuf[...], q_all[...], ((1,), (0,))) * scaling
     at = 0
     for out in outs:
         size = out.shape[0]
-        out[:, HD:] = dot(exps_ref[at:at + size, :], g_all[...], ((1,), (0,))).astype(out.dtype)
-        out[:, :HD] = (dot(dbuf[at:at + size, :], q_all[...], ((1,), (0,))) * scaling).astype(out.dtype)
+        out[:, HD:] = value_grad[at:at + size].astype(out.dtype)
+        out[:, :HD] = key_grad[at:at + size].astype(out.dtype)
         at += size
 
 
@@ -287,47 +288,55 @@
         prefix = [fetched.reshape(n_rows, 2 * HD)]
     n_pre = len(prefix)
 
-    weight_bufs = [pltpu.VMEM((n_tp - 1, width, HD), BF16)] * 2
-    part_k, part_v = pl.pallas_call(
-        functools.partial(kv_kernel, (1, 0, 2)),
-        out_shape=[jax.ShapeDtypeStruct((length, HD), F32)] * 2,
-        in_specs=[SMEM, HBM] + [VMEM] * (n_tp - 2) + [HBM] * 2,
-        out_specs=[VMEM] * 2,
+    part = jax.ShapeDtypeStruct((length, HD), F32)
+    weight = jax.ShapeDtypeStruct((width, HD), BF16)
+    part_k, part_v, q, last_k, last_v = pl.pallas_call(
+        functools.partial(kv_kernel, (1, 0, 2), n_tp - 1),
+        out_shape=[part, part, jax.ShapeDtypeStruct(queries.shape, BF16), weight, weight],
+        in_specs=[SMEM, HBM] + [VMEM] * (n_tp - 2) + [HBM] * 3,
+        out_specs=[VMEM] * 5,
         scratch_shapes=[
             pltpu.VMEM((length, width), BF16),
-            *weight_bufs,
+            pltpu.VMEM((n_tp - 1, width, HD), BF16),
+            pltpu.VMEM((n_tp - 1, width, HD), BF16),
             pltpu.SemaphoreType.DMA((2, n_tp - 1)),
-            pltpu.SemaphoreType.DMA,
+            pltpu.SemaphoreType.DMA((4,)),
         ],
         compiler_params=grant(8),
         cost_estimate=cost(4e8, 3e6),
         name="kv",
-    )(me_tp, hbm(hidden_states), near_hidden, far_hidden, hbm(key_weight), hbm(value_weight))
-
-    ctx, exps, row, col, new_v = pl.pallas_call(
-        functools.partial(forward_kernel, n_pre, scaling, n_tp - 1),
+    )(me_tp, hbm(hidden_states), near_hidden, far_hidden, hbm(key_weight), hbm(value_weight), hbm(queries))
+
+    ctx, exps, row, v_all = pl.pallas_call(
+        functools.partial(forward_kernel, n_pre, scaling),
         out_shape=[
             jax.ShapeDtypeStruct((length, heads * HD), BF16),
             jax.ShapeDtypeStruct((keys, heads * length), BF16),
             jax.ShapeDtypeStruct((heads + (-heads) % 8, length), F32),
-            jax.ShapeDtypeStruct((length, HD), F32),
-            jax.ShapeDtypeStruct((length, HD), BF16),
+            jax.ShapeDtypeStruct((keys, HD), BF16),
         ],
-        in_specs=[SMEM, HBM, HBM] + [VMEM] * (4 + n_pre),
-        out_specs=[VMEM] * 5,
+        in_specs=[VMEM] * (6 + n_pre),
+        out_specs=[VMEM] * 4,
         scratch_shapes=[
-            pltpu.VMEM((length, HD), BF16),
-            pltpu.VMEM((1, width, HD), BF16),
-            pltpu.VMEM((1, width, HD), BF16),
+            pltpu.VMEM((keys, HD), BF16),
             pltpu.VMEM((HD, keys), BF16),
             pltpu.VMEM((2, keys, length), F32),
-            pltpu.VMEM((HD, length), F32),
-            pltpu.SemaphoreType.DMA((2, 1)),
+            pltpu.VMEM((heads + (-heads) % 8, length), F32),
         ],
         compiler_params=grant(20),
         cost_estimate=cost(5e9, 1e7, 3e6),
         name="forward",
-    )(me_tp, hbm(key_weight), hbm(value_weight), last_hidden, queries, part_k, part_v, *prefix)
+    )(last_k, last_v, last_hidden, q, part_k, part_v, *prefix)
+
+    part_grad = pl.pallas_call(
+        functools.partial(grad_kernel, (0, 1, 2)),
+        out_shape=jax.ShapeDtypeStruct((heads * HD, length), F32),
+        in_specs=[SMEM] + [VMEM] * 4,
+        out_specs=VMEM,
+        compiler_params=grant(16),
+        cost_estimate=cost(1.5e9, 8e6),
+        name="grad",
+    )(me_tp, output_weight, out_grad, near_grad, far_grad)
 
     def project(order):
         return pl.pallas_call(
@@ -339,9 +348,9 @@
             cost_estimate=cost(5e8 * len(order), 2e6 * len(order)),
         )(me_tp, ctx, output_weight)
 
-    share3, = project((3,))
+    share3, share2 = project((3, 2))
     near3 = hop(share3, "tp", 1)
-    share2, share1, share0 = project((2, 1, 0))
+    share1, share0 = project((1, 0))
     near1 = hop(share1, "tp", 1)
     cross = (share2.astype(F32) + near3.astype(F32)).astype(BF16)
     across = hop(cross, "tp", 2)
@@ -349,12 +358,12 @@
 
     grad_type = BF16 if dense else F32
     parts = pl.pallas_call(
-        functools.partial(backward_kernel, (0, 1, 2, 3), n_pre, scaling),
+        functools.partial(backward_kernel, n_tp - 1, n_pre, scaling),
         out_shape=[jax.ShapeDtypeStruct(x.shape, grad_type) for x in prefix],
-        in_specs=[SMEM] + [VMEM] * (10 + n_pre),
+        in_specs=[SMEM] + [VMEM] * 7,
         out_specs=[VMEM] * n_pre,
         scratch_shapes=[
-            pltpu.VMEM((heads * length, HD), BF16),
+            pltpu.VMEM((HD, heads * length), BF16),
             pltpu.VMEM((heads * length, HD), BF16),
             pltpu.VMEM((n_rows, heads * length), BF16),
             pltpu.VMEM((2, n_rows, length), F32),
@@ -362,7 +371,7 @@
         compiler_params=grant(32),
         cost_estimate=cost(7e9, 1e7),
         name="backward",
-    )(me_tp, output_weight, queries, new_v, exps, row, col, out_grad, near_grad, far_grad, last_grad, *prefix)
+    )(me_tp, output_weight, part_grad, last_grad, q, v_all, exps, row)
 
     if dense:
         back = {k: hop(parts[k], "seq", k) for k in far_first}

time: 75.8 us -> 78.3 us (1.033)
  waiting for transfers between devices: 16.3 us -> 26.3 us
  starting transfers between devices: 36 us -> 31 us
  local copies, waits for them, and re-layouts: 1.23 us -> 0.02 us
  Pallas kernels: 20.2 us -> 19 us
    ppermute x23, waiting for transfers between devices: 16.3 us -> 26.3 us  [hop(): return lax.ppermute(x, axis, [(i, i ^ k) for i in range(n)])]
    ppermute x23, starting transfers between devices: 36 us -> 31 us  [hop(): return lax.ppermute(x, axis, [(i, i ^ k) for i in range(n)])]
    pallas_call x3 -> x4, Pallas kernels: 15.3 us -> 14.1 us  [the longest x1 5.73 us: local(): pl.pallas_call(functools.partial(backward_kernel, n_tp - 1, n_pre, scalin...]
    unnamed x12 -> x8, local copies, waits for them, and re-layouts: 1.23 us -> 0.02 us
  transfers between devices with their start and end apart: 23 -> 23, of which waited for: 6 -> 9; matrix products, arithmetic and copies ran while one was open for 0% -> 0% of each run, Pallas kernels for 27% -> 24%
where the time goes in v3:
time: 78.3 us; the launch traced here: 78.1 us
  starting transfers between devices  31 us (40%)
  waiting for transfers between devices  26.3 us (34%)
  Pallas kernels  19 us (24%)
  other arithmetic  1.07 us (1%)
    ppermute x23, starting transfers between devices, hop(): return lax.ppermute(x, axis, [(i, i ^ k) for i in range(n)])  31 us
    ppermute x23, waiting for transfers between devices, hop(): return lax.ppermute(x, axis, [(i, i ^ k) for i in range(n)])  26.3 us
    pallas_call x1, Pallas kernels, local(): pl.pallas_call(functools.partial(backward_kernel, n_tp - 1, n_pre, scalin...  5.73 us
    pallas_call x1, Pallas kernels, local(): pl.pallas_call(functools.partial(forward_kernel, n_pre, scaling), out_sha...  4.07 us
    pallas_call x1, Pallas kernels, local(): pl.pallas_call(functools.partial(kv_kernel, (1, 0, 2), n_tp - 1), out_sha...  2.67 us
    pallas_call x2, Pallas kernels, project(): pl.pallas_call(functools.partial(project_kernel, order), out_shape=[jax.S...  2.49 us
    pallas_call x1, Pallas kernels, local(): pl.pallas_call(functools.partial(grad_kernel, (0, 1, 2)), out_shape=jax.S...  1.62 us
  transfers between devices with their start and end apart: 23, of which 9 were waited for; matrix products, arithmetic and copies ran while one was open for 0% of the time, Pallas kernels for 24%

profile of v3, /device:TPU:0, one launch (start us, length us, event | category | flops | bytes accessed | tf_op | source)
XLA Modules:
  0.0 78.1 jit_solution(1017792919882659637)
XLA Ops:
  0.6 3.1 %collective-permute-start.1 = (bf16[256,896]{1,0:T(8,128)(2,1)}, bf16[256,896]{1,0:T(8,128)(2,1)S(1)}, u32[]{:S(2)}, u32[]{:S(2)}) collective-permute-start(bf16[256,896]{1,0:T(8,128)(2,1)} %own_hbm.1), channel_id=1, source_target_pairs={{0,2},{1,3},{2,0},{3,1},{4,6},{5,7},{6,4},{7,5},{8,10},{9,11},{10,... | collective-permute-start | bytes 1376264 | tf_op jit(solution)/shard_map/ppermute | solution.py:239
  3.7 10.7 %collective-permute-done.1.refs_1_ = bf16[256,896]{1,0:T(8,128)(2,1)S(1)} collective-permute-done((bf16[256,896]{1,0:T(8,128)(2,1)}, bf16[256,896]{1,0:T(8,128)(2,1)S(1)}, u32[]{:S(2)}, u32[]{:S(2)}) %collective-permute-start.1) | collective-permute-done | bytes 458784 | tf_op jit(solution)/shard_map/ppermute | solution.py:239
  15.4 1.8 %collective-permute-start.3 = (bf16[128,256]{1,0:T(8,128)(2,1)S(1)}, bf16[128,256]{1,0:T(8,128)(2,1)S(1)}, u32[]{:S(2)}, u32[]{:S(2)}) collective-permute-start(bf16[128,256]{1,0:T(8,128)(2,1)S(1)} %get-tuple-element.40), channel_id=1, source_target_pairs={{0,4},{4,0},{8,12},{12,8},{16,20},{20,16},{24,28},{28,24},{1,5},{5... | collective-permute-start | bytes 196616 | tf_op jit(solution)/shard_map/ppermute | solution.py:239
  17.2 1.6 %collective-permute-start.4 = (bf16[128,256]{1,0:T(8,128)(2,1)S(1)}, bf16[128,256]{1,0:T(8,128)(2,1)S(1)}, u32[]{:S(2)}, u32[]{:S(2)}) collective-permute-start(bf16[128,256]{1,0:T(8,128)(2,1)S(1)} %get-tuple-element.41), channel_id=1, source_target_pairs={{0,8},{4,12},{8,0},{12,4},{16,24},{20,28},{24,16},{28,20},{1,9},{5... | collective-permute-start | bytes 196616 | tf_op jit(solution)/shard_map/ppermute | solution.py:239
  20.0 2.8 %collective-permute-start.6 = (bf16[128,256]{1,0:T(8,128)(2,1)S(1)}, bf16[128,256]{1,0:T(8,128)(2,1)S(1)}, u32[]{:S(2)}, u32[]{:S(2)}) collective-permute-start(bf16[128,256]{1,0:T(8,128)(2,1)S(1)} %get-tuple-element.43), channel_id=1, source_target_pairs={{0,16},{4,20},{8,24},{12,28},{16,0},{20,4},{24,8},{28,12},{1,17},{... | collective-permute-start | bytes 196616 | tf_op jit(solution)/shard_map/ppermute | solution.py:239
  24.1 3.6 %collective-permute-start.8 = (bf16[128,256]{1,0:T(8,128)(2,1)S(1)}, bf16[128,256]{1,0:T(8,128)(2,1)S(1)}, u32[]{:S(2)}, u32[]{:S(2)}) collective-permute-start(bf16[128,256]{1,0:T(8,128)(2,1)S(1)} %get-tuple-element.45), channel_id=1, source_target_pairs={{0,24},{4,28},{8,16},{12,20},{16,8},{20,12},{24,0},{28,4},{1,25},{... | collective-permute-start | bytes 196616 | tf_op jit(solution)/shard_map/ppermute | solution.py:239
  27.7 1.3 %collective-permute-start.9 = (bf16[128,256]{1,0:T(8,128)(2,1)S(1)}, bf16[128,256]{1,0:T(8,128)(2,1)S(1)}, u32[]{:S(2)}, u32[]{:S(2)}) collective-permute-start(bf16[128,256]{1,0:T(8,128)(2,1)S(1)} %get-tuple-element.46), channel_id=1, source_target_pairs={{0,28},{4,24},{8,20},{12,16},{16,12},{20,8},{24,4},{28,0},{1,29},{... | collective-permute-start | bytes 196616 | tf_op jit(solution)/shard_map/ppermute | solution.py:239
  29.0 2.7 %kv.1 = (f32[256,128]{1,0:T(8,128)S(1)}, f32[256,128]{1,0:T(8,128)S(1)}, bf16[256,896]{1,0:T(8,128)(2,1)S(1)}, bf16[896,128]{1,0:T(8,128)(2,1)S(1)}, bf16[896,128]{1,0:T(8,128)(2,1)S(1)}) custom-call(s32[1]{0:T(128)} %bitcast.me_ref, bf16[256,896]{1,0:T(8,128)(2,1)} %own_hbm.1, bf16[256,896]{1,0:T(8,128)(2,1)S(1)} %collective-permute-done.refs_0_, ...), custom_call_target="tpu_custom_call" | custom-call | flops 400000000 | bytes 3000000 | tf_op jit(solution)/shard_map/kv/pallas_call | solution.py:293
  32.7 1.5 %collective-permute-start.14 = (bf16[256,896]{1,0:T(8,128)(2,1)}, bf16[256,896]{1,0:T(8,128)(2,1)S(1)}, u32[]{:S(2)}, u32[]{:S(2)}) collective-permute-start(bf16[256,896]{1,0:T(8,128)(2,1)} %refs_0_.1), channel_id=1, source_target_pairs={{0,2},{1,3},{2,0},{3,1},{4,6},{5,7},{6,4},{7,5},{8,10},{9,11},{10,... | collective-permute-start | bytes 1376264 | tf_op jit(solution)/shard_map/ppermute | solution.py:239
  34.8 4.1 %forward.1 = (bf16[256,896]{1,0:T(8,128)(2,1)S(1)}, bf16[1280,1792]{1,0:T(8,128)(2,1)S(1)}, f32[8,256]{1,0:T(8,128)S(1)}, bf16[1280,128]{1,0:T(8,128)(2,1)S(1)}) custom-call(bf16[896,128]{1,0:T(8,128)(2,1)S(1)} %get-tuple-element.34.wk_ref, bf16[896,128]{1,0:T(8,128)(2,1)S(1)} %get-tuple-element.35.wv_ref, ...), custom_call_target="tpu_custom_call" | custom-call | flops 5000000000 | bytes 10000000 | tf_op jit(solution)/shard_map/forward/pallas_call | solution.py:310
  40.2 4.7 %collective-permute-done.14.refs_2_ = bf16[256,896]{1,0:T(8,128)(2,1)S(1)} collective-permute-done((bf16[256,896]{1,0:T(8,128)(2,1)}, bf16[256,896]{1,0:T(8,128)(2,1)S(1)}, u32[]{:S(2)}, u32[]{:S(2)}) %collective-permute-start.14) | collective-permute-done | bytes 458784 | tf_op jit(solution)/shard_map/ppermute | solution.py:239
  44.9 1.6 %grad.1.part_ref = f32[896,256]{1,0:T(8,128)S(1)} custom-call(s32[1]{0:T(128)} %bitcast.me_ref, bf16[896,3584]{1,0:T(8,128)(2,1)S(1)} %bitcast.3, bf16[256,896]{1,0:T(8,128)(2,1)S(1)} %copy-done, bf16[256,896]{1,0:T(8,128)(2,1)S(1)} %collective-permute-done.13.refs_1_, bf16[256,896]{1,0:T(8,128)(2,1)S(1)} %collective-permute-done.14.refs_2_), custom_call_target="tpu_custom_call" | custom-call | flops 1500000000 | bytes 8000000 | tf_op jit(solution)/shard_map/grad/pallas_call | solution.py:331
  48.5 1.6 %collective-permute-start.12 = (bf16[256,896]{1,0:T(8,128)(2,1)S(1)}, bf16[256,896]{1,0:T(8,128)(2,1)S(1)}, u32[]{:S(2)}, u32[]{:S(2)}) collective-permute-start(bf16[256,896]{1,0:T(8,128)(2,1)S(1)} %add_convert_fusion.1), channel_id=1, source_target_pairs={{0,2},{1,3},{2,0},{3,1},{4,6},{5,7},{6,4},{7,5},{8,10},{9,11},{10,... | collective-permute-start | bytes 1376264 | tf_op jit(solution)/shard_map/ppermute | solution.py:239
  50.1 5.7 %backward.1 = (bf16[128,256]{1,0:T(8,128)(2,1)S(1)}, bf16[128,256]{1,0:T(8,128)(2,1)S(1)}, bf16[128,256]{1,0:T(8,128)(2,1)S(1)}, bf16[128,256]{1,0:T(8,128)(2,1)...) custom-call(s32[1]{0:T(128)} %bitcast.me_ref, ...), custom_call_target="tpu_custom_call" | custom-call | flops 7000000000 | bytes 10000000 | tf_op jit(solution)/shard_map/backward/pallas_call | solution.py:360
  56.3 1.3 %collective-permute-start.17 = (bf16[128,256]{1,0:T(8,128)(2,1)S(1)}, bf16[128,256]{1,0:T(8,128)(2,1)S(1)}, u32[]{:S(2)}, u32[]{:S(2)}) collective-permute-start(bf16[128,256]{1,0:T(8,128)(2,1)S(1)} %get-tuple-element.57), channel_id=1, source_target_pairs={{0,8},{4,12},{8,0},{12,4},{16,24},{20,28},{24,16},{28,20},{1,9},{5... | collective-permute-start | bytes 196616 | tf_op jit(solution)/shard_map/ppermute | solution.py:239
  57.6 1.8 %collective-permute-start.18 = (bf16[128,256]{1,0:T(8,128)(2,1)S(1)}, bf16[128,256]{1,0:T(8,128)(2,1)S(1)}, u32[]{:S(2)}, u32[]{:S(2)}) collective-permute-start(bf16[128,256]{1,0:T(8,128)(2,1)S(1)} %get-tuple-element.58), channel_id=1, source_target_pairs={{0,12},{4,8},{8,4},{12,0},{16,28},{20,24},{24,20},{28,16},{1,13},{... | collective-permute-start | bytes 196616 | tf_op jit(solution)/shard_map/ppermute | solution.py:239
  60.1 1.8 %collective-permute-start.19 = (bf16[128,256]{1,0:T(8,128)(2,1)S(1)}, bf16[128,256]{1,0:T(8,128)(2,1)S(1)}, u32[]{:S(2)}, u32[]{:S(2)}) collective-permute-start(bf16[128,256]{1,0:T(8,128)(2,1)S(1)} %get-tuple-element.59), channel_id=1, source_target_pairs={{0,16},{4,20},{8,24},{12,28},{16,0},{20,4},{24,8},{28,12},{1,17},{... | collective-permute-start | bytes 196616 | tf_op jit(solution)/shard_map/ppermute | solution.py:239
  61.9 2.9 %collective-permute-start.20 = (bf16[128,256]{1,0:T(8,128)(2,1)S(1)}, bf16[128,256]{1,0:T(8,128)(2,1)S(1)}, u32[]{:S(2)}, u32[]{:S(2)}) collective-permute-start(bf16[128,256]{1,0:T(8,128)(2,1)S(1)} %get-tuple-element.60), channel_id=1, source_target_pairs={{0,20},{4,16},{8,28},{12,24},{16,4},{20,0},{24,12},{28,8},{1,21},{... | collective-permute-start | bytes 196616 | tf_op jit(solution)/shard_map/ppermute | solution.py:239
  64.8 1.7 %collective-permute-start.21 = (bf16[128,256]{1,0:T(8,128)(2,1)S(1)}, bf16[128,256]{1,0:T(8,128)(2,1)S(1)}, u32[]{:S(2)}, u32[]{:S(2)}) collective-permute-start(bf16[128,256]{1,0:T(8,128)(2,1)S(1)} %get-tuple-element.61), channel_id=1, source_target_pairs={{0,24},{4,28},{8,16},{12,20},{16,8},{20,12},{24,0},{28,4},{1,25},{... | collective-permute-start | bytes 196616 | tf_op jit(solution)/shard_map/ppermute | solution.py:239
  66.5 2.3 %collective-permute-done.19.refs_4_ = bf16[128,256]{1,0:T(8,128)(2,1)S(1)} collective-permute-done((bf16[128,256]{1,0:T(8,128)(2,1)S(1)}, bf16[128,256]{1,0:T(8,128)(2,1)S(1)}, u32[]{:S(2)}, u32[]{:S(2)}) %collective-permute-start.19) | collective-permute-done | bytes 65568 | tf_op jit(solution)/shard_map/ppermute | solution.py:239
  68.8 1.7 %collective-permute-start.22 = (bf16[128,256]{1,0:T(8,128)(2,1)S(1)}, bf16[128,256]{1,0:T(8,128)(2,1)S(1)}, u32[]{:S(2)}, u32[]{:S(2)}) collective-permute-start(bf16[128,256]{1,0:T(8,128)(2,1)S(1)} %get-tuple-element.62), channel_id=1, source_target_pairs={{0,28},{4,24},{8,20},{12,16},{16,12},{20,8},{24,4},{28,0},{1,29},{... | collective-permute-start | bytes 196616 | tf_op jit(solution)/shard_map/ppermute | solution.py:239
  70.5 1.6 %collective-permute-done.20.refs_5_ = bf16[128,256]{1,0:T(8,128)(2,1)S(1)} collective-permute-done((bf16[128,256]{1,0:T(8,128)(2,1)S(1)}, bf16[128,256]{1,0:T(8,128)(2,1)S(1)}, u32[]{:S(2)}, u32[]{:S(2)}) %collective-permute-start.20) | collective-permute-done | bytes 65568 | tf_op jit(solution)/shard_map/ppermute | solution.py:239
  72.1 3.6 %collective-permute-done.22.refs_7_ = bf16[128,256]{1,0:T(8,128)(2,1)S(1)} collective-permute-done((bf16[128,256]{1,0:T(8,128)(2,1)S(1)}, bf16[128,256]{1,0:T(8,128)(2,1)S(1)}, u32[]{:S(2)}, u32[]{:S(2)}) %collective-permute-start.22) | collective-permute-done | bytes 65568 | tf_op jit(solution)/shard_map/ppermute | solution.py:239
  75.8 1.4 %place.1 = (f32[256,128]{1,0:T(8,128)}, f32[256,128]{1,0:T(8,128)}) custom-call(s32[1]{0:T(128)} %bitcast.1.me_ref, s32[8,16]{1,0:T(8,128)S(1)} %copy-done.1, bf16[128,256]{1,0:T(8,128)(2,1)S(1)} %get-tuple-element.55.refs_0_, bf16[128,256]{1,0:T(8,128)(2,1)S(1)} %collective-permute-done.16.refs_1_, bf16[128,256]{1,0:T(8,128)(2,1)S(1)} %collective-permute-done.17.refs_2_, ...), custom_call_target="tpu_custom_call" | custom-call | bytes 1048576 | tf_op jit(solution)/shard_map/place/pallas_call | solution.py:380
  (41 shorter events, 10.6 us)
Async XLA Ops:
  0.6 13.8 %collective-permute-start.1 = (bf16[256,896]{1,0:T(8,128)(2,1)}, bf16[256,896]{1,0:T(8,128)(2,1)S(1)}, u32[]{:S(2)}, u32[]{:S(2)}) collective-permute-start(bf16[256,896]{1,0:T(8,128)(2,1)} %own_hbm.1), channel_id=1, source_target_pairs={{0,2},{1,3},{2,0},{3,1},{4,6},{5,7},{6,4},{7,5},{8,10},{9,11},{10,... | collective-permute-start | bytes 1376264 | tf_op jit(solution)/shard_map/ppermute | solution.py:239
  3.7 24.0 %collective-permute-start = (bf16[256,896]{1,0:T(8,128)(2,1)}, bf16[256,896]{1,0:T(8,128)(2,1)S(1)}, u32[]{:S(2)}, u32[]{:S(2)}) collective-permute-start(bf16[256,896]{1,0:T(8,128)(2,1)} %own_hbm.1), channel_id=1, source_target_pairs={{0,1},{1,0},{2,3},{3,2},{4,5},{5,4},{6,7},{7,6},{8,9},{9,8},{10,11... | collective-permute-start | bytes 1376264 | tf_op jit(solution)/shard_map/ppermute | solution.py:239
  14.4 20.3 %collective-permute-start.2 = (bf16[256,896]{1,0:T(8,128)(2,1)S(1)}, bf16[256,896]{1,0:T(8,128)(2,1)S(1)}, u32[]{:S(2)}, u32[]{:S(2)}) collective-permute-start(bf16[256,896]{1,0:T(8,128)(2,1)S(1)} %collective-permute-done.1.refs_1_), channel_id=1, source_target_pairs={{0,1},{1,0},{2,3},{3,2},{4,5},{5,4},{6,7},{7,6},{8,9},{9,8},{10,11... | collective-permute-start | bytes 1376264 | tf_op jit(solution)/shard_map/ppermute | solution.py:239
  15.4 4.6 %collective-permute-start.3 = (bf16[128,256]{1,0:T(8,128)(2,1)S(1)}, bf16[128,256]{1,0:T(8,128)(2,1)S(1)}, u32[]{:S(2)}, u32[]{:S(2)}) collective-permute-start(bf16[128,256]{1,0:T(8,128)(2,1)S(1)} %get-tuple-element.40), channel_id=1, source_target_pairs={{0,4},{4,0},{8,12},{12,8},{16,20},{20,16},{24,28},{28,24},{1,5},{5... | collective-permute-start | bytes 196616 | tf_op jit(solution)/shard_map/ppermute | solution.py:239
  17.2 5.6 %collective-permute-start.4 = (bf16[128,256]{1,0:T(8,128)(2,1)S(1)}, bf16[128,256]{1,0:T(8,128)(2,1)S(1)}, u32[]{:S(2)}, u32[]{:S(2)}) collective-permute-start(bf16[128,256]{1,0:T(8,128)(2,1)S(1)} %get-tuple-element.41), channel_id=1, source_target_pairs={{0,8},{4,12},{8,0},{12,4},{16,24},{20,28},{24,16},{28,20},{1,9},{5... | collective-permute-start | bytes 196616 | tf_op jit(solution)/shard_map/ppermute | solution.py:239
  18.8 5.3 %collective-permute-start.5 = (bf16[128,256]{1,0:T(8,128)(2,1)S(1)}, bf16[128,256]{1,0:T(8,128)(2,1)S(1)}, u32[]{:S(2)}, u32[]{:S(2)}) collective-permute-start(bf16[128,256]{1,0:T(8,128)(2,1)S(1)} %get-tuple-element.42), channel_id=1, source_target_pairs={{0,12},{4,8},{8,4},{12,0},{16,28},{20,24},{24,20},{28,16},{1,13},{... | collective-permute-start | bytes 196616 | tf_op jit(solution)/shard_map/ppermute | solution.py:239
  20.0 11.6 %collective-permute-start.6 = (bf16[128,256]{1,0:T(8,128)(2,1)S(1)}, bf16[128,256]{1,0:T(8,128)(2,1)S(1)}, u32[]{:S(2)}, u32[]{:S(2)}) collective-permute-start(bf16[128,256]{1,0:T(8,128)(2,1)S(1)} %get-tuple-element.43), channel_id=1, source_target_pairs={{0,16},{4,20},{8,24},{12,28},{16,0},{20,4},{24,8},{28,12},{1,17},{... | collective-permute-start | bytes 196616 | tf_op jit(solution)/shard_map/ppermute | solution.py:239
  22.8 9.9 %collective-permute-start.7 = (bf16[128,256]{1,0:T(8,128)(2,1)S(1)}, bf16[128,256]{1,0:T(8,128)(2,1)S(1)}, u32[]{:S(2)}, u32[]{:S(2)}) collective-permute-start(bf16[128,256]{1,0:T(8,128)(2,1)S(1)} %get-tuple-element.44), channel_id=1, source_target_pairs={{0,20},{4,16},{8,28},{12,24},{16,4},{20,0},{24,12},{28,8},{1,21},{... | collective-permute-start | bytes 196616 | tf_op jit(solution)/shard_map/ppermute | solution.py:239
  24.1 10.1 %collective-permute-start.8 = (bf16[128,256]{1,0:T(8,128)(2,1)S(1)}, bf16[128,256]{1,0:T(8,128)(2,1)S(1)}, u32[]{:S(2)}, u32[]{:S(2)}) collective-permute-start(bf16[128,256]{1,0:T(8,128)(2,1)S(1)} %get-tuple-element.45), channel_id=1, source_target_pairs={{0,24},{4,28},{8,16},{12,20},{16,8},{20,12},{24,0},{28,4},{1,25},{... | collective-permute-start | bytes 196616 | tf_op jit(solution)/shard_map/ppermute | solution.py:239
  27.7 7.1 %collective-permute-start.9 = (bf16[128,256]{1,0:T(8,128)(2,1)S(1)}, bf16[128,256]{1,0:T(8,128)(2,1)S(1)}, u32[]{:S(2)}, u32[]{:S(2)}) collective-permute-start(bf16[128,256]{1,0:T(8,128)(2,1)S(1)} %get-tuple-element.46), channel_id=1, source_target_pairs={{0,28},{4,24},{8,20},{12,16},{16,12},{20,8},{24,4},{28,0},{1,29},{... | collective-permute-start | bytes 196616 | tf_op jit(solution)/shard_map/ppermute | solution.py:239
  31.7 13.2 %collective-permute-start.13 = (bf16[256,896]{1,0:T(8,128)(2,1)}, bf16[256,896]{1,0:T(8,128)(2,1)S(1)}, u32[]{:S(2)}, u32[]{:S(2)}) collective-permute-start(bf16[256,896]{1,0:T(8,128)(2,1)} %refs_0_.1), channel_id=1, source_target_pairs={{0,1},{1,0},{2,3},{3,2},{4,5},{5,4},{6,7},{7,6},{8,9},{9,8},{10,11... | collective-permute-start | bytes 1376264 | tf_op jit(solution)/shard_map/ppermute | solution.py:239
  32.7 12.2 %collective-permute-start.14 = (bf16[256,896]{1,0:T(8,128)(2,1)}, bf16[256,896]{1,0:T(8,128)(2,1)S(1)}, u32[]{:S(2)}, u32[]{:S(2)}) collective-permute-start(bf16[256,896]{1,0:T(8,128)(2,1)} %refs_0_.1), channel_id=1, source_target_pairs={{0,2},{1,3},{2,0},{3,1},{4,6},{5,7},{6,4},{7,5},{8,10},{9,11},{10,... | collective-permute-start | bytes 1376264 | tf_op jit(solution)/shard_map/ppermute | solution.py:239
  40.1 8.2 %collective-permute-start.11 = (bf16[256,896]{1,0:T(8,128)(2,1)S(1)}, bf16[256,896]{1,0:T(8,128)(2,1)S(1)}, u32[]{:S(2)}, u32[]{:S(2)}) collective-permute-start(bf16[256,896]{1,0:T(8,128)(2,1)S(1)} %get-tuple-element.51), channel_id=1, source_target_pairs={{0,1},{1,0},{2,3},{3,2},{4,5},{5,4},{6,7},{7,6},{8,9},{9,8},{10,11... | collective-permute-start | bytes 1376264 | tf_op jit(solution)/shard_map/ppermute | solution.py:239
  44.9 5.2 %collective-permute-start.15 = (bf16[256,896]{1,0:T(8,128)(2,1)S(1)}, bf16[256,896]{1,0:T(8,128)(2,1)S(1)}, u32[]{:S(2)}, u32[]{:S(2)}) collective-permute-start(bf16[256,896]{1,0:T(8,128)(2,1)S(1)} %collective-permute-done.14.refs_2_), channel_id=1, source_target_pairs={{0,1},{1,0},{2,3},{3,2},{4,5},{5,4},{6,7},{7,6},{8,9},{9,8},{10,11... | collective-permute-start | bytes 1376264 | tf_op jit(solution)/shard_map/ppermute | solution.py:239
  47.8 29.4 %collective-permute-start.10 = (bf16[256,896]{1,0:T(8,128)(2,1)S(1)}, bf16[256,896]{1,0:T(8,128)(2,1)S(1)}, u32[]{:S(2)}, u32[]{:S(2)}) collective-permute-start(bf16[256,896]{1,0:T(8,128)(2,1)S(1)} %get-tuple-element.49), channel_id=1, source_target_pairs={{0,1},{1,0},{2,3},{3,2},{4,5},{5,4},{6,7},{7,6},{8,9},{9,8},{10,11... | collective-permute-start | bytes 1376264 | tf_op jit(solution)/shard_map/ppermute | solution.py:239
  48.5 28.7 %collective-permute-start.12 = (bf16[256,896]{1,0:T(8,128)(2,1)S(1)}, bf16[256,896]{1,0:T(8,128)(2,1)S(1)}, u32[]{:S(2)}, u32[]{:S(2)}) collective-permute-start(bf16[256,896]{1,0:T(8,128)(2,1)S(1)} %add_convert_fusion.1), channel_id=1, source_target_pairs={{0,2},{1,3},{2,0},{3,1},{4,6},{5,7},{6,4},{7,5},{8,10},{9,11},{10,... | collective-permute-start | bytes 1376264 | tf_op jit(solution)/shard_map/ppermute | solution.py:239
  50.1 25.7 %copy-start.1 = (s32[8,16]{1,0:T(8,128)S(1)}, s32[8,16]{1,0:T(8,128)}, u32[]{:S(2)}) copy-start(s32[8,16]{1,0:T(8,128)} %reads_ref.1) | copy-start | bytes 1540
  55.8 4.3 %collective-permute-start.16 = (bf16[128,256]{1,0:T(8,128)(2,1)S(1)}, bf16[128,256]{1,0:T(8,128)(2,1)S(1)}, u32[]{:S(2)}, u32[]{:S(2)}) collective-permute-start(bf16[128,256]{1,0:T(8,128)(2,1)S(1)} %get-tuple-element.56), channel_id=1, source_target_pairs={{0,4},{4,0},{8,12},{12,8},{16,20},{20,16},{24,28},{28,24},{1,5},{5... | collective-permute-start | bytes 196616 | tf_op jit(solution)/shard_map/ppermute | solution.py:239
  56.3 5.6 %collective-permute-start.17 = (bf16[128,256]{1,0:T(8,128)(2,1)S(1)}, bf16[128,256]{1,0:T(8,128)(2,1)S(1)}, u32[]{:S(2)}, u32[]{:S(2)}) collective-permute-start(bf16[128,256]{1,0:T(8,128)(2,1)S(1)} %get-tuple-element.57), channel_id=1, source_target_pairs={{0,8},{4,12},{8,0},{12,4},{16,24},{20,28},{24,16},{28,20},{1,9},{5... | collective-permute-start | bytes 196616 | tf_op jit(solution)/shard_map/ppermute | solution.py:239
  57.6 7.2 %collective-permute-start.18 = (bf16[128,256]{1,0:T(8,128)(2,1)S(1)}, bf16[128,256]{1,0:T(8,128)(2,1)S(1)}, u32[]{:S(2)}, u32[]{:S(2)}) collective-permute-start(bf16[128,256]{1,0:T(8,128)(2,1)S(1)} %get-tuple-element.58), channel_id=1, source_target_pairs={{0,12},{4,8},{8,4},{12,0},{16,28},{20,24},{24,20},{28,16},{1,13},{... | collective-permute-start | bytes 196616 | tf_op jit(solution)/shard_map/ppermute | solution.py:239
  60.1 8.7 %collective-permute-start.19 = (bf16[128,256]{1,0:T(8,128)(2,1)S(1)}, bf16[128,256]{1,0:T(8,128)(2,1)S(1)}, u32[]{:S(2)}, u32[]{:S(2)}) collective-permute-start(bf16[128,256]{1,0:T(8,128)(2,1)S(1)} %get-tuple-element.59), channel_id=1, source_target_pairs={{0,16},{4,20},{8,24},{12,28},{16,0},{20,4},{24,8},{28,12},{1,17},{... | collective-permute-start | bytes 196616 | tf_op jit(solution)/shard_map/ppermute | solution.py:239
  61.9 10.3 %collective-permute-start.20 = (bf16[128,256]{1,0:T(8,128)(2,1)S(1)}, bf16[128,256]{1,0:T(8,128)(2,1)S(1)}, u32[]{:S(2)}, u32[]{:S(2)}) collective-permute-start(bf16[128,256]{1,0:T(8,128)(2,1)S(1)} %get-tuple-element.60), channel_id=1, source_target_pairs={{0,20},{4,16},{8,28},{12,24},{16,4},{20,0},{24,12},{28,8},{1,21},{... | collective-permute-start | bytes 196616 | tf_op jit(solution)/shard_map/ppermute | solution.py:239
  64.8 7.4 %collective-permute-start.21 = (bf16[128,256]{1,0:T(8,128)(2,1)S(1)}, bf16[128,256]{1,0:T(8,128)(2,1)S(1)}, u32[]{:S(2)}, u32[]{:S(2)}) collective-permute-start(bf16[128,256]{1,0:T(8,128)(2,1)S(1)} %get-tuple-element.61), channel_id=1, source_target_pairs={{0,24},{4,28},{8,16},{12,20},{16,8},{20,12},{24,0},{28,4},{1,25},{... | collective-permute-start | bytes 196616 | tf_op jit(solution)/shard_map/ppermute | solution.py:239
  68.8 7.0 %collective-permute-start.22 = (bf16[128,256]{1,0:T(8,128)(2,1)S(1)}, bf16[128,256]{1,0:T(8,128)(2,1)S(1)}, u32[]{:S(2)}, u32[]{:S(2)}) collective-permute-start(bf16[128,256]{1,0:T(8,128)(2,1)S(1)} %get-tuple-element.62), channel_id=1, source_target_pairs={{0,28},{4,24},{8,20},{12,16},{16,12},{20,8},{24,4},{28,0},{1,29},{... | collective-permute-start | bytes 196616 | tf_op jit(solution)/shard_map/ppermute | solution.py:239
  (3 other events, 20.0 us)

commit v4 on v3

--- a/solution.py
+++ b/solution.py
@@ -30,24 +30,33 @@
     return pl.CostEstimate(flops=int(flops), bytes_accessed=int(nbytes), transcendentals=int(trans))
 
 
-def pick_kernel(n, cap, here, me_ref, reads_hbm, keys_hbm, values_hbm, *refs):
-    outs, (reads_ref, keys_ref, values_ref, sems) = refs[:n], refs[n:]
-    me = me_ref[0]
+def pick_into(outs, cap, here, me, holder, reads_ref, keys_ref, values_ref):
+    for k, out in enumerate(outs):
+        for r in range(cap):
+            block = reads_ref[me ^ k, cap * holder + r] - here * holder
+            rows = pl.ds(pl.multiple_of(block * PBLK, PBLK), PBLK)
+            out[r * PBLK:(r + 1) * PBLK, :HD] = keys_ref[rows, :]
+            out[r * PBLK:(r + 1) * PBLK, HD:] = values_ref[rows, :]
+
+
+def pick_kernel(cap, here, me_ref, reads_hbm, keys_hbm, values_hbm, *refs):
+    outs, (kept_ref, reads_ref, keys_ref, values_ref, sems) = refs[:-5], refs[-5:]
     copies = [
         pltpu.make_async_copy(src, dst, sems.at[i])
         for i, (src, dst) in enumerate(
-            ((reads_hbm, reads_ref), (keys_hbm, keys_ref), (values_hbm, values_ref)))
+            ((reads_hbm, reads_ref), (keys_hbm, keys_ref), (values_hbm, values_ref), (reads_hbm, kept_ref)))
     ]
     for copy in copies:
         copy.start()
     for copy in copies:
         copy.wait()
-    for k in range(n):
-        for r in range(cap):
-            block = reads_ref[me ^ k, cap * me + r] - here * me
-            rows = pl.ds(pl.multiple_of(block * PBLK, PBLK), PBLK)
-            outs[k][r * PBLK:(r + 1) * PBLK, :HD] = keys_ref[rows, :]
-            outs[k][r * PBLK:(r + 1) * PBLK, HD:] = values_ref[rows, :]
+    me = me_ref[0]
+    pick_into(outs, cap, here, me, me, reads_ref, keys_ref, values_ref)
+
+
+def pick_far_kernel(cap, here, flip, me_ref, reads_ref, keys_ref, values_ref, *outs):
+    me = me_ref[0]
+    pick_into(outs, cap, here, me, me ^ flip, reads_ref, keys_ref, values_ref)
 
 
 def place_kernel(n, cap, here, me_ref, reads_ref, *refs):
@@ -69,8 +78,8 @@
     return [pltpu.make_async_copy(w.at[rows], buf.at[slot], sems.at[j, slot]) for j, (w, buf) in enumerate(zip(hbms, bufs))]
 
 
-def kv_kernel(order, last, me_ref, own_hbm, *refs):
-    hidden, (wk_hbm, wv_hbm, q_hbm, k_ref, v_ref, q_ref, lastk_ref, lastv_ref) = refs[:-13], refs[-13:-5]
+def kv_kernel(order, rest, me_ref, own_hbm, *refs):
+    hidden, (wk_hbm, wv_hbm, q_hbm, k_ref, v_ref, q_ref, restk_ref, restv_ref) = refs[:-13], refs[-13:-5]
     own_ref, wk_ref, wv_ref, sems, far_sems = refs[-5:]
     me = me_ref[0]
     width = own_ref.shape[1]
@@ -83,12 +92,11 @@
             copy.start()
     own = pltpu.make_async_copy(own_hbm, own_ref, far_sems.at[0])
     own.start()
-    rows = pl.ds(pl.multiple_of((me ^ last) * width, width), width)
-    later = [
-        pltpu.make_async_copy(q_hbm, q_ref, far_sems.at[1]),
-        pltpu.make_async_copy(wk_hbm.at[rows], lastk_ref, far_sems.at[2]),
-        pltpu.make_async_copy(wv_hbm.at[rows], lastv_ref, far_sems.at[3]),
-    ]
+    later = [pltpu.make_async_copy(q_hbm, q_ref, far_sems.at[1])]
+    for slot, i in enumerate(rest):
+        rows = pl.ds(pl.multiple_of((me ^ i) * width, width), width)
+        later.append(pltpu.make_async_copy(wk_hbm.at[rows], restk_ref.at[slot], far_sems.at[2 + 2 * slot]))
+        later.append(pltpu.make_async_copy(wv_hbm.at[rows], restv_ref.at[slot], far_sems.at[3 + 2 * slot]))
     for copy in later:
         copy.start()
     new_k = jnp.zeros(k_ref.shape, F32)
@@ -107,10 +115,11 @@
         copy.wait()
 
 
-def forward_kernel(n_pre, scaling, wk_ref, wv_ref, hidden_ref, q_ref, partk_ref, partv_ref, *refs):
+def forward_kernel(n_rest, n_pre, scaling, wk_ref, wv_ref, *refs):
+    hidden, (q_ref, partk_ref, partv_ref), refs = refs[:n_rest], refs[n_rest:n_rest + 3], refs[n_rest + 3:]
     prefix = refs[:n_pre]
     ctx_ref, exps_ref, row_ref, v_all, k_all, vt_all, s_buf, sums = refs[n_pre:]
-    length = hidden_ref.shape[0]
+    length = q_ref.shape[0]
     heads = q_ref.shape[1] // HD
     factor = scaling * LOG2E
     at = 0
@@ -119,9 +128,12 @@
         k_all[at:at + size, :] = ref[:, :HD]
         v_all[at:at + size, :] = ref[:, HD:]
         at += size
-    piece = hidden_ref[...]
-    k_all[at:, :] = (partk_ref[...] + dot(piece, wk_ref[...], ((1,), (0,)))).astype(BF16)
-    v_all[at:, :] = (partv_ref[...] + dot(piece, wv_ref[...], ((1,), (0,)))).astype(BF16)
+    new_k, new_v = partk_ref[...], partv_ref[...]
+    for slot, ref in enumerate(hidden):
+        new_k += dot(ref[...], wk_ref[slot], ((1,), (0,)))
+        new_v += dot(ref[...], wv_ref[slot], ((1,), (0,)))
+    k_all[at:, :] = new_k.astype(BF16)
+    v_all[at:, :] = new_v.astype(BF16)
     vt_all[...] = v_all[...].astype(F32).T.astype(BF16)
     visible = lax.broadcasted_iota(jnp.int32, (length, length), 0) <= lax.broadcasted_iota(
         jnp.int32, (length, length), 1)
@@ -251,23 +263,36 @@
 
     if dense:
         shape = jax.ShapeDtypeStruct((cap * PBLK, 2 * HD), BF16)
-        picked = pl.pallas_call(
-            functools.partial(pick_kernel, n_seq, cap, here),
-            out_shape=[shape] * n_seq,
+        half = max(1, n_seq // 2)
+        out_types = [shape] * half
+        far_keys = hop(prefix_keys, "seq", half)
+        far_values = hop(prefix_values, "seq", half)
+        *picked, kept_reads = pl.pallas_call(
+            functools.partial(pick_kernel, cap, here),
+            out_shape=out_types + [jax.ShapeDtypeStruct(reads.shape, jnp.int32)],
             in_specs=[SMEM, HBM, HBM, HBM],
-            out_specs=[VMEM] * n_seq,
+            out_specs=[VMEM] * (half + 1),
             scratch_shapes=[
                 pltpu.SMEM(reads.shape, jnp.int32),
                 pltpu.VMEM(prefix_keys.shape, BF16),
                 pltpu.VMEM(prefix_keys.shape, BF16),
-                pltpu.SemaphoreType.DMA((3,)),
+                pltpu.SemaphoreType.DMA((4,)),
             ],
             cost_estimate=cost(0, 2 ** 20),
             compiler_params=grant(4),
             name="pick",
         )(me_seq, hbm(reads), hbm(prefix_keys), hbm(prefix_values))
-        moved = {k: hop(picked[k], "seq", k) for k in far_first}
-        prefix = [picked[0]] + [moved[k] for k in range(1, n_seq)]
+        picked_far = pl.pallas_call(
+            functools.partial(pick_far_kernel, cap, here, half),
+            out_shape=out_types,
+            in_specs=[SMEM, SMEM, VMEM, VMEM],
+            out_specs=[VMEM] * half,
+            cost_estimate=cost(0, 2 ** 20),
+            compiler_params=grant(4),
+            name="pick_far",
+        )(me_seq, kept_reads, far_keys, far_values)
+        prefix = [picked[0]] + [hop(picked[k], "seq", k) for k in range(1, half)]
+        prefix += [picked_far[0]] + [hop(picked_far[k], "seq", k) for k in range(1, half)]
     else:
         flat = PBLK * 2 * HD
         local_cache = jnp.concatenate([prefix_keys, prefix_values], axis=1).reshape(here, flat)
@@ -289,33 +314,34 @@
     n_pre = len(prefix)
 
     part = jax.ShapeDtypeStruct((length, HD), F32)
-    weight = jax.ShapeDtypeStruct((width, HD), BF16)
-    part_k, part_v, q, last_k, last_v = pl.pallas_call(
-        functools.partial(kv_kernel, (1, 0, 2), n_tp - 1),
+    n_rest = n_tp - 2
+    weight = jax.ShapeDtypeStruct((n_rest, width, HD), BF16)
+    part_k, part_v, q, rest_k, rest_v = pl.pallas_call(
+        functools.partial(kv_kernel, (0, 1), tuple(range(2, n_tp))),
         out_shape=[part, part, jax.ShapeDtypeStruct(queries.shape, BF16), weight, weight],
-        in_specs=[SMEM, HBM] + [VMEM] * (n_tp - 2) + [HBM] * 3,
+        in_specs=[SMEM, HBM, VMEM] + [HBM] * 3,
         out_specs=[VMEM] * 5,
         scratch_shapes=[
             pltpu.VMEM((length, width), BF16),
-            pltpu.VMEM((n_tp - 1, width, HD), BF16),
-            pltpu.VMEM((n_tp - 1, width, HD), BF16),
-            pltpu.SemaphoreType.DMA((2, n_tp - 1)),
-            pltpu.SemaphoreType.DMA((4,)),
+            pltpu.VMEM((2, width, HD), BF16),
+            pltpu.VMEM((2, width, HD), BF16),
+            pltpu.SemaphoreType.DMA((2, 2)),
+            pltpu.SemaphoreType.DMA((2 + 2 * n_rest,)),
         ],
         compiler_params=grant(8),
         cost_estimate=cost(4e8, 3e6),
         name="kv",
-    )(me_tp, hbm(hidden_states), near_hidden, far_hidden, hbm(key_weight), hbm(value_weight), hbm(queries))
+    )(me_tp, hbm(hidden_states), near_hidden, hbm(key_weight), hbm(value_weight), hbm(queries))
 
     ctx, exps, row, v_all = pl.pallas_call(
-        functools.partial(forward_kernel, n_pre, scaling),
+        functools.partial(forward_kernel, n_rest, n_pre, scaling),
         out_shape=[
             jax.ShapeDtypeStruct((length, heads * HD), BF16),
             jax.ShapeDtypeStruct((keys, heads * length), BF16),
             jax.ShapeDtypeStruct((heads + (-heads) % 8, length), F32),
             jax.ShapeDtypeStruct((keys, HD), BF16),
         ],
-        in_specs=[VMEM] * (6 + n_pre),
+        in_specs=[VMEM] * (5 + n_rest + n_pre),
         out_specs=[VMEM] * 4,
         scratch_shapes=[
             pltpu.VMEM((keys, HD), BF16),
@@ -326,7 +352,7 @@
         compiler_params=grant(20),
         cost_estimate=cost(5e9, 1e7, 3e6),
         name="forward",
-    )(last_k, last_v, last_hidden, q, part_k, part_v, *prefix)
+    )(rest_k, rest_v, far_hidden, last_hidden, q, part_k, part_v, *prefix)
 
     part_grad = pl.pallas_call(
         functools.partial(grad_kernel, (0, 1, 2)),
@@ -385,7 +411,7 @@
             cost_estimate=cost(0, 2 ** 20),
             compiler_params=grant(4),
             name="place",
-        )(me_seq, reads, *returned)
+        )(me_seq, kept_reads, *returned)
     else:
         cache_grads = parts[0].reshape(read_count, flat)
         placer = ((my_owner[None, None, :] == jnp.arange(n_seq, dtype=jnp.int32)[:, None, None])

time: 78.3 us -> 77.4 us (0.989)
  waiting for transfers between devices: 26.3 us -> 21 us
  starting transfers between devices: 31 us -> 34.1 us
  Pallas kernels: 19 us -> 19.8 us
    ppermute x23 -> x24, waiting for transfers between devices: 26.3 us -> 21 us  [hop(): return lax.ppermute(x, axis, [(i, i ^ k) for i in range(n)])]
    ppermute x23 -> x24, starting transfers between devices: 31 us -> 34.1 us  [hop(): return lax.ppermute(x, axis, [(i, i ^ k) for i in range(n)])]
    pallas_call x3 -> x4, Pallas kernels: 7.74 us -> 8.49 us  [the longest x1 4.37 us: local(): pl.pallas_call(functools.partial(forward_kernel, n_rest, n_pre, scaling),...]
  transfers between devices with their start and end apart: 23 -> 24, of which waited for: 9 -> 8; matrix products, arithmetic and copies ran while one was open for 0% -> 0% of each run, Pallas kernels for 24% -> 26%
where the time goes in v4:
time: 77.4 us; the launch traced here: 76.7 us
  starting transfers between devices  34.1 us (44%)
  waiting for transfers between devices  21 us (27%)
  Pallas kernels  19.8 us (26%)
  other arithmetic  1.06 us (1%)
  between operations  0.79 us (1%)
    ppermute x24, starting transfers between devices, hop(): return lax.ppermute(x, axis, [(i, i ^ k) for i in range(n)])  34.1 us
    ppermute x24, waiting for transfers between devices, hop(): return lax.ppermute(x, axis, [(i, i ^ k) for i in range(n)])  21 us
    pallas_call x1, Pallas kernels, local(): pl.pallas_call(functools.partial(backward_kernel, n_tp - 1, n_pre, scalin...  5.73 us
    pallas_call x1, Pallas kernels, local(): pl.pallas_call(functools.partial(forward_kernel, n_rest, n_pre, scaling),...  4.37 us
    pallas_call x1, Pallas kernels, local(): pl.pallas_call(functools.partial(kv_kernel, (0, 1), tuple(range(2, n_tp))...  2.5 us
    pallas_call x2, Pallas kernels, project(): pl.pallas_call(functools.partial(project_kernel, order), out_shape=[jax.S...  2.49 us
    pallas_call x1, Pallas kernels, local(): pl.pallas_call(functools.partial(grad_kernel, (0, 1, 2)), out_shape=jax.S...  1.62 us
  transfers between devices with their start and end apart: 24, of which 8 were waited for; matrix products, arithmetic and copies ran while one was open for 0% of the time, Pallas kernels for 26%

profile of v4, /device:TPU:0, one launch (start us, length us, event | category | flops | bytes accessed | tf_op | source)
XLA Modules:
  0.0 76.7 jit_solution(12695665667152742535)
XLA Ops:
  0.6 3.1 %collective-permute-start.1 = (bf16[256,896]{1,0:T(8,128)(2,1)}, bf16[256,896]{1,0:T(8,128)(2,1)S(1)}, u32[]{:S(2)}, u32[]{:S(2)}) collective-permute-start(bf16[256,896]{1,0:T(8,128)(2,1)} %own_hbm.1), channel_id=1, source_target_pairs={{0,2},{1,3},{2,0},{3,1},{4,6},{5,7},{6,4},{7,5},{8,10},{9,11},{10,... | collective-permute-start | bytes 1376264 | tf_op jit(solution)/shard_map/ppermute | solution.py:251
  3.7 10.7 %collective-permute-done.1.refs_0_ = bf16[256,896]{1,0:T(8,128)(2,1)S(1)} collective-permute-done((bf16[256,896]{1,0:T(8,128)(2,1)}, bf16[256,896]{1,0:T(8,128)(2,1)S(1)}, u32[]{:S(2)}, u32[]{:S(2)}) %collective-permute-start.1) | collective-permute-done | bytes 458784 | tf_op jit(solution)/shard_map/ppermute | solution.py:251
  14.4 2.8 %collective-permute-start.6 = (bf16[256,128]{1,0:T(8,128)(2,1)}, bf16[256,128]{1,0:T(8,128)(2,1)S(1)}, u32[]{:S(2)}, u32[]{:S(2)}) collective-permute-start(bf16[256,128]{1,0:T(8,128)(2,1)} %keys_hbm.1), channel_id=1, source_target_pairs={{0,16},{4,20},{8,24},{12,28},{16,0},{20,4},{24,8},{28,12},{1,17},{... | collective-permute-start | bytes 196616 | tf_op jit(solution)/shard_map/ppermute | solution.py:251
  18.3 1.8 %collective-permute-start.3 = (bf16[128,256]{1,0:T(8,128)(2,1)S(1)}, bf16[128,256]{1,0:T(8,128)(2,1)S(1)}, u32[]{:S(2)}, u32[]{:S(2)}) collective-permute-start(bf16[128,256]{1,0:T(8,128)(2,1)S(1)} %get-tuple-element.41), channel_id=1, source_target_pairs={{0,4},{4,0},{8,12},{12,8},{16,20},{20,16},{24,28},{28,24},{1,5},{5... | collective-permute-start | bytes 196616 | tf_op jit(solution)/shard_map/ppermute | solution.py:251
  20.1 1.7 %collective-permute-done.6.keys_ref = bf16[256,128]{1,0:T(8,128)(2,1)S(1)} collective-permute-done((bf16[256,128]{1,0:T(8,128)(2,1)}, bf16[256,128]{1,0:T(8,128)(2,1)S(1)}, u32[]{:S(2)}, u32[]{:S(2)}) %collective-permute-start.6) | collective-permute-done | bytes 65568 | tf_op jit(solution)/shard_map/ppermute | solution.py:251
  21.8 2.0 %collective-permute-start.4 = (bf16[128,256]{1,0:T(8,128)(2,1)S(1)}, bf16[128,256]{1,0:T(8,128)(2,1)S(1)}, u32[]{:S(2)}, u32[]{:S(2)}) collective-permute-start(bf16[128,256]{1,0:T(8,128)(2,1)S(1)} %get-tuple-element.42), channel_id=1, source_target_pairs={{0,8},{4,12},{8,0},{12,4},{16,24},{20,28},{24,16},{28,20},{1,9},{5... | collective-permute-start | bytes 196616 | tf_op jit(solution)/shard_map/ppermute | solution.py:251
  24.4 1.8 %collective-permute-start.5 = (bf16[128,256]{1,0:T(8,128)(2,1)S(1)}, bf16[128,256]{1,0:T(8,128)(2,1)S(1)}, u32[]{:S(2)}, u32[]{:S(2)}) collective-permute-start(bf16[128,256]{1,0:T(8,128)(2,1)S(1)} %get-tuple-element.43), channel_id=1, source_target_pairs={{0,12},{4,8},{8,4},{12,0},{16,28},{20,24},{24,20},{28,16},{1,13},{... | collective-permute-start | bytes 196616 | tf_op jit(solution)/shard_map/ppermute | solution.py:251
  28.1 1.5 %collective-permute-start.8 = (bf16[128,256]{1,0:T(8,128)(2,1)S(1)}, bf16[128,256]{1,0:T(8,128)(2,1)S(1)}, u32[]{:S(2)}, u32[]{:S(2)}) collective-permute-start(bf16[128,256]{1,0:T(8,128)(2,1)S(1)} %get-tuple-element.46), channel_id=1, source_target_pairs={{0,4},{4,0},{8,12},{12,8},{16,20},{20,16},{24,28},{28,24},{1,5},{5... | collective-permute-start | bytes 196616 | tf_op jit(solution)/shard_map/ppermute | solution.py:251
  30.4 2.5 %kv.1 = (f32[256,128]{1,0:T(8,128)S(1)}, f32[256,128]{1,0:T(8,128)S(1)}, bf16[256,896]{1,0:T(8,128)(2,1)S(1)}, bf16[2,896,128]{2,1,0:T(8,128)(2,1)S(1)}, bf16[2,896,128]{2,1,0:T(8,128)(2,1)S(1)}) custom-call(s32[1]{0:T(128)} %bitcast.me_ref, bf16[256,896]{1,0:T(8,128)(2,1)} %own_hbm.1, bf16[256,896]{1,0:T(8,128)(2,1)S(1)} %collective-permute-done.refs_0_, ...), custom_call_target="tpu_custom_call" | custom-call | flops 400000000 | bytes 3000000 | tf_op jit(solution)/shard_map/kv/pallas_call | solution.py:319
  32.9 1.6 %collective-permute-start.15 = (bf16[256,896]{1,0:T(8,128)(2,1)}, bf16[256,896]{1,0:T(8,128)(2,1)S(1)}, u32[]{:S(2)}, u32[]{:S(2)}) collective-permute-start(bf16[256,896]{1,0:T(8,128)(2,1)} %refs_0_.1), channel_id=1, source_target_pairs={{0,2},{1,3},{2,0},{3,1},{4,6},{5,7},{6,4},{7,5},{8,10},{9,11},{10,... | collective-permute-start | bytes 1376264 | tf_op jit(solution)/shard_map/ppermute | solution.py:251
  34.6 4.4 %forward.1 = (bf16[256,896]{1,0:T(8,128)(2,1)S(1)}, bf16[1280,1792]{1,0:T(8,128)(2,1)S(1)}, f32[8,256]{1,0:T(8,128)S(1)}, bf16[1280,128]{1,0:T(8,128)(2,1)S(1)}) custom-call(bf16[2,896,128]{2,1,0:T(8,128)(2,1)S(1)} %get-tuple-element.35.wk_ref, bf16[2,896,128]{2,1,0:T(8,128)(2,1)S(1)} %get-tuple-element.36.wv_ref, ...), custom_call_target="tpu_custom_call" | custom-call | flops 5000000000 | bytes 10000000 | tf_op jit(solution)/shard_map/forward/pallas_call | solution.py:336
  39.0 1.2 %shard_map.113 = (bf16[256,896]{1,0:T(8,128)(2,1)S(1)}, bf16[256,896]{1,0:T(8,128)(2,1)S(1)}) custom-call(s32[1]{0:T(128)} %bitcast.me_ref, bf16[256,896]{1,0:T(8,128)(2,1)S(1)} %get-tuple-element.49.ctx_ref, bf16[896,3584]{1,0:T(8,128)(2,1)S(1)} %bitcast.3), custom_call_target="tpu_custom_call" | custom-call | flops 1000000000 | bytes 4000000 | tf_op jit(solution)/shard_map/pallas_call | solution.py:368
  40.8 3.8 %collective-permute-done.15.refs_2_ = bf16[256,896]{1,0:T(8,128)(2,1)S(1)} collective-permute-done((bf16[256,896]{1,0:T(8,128)(2,1)}, bf16[256,896]{1,0:T(8,128)(2,1)S(1)}, u32[]{:S(2)}, u32[]{:S(2)}) %collective-permute-start.15) | collective-permute-done | bytes 458784 | tf_op jit(solution)/shard_map/ppermute | solution.py:251
  44.6 1.6 %grad.1.part_ref = f32[896,256]{1,0:T(8,128)S(1)} custom-call(s32[1]{0:T(128)} %bitcast.me_ref, bf16[896,3584]{1,0:T(8,128)(2,1)S(1)} %bitcast.3, bf16[256,896]{1,0:T(8,128)(2,1)S(1)} %copy-done, bf16[256,896]{1,0:T(8,128)(2,1)S(1)} %collective-permute-done.14.refs_1_, bf16[256,896]{1,0:T(8,128)(2,1)S(1)} %collective-permute-done.15.refs_2_), custom_call_target="tpu_custom_call" | custom-call | flops 1500000000 | bytes 8000000 | tf_op jit(solution)/shard_map/grad/pallas_call | solution.py:357
  46.2 1.3 %shard_map.112 = (bf16[256,896]{1,0:T(8,128)(2,1)S(1)}, bf16[256,896]{1,0:T(8,128)(2,1)S(1)}) custom-call(s32[1]{0:T(128)} %bitcast.me_ref, bf16[256,896]{1,0:T(8,128)(2,1)S(1)} %get-tuple-element.49.ctx_ref, bf16[896,3584]{1,0:T(8,128)(2,1)S(1)} %bitcast.3), custom_call_target="tpu_custom_call" | custom-call | flops 1000000000 | bytes 4000000 | tf_op jit(solution)/shard_map/pallas_call | solution.py:368
  48.2 1.6 %collective-permute-start.13 = (bf16[256,896]{1,0:T(8,128)(2,1)S(1)}, bf16[256,896]{1,0:T(8,128)(2,1)S(1)}, u32[]{:S(2)}, u32[]{:S(2)}) collective-permute-start(bf16[256,896]{1,0:T(8,128)(2,1)S(1)} %add_convert_fusion.1), channel_id=1, source_target_pairs={{0,2},{1,3},{2,0},{3,1},{4,6},{5,7},{6,4},{7,5},{8,10},{9,11},{10,... | collective-permute-start | bytes 1376264 | tf_op jit(solution)/shard_map/ppermute | solution.py:251
  49.8 5.7 %backward.1 = (bf16[128,256]{1,0:T(8,128)(2,1)S(1)}, bf16[128,256]{1,0:T(8,128)(2,1)S(1)}, bf16[128,256]{1,0:T(8,128)(2,1)S(1)}, bf16[128,256]{1,0:T(8,128)(2,1)...) custom-call(s32[1]{0:T(128)} %bitcast.me_ref, ...), custom_call_target="tpu_custom_call" | custom-call | flops 7000000000 | bytes 10000000 | tf_op jit(solution)/shard_map/backward/pallas_call | solution.py:386
  57.1 2.0 %collective-permute-start.19 = (bf16[128,256]{1,0:T(8,128)(2,1)S(1)}, bf16[128,256]{1,0:T(8,128)(2,1)S(1)}, u32[]{:S(2)}, u32[]{:S(2)}) collective-permute-start(bf16[128,256]{1,0:T(8,128)(2,1)S(1)} %get-tuple-element.60), channel_id=1, source_target_pairs={{0,12},{4,8},{8,4},{12,0},{16,28},{20,24},{24,20},{28,16},{1,13},{... | collective-permute-start | bytes 196616 | tf_op jit(solution)/shard_map/ppermute | solution.py:251
  59.9 3.3 %collective-permute-start.20 = (bf16[128,256]{1,0:T(8,128)(2,1)S(1)}, bf16[128,256]{1,0:T(8,128)(2,1)S(1)}, u32[]{:S(2)}, u32[]{:S(2)}) collective-permute-start(bf16[128,256]{1,0:T(8,128)(2,1)S(1)} %get-tuple-element.61), channel_id=1, source_target_pairs={{0,16},{4,20},{8,24},{12,28},{16,0},{20,4},{24,8},{28,12},{1,17},{... | collective-permute-start | bytes 196616 | tf_op jit(solution)/shard_map/ppermute | solution.py:251
  63.1 2.1 %collective-permute-start.21 = (bf16[128,256]{1,0:T(8,128)(2,1)S(1)}, bf16[128,256]{1,0:T(8,128)(2,1)S(1)}, u32[]{:S(2)}, u32[]{:S(2)}) collective-permute-start(bf16[128,256]{1,0:T(8,128)(2,1)S(1)} %get-tuple-element.62), channel_id=1, source_target_pairs={{0,20},{4,16},{8,28},{12,24},{16,4},{20,0},{24,12},{28,8},{1,21},{... | collective-permute-start | bytes 196616 | tf_op jit(solution)/shard_map/ppermute | solution.py:251
  65.2 1.5 %collective-permute-start.22 = (bf16[128,256]{1,0:T(8,128)(2,1)S(1)}, bf16[128,256]{1,0:T(8,128)(2,1)S(1)}, u32[]{:S(2)}, u32[]{:S(2)}) collective-permute-start(bf16[128,256]{1,0:T(8,128)(2,1)S(1)} %get-tuple-element.63), channel_id=1, source_target_pairs={{0,24},{4,28},{8,16},{12,20},{16,8},{20,12},{24,0},{28,4},{1,25},{... | collective-permute-start | bytes 196616 | tf_op jit(solution)/shard_map/ppermute | solution.py:251
  67.3 4.3 %collective-permute-start.23 = (bf16[128,256]{1,0:T(8,128)(2,1)S(1)}, bf16[128,256]{1,0:T(8,128)(2,1)S(1)}, u32[]{:S(2)}, u32[]{:S(2)}) collective-permute-start(bf16[128,256]{1,0:T(8,128)(2,1)S(1)} %get-tuple-element.64), channel_id=1, source_target_pairs={{0,28},{4,24},{8,20},{12,16},{16,12},{20,8},{24,4},{28,0},{1,29},{... | collective-permute-start | bytes 196616 | tf_op jit(solution)/shard_map/ppermute | solution.py:251
  71.8 2.6 %collective-permute-done.23.refs_7_ = bf16[128,256]{1,0:T(8,128)(2,1)S(1)} collective-permute-done((bf16[128,256]{1,0:T(8,128)(2,1)S(1)}, bf16[128,256]{1,0:T(8,128)(2,1)S(1)}, u32[]{:S(2)}, u32[]{:S(2)}) %collective-permute-start.23) | collective-permute-done | bytes 65568 | tf_op jit(solution)/shard_map/ppermute | solution.py:251
  74.4 1.4 %place.1 = (f32[256,128]{1,0:T(8,128)}, f32[256,128]{1,0:T(8,128)}) custom-call(s32[1]{0:T(128)} %bitcast.1.me_ref, s32[8,16]{1,0:T(8,128)S(1)} %get-tuple-element.44.reads_ref, bf16[128,256]{1,0:T(8,128)(2,1)S(1)} %get-tuple-element.57.refs_0_, bf16[128,256]{1,0:T(8,128)(2,1)S(1)} %collective-permute-done.17.refs_1_, ...), custom_call_target="tpu_custom_call" | custom-call | bytes 1048576 | tf_op jit(solution)/shard_map/place/pallas_call | solution.py:406
  (42 shorter events, 9.7 us)
Async XLA Ops:
  0.6 13.8 %collective-permute-start.1 = (bf16[256,896]{1,0:T(8,128)(2,1)}, bf16[256,896]{1,0:T(8,128)(2,1)S(1)}, u32[]{:S(2)}, u32[]{:S(2)}) collective-permute-start(bf16[256,896]{1,0:T(8,128)(2,1)} %own_hbm.1), channel_id=1, source_target_pairs={{0,2},{1,3},{2,0},{3,1},{4,6},{5,7},{6,4},{7,5},{8,10},{9,11},{10,... | collective-permute-start | bytes 1376264 | tf_op jit(solution)/shard_map/ppermute | solution.py:251
  3.7 26.0 %collective-permute-start = (bf16[256,896]{1,0:T(8,128)(2,1)}, bf16[256,896]{1,0:T(8,128)(2,1)S(1)}, u32[]{:S(2)}, u32[]{:S(2)}) collective-permute-start(bf16[256,896]{1,0:T(8,128)(2,1)} %own_hbm.1), channel_id=1, source_target_pairs={{0,1},{1,0},{2,3},{3,2},{4,5},{5,4},{6,7},{7,6},{8,9},{9,8},{10,11... | collective-permute-start | bytes 1376264 | tf_op jit(solution)/shard_map/ppermute | solution.py:251
  14.4 20.1 %collective-permute-start.2 = (bf16[256,896]{1,0:T(8,128)(2,1)S(1)}, bf16[256,896]{1,0:T(8,128)(2,1)S(1)}, u32[]{:S(2)}, u32[]{:S(2)}) collective-permute-start(bf16[256,896]{1,0:T(8,128)(2,1)S(1)} %collective-permute-done.1.refs_0_), channel_id=1, source_target_pairs={{0,1},{1,0},{2,3},{3,2},{4,5},{5,4},{6,7},{7,6},{8,9},{9,8},{10,11... | collective-permute-start | bytes 1376264 | tf_op jit(solution)/shard_map/ppermute | solution.py:251
  14.4 7.4 %collective-permute-start.6 = (bf16[256,128]{1,0:T(8,128)(2,1)}, bf16[256,128]{1,0:T(8,128)(2,1)S(1)}, u32[]{:S(2)}, u32[]{:S(2)}) collective-permute-start(bf16[256,128]{1,0:T(8,128)(2,1)} %keys_hbm.1), channel_id=1, source_target_pairs={{0,16},{4,20},{8,24},{12,28},{16,0},{20,4},{24,8},{28,12},{1,17},{... | collective-permute-start | bytes 196616 | tf_op jit(solution)/shard_map/ppermute | solution.py:251
  17.2 7.2 %collective-permute-start.7 = (bf16[256,128]{1,0:T(8,128)(2,1)}, bf16[256,128]{1,0:T(8,128)(2,1)S(1)}, u32[]{:S(2)}, u32[]{:S(2)}) collective-permute-start(bf16[256,128]{1,0:T(8,128)(2,1)} %values_hbm.1), channel_id=1, source_target_pairs={{0,16},{4,20},{8,24},{12,28},{16,0},{20,4},{24,8},{28,12},{1,17},{... | collective-permute-start | bytes 196616 | tf_op jit(solution)/shard_map/ppermute | solution.py:251
  18.3 8.5 %collective-permute-start.3 = (bf16[128,256]{1,0:T(8,128)(2,1)S(1)}, bf16[128,256]{1,0:T(8,128)(2,1)S(1)}, u32[]{:S(2)}, u32[]{:S(2)}) collective-permute-start(bf16[128,256]{1,0:T(8,128)(2,1)S(1)} %get-tuple-element.41), channel_id=1, source_target_pairs={{0,4},{4,0},{8,12},{12,8},{16,20},{20,16},{24,28},{28,24},{1,5},{5... | collective-permute-start | bytes 196616 | tf_op jit(solution)/shard_map/ppermute | solution.py:251
  21.8 6.2 %collective-permute-start.4 = (bf16[128,256]{1,0:T(8,128)(2,1)S(1)}, bf16[128,256]{1,0:T(8,128)(2,1)S(1)}, u32[]{:S(2)}, u32[]{:S(2)}) collective-permute-start(bf16[128,256]{1,0:T(8,128)(2,1)S(1)} %get-tuple-element.42), channel_id=1, source_target_pairs={{0,8},{4,12},{8,0},{12,4},{16,24},{20,28},{24,16},{28,20},{1,9},{5... | collective-permute-start | bytes 196616 | tf_op jit(solution)/shard_map/ppermute | solution.py:251
  24.4 8.5 %collective-permute-start.5 = (bf16[128,256]{1,0:T(8,128)(2,1)S(1)}, bf16[128,256]{1,0:T(8,128)(2,1)S(1)}, u32[]{:S(2)}, u32[]{:S(2)}) collective-permute-start(bf16[128,256]{1,0:T(8,128)(2,1)S(1)} %get-tuple-element.43), channel_id=1, source_target_pairs={{0,12},{4,8},{8,4},{12,0},{16,28},{20,24},{24,20},{28,16},{1,13},{... | collective-permute-start | bytes 196616 | tf_op jit(solution)/shard_map/ppermute | solution.py:251
  26.9 7.7 %collective-permute-start.10 = (bf16[128,256]{1,0:T(8,128)(2,1)S(1)}, bf16[128,256]{1,0:T(8,128)(2,1)S(1)}, u32[]{:S(2)}, u32[]{:S(2)}) collective-permute-start(bf16[128,256]{1,0:T(8,128)(2,1)S(1)} %get-tuple-element.48), channel_id=1, source_target_pairs={{0,12},{4,8},{8,4},{12,0},{16,28},{20,24},{24,20},{28,16},{1,13},{... | collective-permute-start | bytes 196616 | tf_op jit(solution)/shard_map/ppermute | solution.py:251
  28.1 6.4 %collective-permute-start.8 = (bf16[128,256]{1,0:T(8,128)(2,1)S(1)}, bf16[128,256]{1,0:T(8,128)(2,1)S(1)}, u32[]{:S(2)}, u32[]{:S(2)}) collective-permute-start(bf16[128,256]{1,0:T(8,128)(2,1)S(1)} %get-tuple-element.46), channel_id=1, source_target_pairs={{0,4},{4,0},{8,12},{12,8},{16,20},{20,16},{24,28},{28,24},{1,5},{5... | collective-permute-start | bytes 196616 | tf_op jit(solution)/shard_map/ppermute | solution.py:251
  29.6 4.9 %collective-permute-start.9 = (bf16[128,256]{1,0:T(8,128)(2,1)S(1)}, bf16[128,256]{1,0:T(8,128)(2,1)S(1)}, u32[]{:S(2)}, u32[]{:S(2)}) collective-permute-start(bf16[128,256]{1,0:T(8,128)(2,1)S(1)} %get-tuple-element.47), channel_id=1, source_target_pairs={{0,8},{4,12},{8,0},{12,4},{16,24},{20,28},{24,16},{28,20},{1,9},{5... | collective-permute-start | bytes 196616 | tf_op jit(solution)/shard_map/ppermute | solution.py:251
  32.9 11.7 %collective-permute-start.15 = (bf16[256,896]{1,0:T(8,128)(2,1)}, bf16[256,896]{1,0:T(8,128)(2,1)S(1)}, u32[]{:S(2)}, u32[]{:S(2)}) collective-permute-start(bf16[256,896]{1,0:T(8,128)(2,1)} %refs_0_.1), channel_id=1, source_target_pairs={{0,2},{1,3},{2,0},{3,1},{4,6},{5,7},{6,4},{7,5},{8,10},{9,11},{10,... | collective-permute-start | bytes 1376264 | tf_op jit(solution)/shard_map/ppermute | solution.py:251
  34.5 10.1 %collective-permute-start.14 = (bf16[256,896]{1,0:T(8,128)(2,1)}, bf16[256,896]{1,0:T(8,128)(2,1)S(1)}, u32[]{:S(2)}, u32[]{:S(2)}) collective-permute-start(bf16[256,896]{1,0:T(8,128)(2,1)} %refs_0_.1), channel_id=1, source_target_pairs={{0,1},{1,0},{2,3},{3,2},{4,5},{5,4},{6,7},{7,6},{8,9},{9,8},{10,11... | collective-permute-start | bytes 1376264 | tf_op jit(solution)/shard_map/ppermute | solution.py:251
  40.2 7.8 %collective-permute-start.12 = (bf16[256,896]{1,0:T(8,128)(2,1)S(1)}, bf16[256,896]{1,0:T(8,128)(2,1)S(1)}, u32[]{:S(2)}, u32[]{:S(2)}) collective-permute-start(bf16[256,896]{1,0:T(8,128)(2,1)S(1)} %get-tuple-element.53), channel_id=1, source_target_pairs={{0,1},{1,0},{2,3},{3,2},{4,5},{5,4},{6,7},{7,6},{8,9},{9,8},{10,11... | collective-permute-start | bytes 1376264 | tf_op jit(solution)/shard_map/ppermute | solution.py:251
  44.6 5.2 %collective-permute-start.16 = (bf16[256,896]{1,0:T(8,128)(2,1)S(1)}, bf16[256,896]{1,0:T(8,128)(2,1)S(1)}, u32[]{:S(2)}, u32[]{:S(2)}) collective-permute-start(bf16[256,896]{1,0:T(8,128)(2,1)S(1)} %collective-permute-done.15.refs_2_), channel_id=1, source_target_pairs={{0,1},{1,0},{2,3},{3,2},{4,5},{5,4},{6,7},{7,6},{8,9},{9,8},{10,11... | collective-permute-start | bytes 1376264 | tf_op jit(solution)/shard_map/ppermute | solution.py:251
  47.5 28.3 %collective-permute-start.11 = (bf16[256,896]{1,0:T(8,128)(2,1)S(1)}, bf16[256,896]{1,0:T(8,128)(2,1)S(1)}, u32[]{:S(2)}, u32[]{:S(2)}) collective-permute-start(bf16[256,896]{1,0:T(8,128)(2,1)S(1)} %get-tuple-element.51), channel_id=1, source_target_pairs={{0,1},{1,0},{2,3},{3,2},{4,5},{5,4},{6,7},{7,6},{8,9},{9,8},{10,11... | collective-permute-start | bytes 1376264 | tf_op jit(solution)/shard_map/ppermute | solution.py:251
  48.2 27.6 %collective-permute-start.13 = (bf16[256,896]{1,0:T(8,128)(2,1)S(1)}, bf16[256,896]{1,0:T(8,128)(2,1)S(1)}, u32[]{:S(2)}, u32[]{:S(2)}) collective-permute-start(bf16[256,896]{1,0:T(8,128)(2,1)S(1)} %add_convert_fusion.1), channel_id=1, source_target_pairs={{0,2},{1,3},{2,0},{3,1},{4,6},{5,7},{6,4},{7,5},{8,10},{9,11},{10,... | collective-permute-start | bytes 1376264 | tf_op jit(solution)/shard_map/ppermute | solution.py:251
  55.5 4.3 %collective-permute-start.17 = (bf16[128,256]{1,0:T(8,128)(2,1)S(1)}, bf16[128,256]{1,0:T(8,128)(2,1)S(1)}, u32[]{:S(2)}, u32[]{:S(2)}) collective-permute-start(bf16[128,256]{1,0:T(8,128)(2,1)S(1)} %get-tuple-element.58), channel_id=1, source_target_pairs={{0,4},{4,0},{8,12},{12,8},{16,20},{20,16},{24,28},{28,24},{1,5},{5... | collective-permute-start | bytes 196616 | tf_op jit(solution)/shard_map/ppermute | solution.py:251
  56.1 7.0 %collective-permute-start.18 = (bf16[128,256]{1,0:T(8,128)(2,1)S(1)}, bf16[128,256]{1,0:T(8,128)(2,1)S(1)}, u32[]{:S(2)}, u32[]{:S(2)}) collective-permute-start(bf16[128,256]{1,0:T(8,128)(2,1)S(1)} %get-tuple-element.59), channel_id=1, source_target_pairs={{0,8},{4,12},{8,0},{12,4},{16,24},{20,28},{24,16},{28,20},{1,9},{5... | collective-permute-start | bytes 196616 | tf_op jit(solution)/shard_map/ppermute | solution.py:251
  57.1 8.1 %collective-permute-start.19 = (bf16[128,256]{1,0:T(8,128)(2,1)S(1)}, bf16[128,256]{1,0:T(8,128)(2,1)S(1)}, u32[]{:S(2)}, u32[]{:S(2)}) collective-permute-start(bf16[128,256]{1,0:T(8,128)(2,1)S(1)} %get-tuple-element.60), channel_id=1, source_target_pairs={{0,12},{4,8},{8,4},{12,0},{16,28},{20,24},{24,20},{28,16},{1,13},{... | collective-permute-start | bytes 196616 | tf_op jit(solution)/shard_map/ppermute | solution.py:251
  59.9 7.4 %collective-permute-start.20 = (bf16[128,256]{1,0:T(8,128)(2,1)S(1)}, bf16[128,256]{1,0:T(8,128)(2,1)S(1)}, u32[]{:S(2)}, u32[]{:S(2)}) collective-permute-start(bf16[128,256]{1,0:T(8,128)(2,1)S(1)} %get-tuple-element.61), channel_id=1, source_target_pairs={{0,16},{4,20},{8,24},{12,28},{16,0},{20,4},{24,8},{28,12},{1,17},{... | collective-permute-start | bytes 196616 | tf_op jit(solution)/shard_map/ppermute | solution.py:251
  63.1 8.6 %collective-permute-start.21 = (bf16[128,256]{1,0:T(8,128)(2,1)S(1)}, bf16[128,256]{1,0:T(8,128)(2,1)S(1)}, u32[]{:S(2)}, u32[]{:S(2)}) collective-permute-start(bf16[128,256]{1,0:T(8,128)(2,1)S(1)} %get-tuple-element.62), channel_id=1, source_target_pairs={{0,20},{4,16},{8,28},{12,24},{16,4},{20,0},{24,12},{28,8},{1,21},{... | collective-permute-start | bytes 196616 | tf_op jit(solution)/shard_map/ppermute | solution.py:251
  65.2 6.6 %collective-permute-start.22 = (bf16[128,256]{1,0:T(8,128)(2,1)S(1)}, bf16[128,256]{1,0:T(8,128)(2,1)S(1)}, u32[]{:S(2)}, u32[]{:S(2)}) collective-permute-start(bf16[128,256]{1,0:T(8,128)(2,1)S(1)} %get-tuple-element.63), channel_id=1, source_target_pairs={{0,24},{4,28},{8,16},{12,20},{16,8},{20,12},{24,0},{28,4},{1,25},{... | collective-permute-start | bytes 196616 | tf_op jit(solution)/shard_map/ppermute | solution.py:251
  67.3 7.1 %collective-permute-start.23 = (bf16[128,256]{1,0:T(8,128)(2,1)S(1)}, bf16[128,256]{1,0:T(8,128)(2,1)S(1)}, u32[]{:S(2)}, u32[]{:S(2)}) collective-permute-start(bf16[128,256]{1,0:T(8,128)(2,1)S(1)} %get-tuple-element.64), channel_id=1, source_target_pairs={{0,28},{4,24},{8,20},{12,16},{16,12},{20,8},{24,4},{28,0},{1,29},{... | collective-permute-start | bytes 196616 | tf_op jit(solution)/shard_map/ppermute | solution.py:251
  (3 other events, 18.6 us)

commit v5 on v4

--- a/solution.py
+++ b/solution.py
@@ -314,24 +314,24 @@
     n_pre = len(prefix)
 
     part = jax.ShapeDtypeStruct((length, HD), F32)
-    n_rest = n_tp - 2
+    n_rest = n_tp - 3
     weight = jax.ShapeDtypeStruct((n_rest, width, HD), BF16)
     part_k, part_v, q, rest_k, rest_v = pl.pallas_call(
-        functools.partial(kv_kernel, (0, 1), tuple(range(2, n_tp))),
+        functools.partial(kv_kernel, (1, 0, 2), tuple(range(3, n_tp))),
         out_shape=[part, part, jax.ShapeDtypeStruct(queries.shape, BF16), weight, weight],
-        in_specs=[SMEM, HBM, VMEM] + [HBM] * 3,
+        in_specs=[SMEM, HBM, VMEM, VMEM] + [HBM] * 3,
         out_specs=[VMEM] * 5,
         scratch_shapes=[
             pltpu.VMEM((length, width), BF16),
-            pltpu.VMEM((2, width, HD), BF16),
-            pltpu.VMEM((2, width, HD), BF16),
-            pltpu.SemaphoreType.DMA((2, 2)),
+            pltpu.VMEM((3, width, HD), BF16),
+            pltpu.VMEM((3, width, HD), BF16),
+            pltpu.SemaphoreType.DMA((2, 3)),
             pltpu.SemaphoreType.DMA((2 + 2 * n_rest,)),
         ],
         compiler_params=grant(8),
         cost_estimate=cost(4e8, 3e6),
         name="kv",
-    )(me_tp, hbm(hidden_states), near_hidden, hbm(key_weight), hbm(value_weight), hbm(queries))
+    )(me_tp, hbm(hidden_states), near_hidden, far_hidden, hbm(key_weight), hbm(value_weight), hbm(queries))
 
     ctx, exps, row, v_all = pl.pallas_call(
         functools.partial(forward_kernel, n_rest, n_pre, scaling),
@@ -352,7 +352,7 @@
         compiler_params=grant(20),
         cost_estimate=cost(5e9, 1e7, 3e6),
         name="forward",
-    )(rest_k, rest_v, far_hidden, last_hidden, q, part_k, part_v, *prefix)
+    )(rest_k, rest_v, last_hidden, q, part_k, part_v, *prefix)
 
     part_grad = pl.pallas_call(
         functools.partial(grad_kernel, (0, 1, 2)),

time: 77.4 us -> 79.4 us (1.026)
  waiting for transfers between devices: 21 us -> 22.3 us
    ppermute x24, waiting for transfers between devices: 21 us -> 22.3 us  [hop(): return lax.ppermute(x, axis, [(i, i ^ k) for i in range(n)])]
  transfers between devices with their start and end apart: 24 -> 24, of which waited for: 8 -> 8; matrix products, arithmetic and copies ran while one was open for 0% -> 0% of each run, Pallas kernels for 26% -> 25%
where the time goes in v5:
time: 79.4 us; the launch traced here: 78.2 us
  starting transfers between devices  34.4 us (43%)
  waiting for transfers between devices  22.3 us (28%)
  Pallas kernels  19.6 us (25%)
  other arithmetic  1.06 us (1%)
    ppermute x24, starting transfers between devices, hop(): return lax.ppermute(x, axis, [(i, i ^ k) for i in range(n)])  34.4 us
    ppermute x24, waiting for transfers between devices, hop(): return lax.ppermute(x, axis, [(i, i ^ k) for i in range(n)])  22.3 us
    pallas_call x1, Pallas kernels, local(): pl.pallas_call(functools.partial(backward_kernel, n_tp - 1, n_pre, scalin...  5.72 us
    pallas_call x1, Pallas kernels, local(): pl.pallas_call(functools.partial(forward_kernel, n_rest, n_pre, scaling),...  4.11 us
    pallas_call x1, Pallas kernels, local(): pl.pallas_call(functools.partial(kv_kernel, (1, 0, 2), tuple(range(3, n_t...  2.66 us
    pallas_call x2, Pallas kernels, project(): pl.pallas_call(functools.partial(project_kernel, order), out_shape=[jax.S...  2.49 us
    pallas_call x1, Pallas kernels, local(): pl.pallas_call(functools.partial(grad_kernel, (0, 1, 2)), out_shape=jax.S...  1.62 us
  transfers between devices with their start and end apart: 24, of which 8 were waited for; matrix products, arithmetic and copies ran while one was open for 0% of the time, Pallas kernels for 25%

profile of v5, /device:TPU:0, one launch (start us, length us, event | category | flops | bytes accessed | tf_op | source)
XLA Modules:
  0.0 78.2 jit_solution(9825027804224732715)
XLA Ops:
  0.6 3.1 %collective-permute-start.1 = (bf16[256,896]{1,0:T(8,128)(2,1)}, bf16[256,896]{1,0:T(8,128)(2,1)S(1)}, u32[]{:S(2)}, u32[]{:S(2)}) collective-permute-start(bf16[256,896]{1,0:T(8,128)(2,1)} %own_hbm.1), channel_id=1, source_target_pairs={{0,2},{1,3},{2,0},{3,1},{4,6},{5,7},{6,4},{7,5},{8,10},{9,11},{10,... | collective-permute-start | bytes 1376264 | tf_op jit(solution)/shard_map/ppermute | solution.py:251
  3.7 10.7 %collective-permute-done.1.refs_1_ = bf16[256,896]{1,0:T(8,128)(2,1)S(1)} collective-permute-done((bf16[256,896]{1,0:T(8,128)(2,1)}, bf16[256,896]{1,0:T(8,128)(2,1)S(1)}, u32[]{:S(2)}, u32[]{:S(2)}) %collective-permute-start.1) | collective-permute-done | bytes 458784 | tf_op jit(solution)/shard_map/ppermute | solution.py:251
  14.4 2.8 %collective-permute-start.6 = (bf16[256,128]{1,0:T(8,128)(2,1)}, bf16[256,128]{1,0:T(8,128)(2,1)S(1)}, u32[]{:S(2)}, u32[]{:S(2)}) collective-permute-start(bf16[256,128]{1,0:T(8,128)(2,1)} %keys_hbm.1), channel_id=1, source_target_pairs={{0,16},{4,20},{8,24},{12,28},{16,0},{20,4},{24,8},{28,12},{1,17},{... | collective-permute-start | bytes 196616 | tf_op jit(solution)/shard_map/ppermute | solution.py:251
  18.3 1.8 %collective-permute-start.3 = (bf16[128,256]{1,0:T(8,128)(2,1)S(1)}, bf16[128,256]{1,0:T(8,128)(2,1)S(1)}, u32[]{:S(2)}, u32[]{:S(2)}) collective-permute-start(bf16[128,256]{1,0:T(8,128)(2,1)S(1)} %get-tuple-element.41), channel_id=1, source_target_pairs={{0,4},{4,0},{8,12},{12,8},{16,20},{20,16},{24,28},{28,24},{1,5},{5... | collective-permute-start | bytes 196616 | tf_op jit(solution)/shard_map/ppermute | solution.py:251
  20.1 1.7 %collective-permute-done.6.keys_ref = bf16[256,128]{1,0:T(8,128)(2,1)S(1)} collective-permute-done((bf16[256,128]{1,0:T(8,128)(2,1)}, bf16[256,128]{1,0:T(8,128)(2,1)S(1)}, u32[]{:S(2)}, u32[]{:S(2)}) %collective-permute-start.6) | collective-permute-done | bytes 65568 | tf_op jit(solution)/shard_map/ppermute | solution.py:251
  21.8 2.0 %collective-permute-start.4 = (bf16[128,256]{1,0:T(8,128)(2,1)S(1)}, bf16[128,256]{1,0:T(8,128)(2,1)S(1)}, u32[]{:S(2)}, u32[]{:S(2)}) collective-permute-start(bf16[128,256]{1,0:T(8,128)(2,1)S(1)} %get-tuple-element.42), channel_id=1, source_target_pairs={{0,8},{4,12},{8,0},{12,4},{16,24},{20,28},{24,16},{28,20},{1,9},{5... | collective-permute-start | bytes 196616 | tf_op jit(solution)/shard_map/ppermute | solution.py:251
  24.4 1.8 %collective-permute-start.5 = (bf16[128,256]{1,0:T(8,128)(2,1)S(1)}, bf16[128,256]{1,0:T(8,128)(2,1)S(1)}, u32[]{:S(2)}, u32[]{:S(2)}) collective-permute-start(bf16[128,256]{1,0:T(8,128)(2,1)S(1)} %get-tuple-element.43), channel_id=1, source_target_pairs={{0,12},{4,8},{8,4},{12,0},{16,28},{20,24},{24,20},{28,16},{1,13},{... | collective-permute-start | bytes 196616 | tf_op jit(solution)/shard_map/ppermute | solution.py:251
  28.7 1.8 %collective-permute-start.10 = (bf16[128,256]{1,0:T(8,128)(2,1)S(1)}, bf16[128,256]{1,0:T(8,128)(2,1)S(1)}, u32[]{:S(2)}, u32[]{:S(2)}) collective-permute-start(bf16[128,256]{1,0:T(8,128)(2,1)S(1)} %get-tuple-element.48), channel_id=1, source_target_pairs={{0,12},{4,8},{8,4},{12,0},{16,28},{20,24},{24,20},{28,16},{1,13},{... | collective-permute-start | bytes 196616 | tf_op jit(solution)/shard_map/ppermute | solution.py:251
  30.4 2.7 %kv.1 = (f32[256,128]{1,0:T(8,128)S(1)}, f32[256,128]{1,0:T(8,128)S(1)}, bf16[256,896]{1,0:T(8,128)(2,1)S(1)}, bf16[1,896,128]{2,1,0:T(8,128)(2,1)S(1)}, bf16[1,896,128]{2,1,0:T(8,128)(2,1)S(1)}) custom-call(s32[1]{0:T(128)} %bitcast.me_ref, bf16[256,896]{1,0:T(8,128)(2,1)} %own_hbm.1, bf16[256,896]{1,0:T(8,128)(2,1)S(1)} %collective-permute-done.refs_0_, ...), custom_call_target="tpu_custom_call" | custom-call | flops 400000000 | bytes 3000000 | tf_op jit(solution)/shard_map/kv/pallas_call | solution.py:319
  33.2 1.6 %collective-permute-start.15 = (bf16[256,896]{1,0:T(8,128)(2,1)}, bf16[256,896]{1,0:T(8,128)(2,1)S(1)}, u32[]{:S(2)}, u32[]{:S(2)}) collective-permute-start(bf16[256,896]{1,0:T(8,128)(2,1)} %refs_0_.1), channel_id=1, source_target_pairs={{0,2},{1,3},{2,0},{3,1},{4,6},{5,7},{6,4},{7,5},{8,10},{9,11},{10,... | collective-permute-start | bytes 1376264 | tf_op jit(solution)/shard_map/ppermute | solution.py:251
  34.8 4.1 %forward.1 = (bf16[256,896]{1,0:T(8,128)(2,1)S(1)}, bf16[1280,1792]{1,0:T(8,128)(2,1)S(1)}, f32[8,256]{1,0:T(8,128)S(1)}, bf16[1280,128]{1,0:T(8,128)(2,1)S(1)}) custom-call(bf16[1,896,128]{2,1,0:T(8,128)(2,1)S(1)} %get-tuple-element.35.wk_ref, bf16[1,896,128]{2,1,0:T(8,128)(2,1)S(1)} %get-tuple-element.36.wv_ref, ...), custom_call_target="tpu_custom_call" | custom-call | flops 5000000000 | bytes 10000000 | tf_op jit(solution)/shard_map/forward/pallas_call | solution.py:336
  40.4 5.9 %collective-permute-done.15.refs_2_ = bf16[256,896]{1,0:T(8,128)(2,1)S(1)} collective-permute-done((bf16[256,896]{1,0:T(8,128)(2,1)}, bf16[256,896]{1,0:T(8,128)(2,1)S(1)}, u32[]{:S(2)}, u32[]{:S(2)}) %collective-permute-start.15) | collective-permute-done | bytes 458784 | tf_op jit(solution)/shard_map/ppermute | solution.py:251
  46.3 1.6 %grad.1.part_ref = f32[896,256]{1,0:T(8,128)S(1)} custom-call(s32[1]{0:T(128)} %bitcast.me_ref, bf16[896,3584]{1,0:T(8,128)(2,1)S(1)} %bitcast.3, bf16[256,896]{1,0:T(8,128)(2,1)S(1)} %copy-done, bf16[256,896]{1,0:T(8,128)(2,1)S(1)} %collective-permute-done.14.refs_1_, bf16[256,896]{1,0:T(8,128)(2,1)S(1)} %collective-permute-done.15.refs_2_), custom_call_target="tpu_custom_call" | custom-call | flops 1500000000 | bytes 8000000 | tf_op jit(solution)/shard_map/grad/pallas_call | solution.py:357
  48.0 1.3 %shard_map.112 = (bf16[256,896]{1,0:T(8,128)(2,1)S(1)}, bf16[256,896]{1,0:T(8,128)(2,1)S(1)}) custom-call(s32[1]{0:T(128)} %bitcast.me_ref, bf16[256,896]{1,0:T(8,128)(2,1)S(1)} %get-tuple-element.49.ctx_ref, bf16[896,3584]{1,0:T(8,128)(2,1)S(1)} %bitcast.3), custom_call_target="tpu_custom_call" | custom-call | flops 1000000000 | bytes 4000000 | tf_op jit(solution)/shard_map/pallas_call | solution.py:368
  49.9 1.6 %collective-permute-start.13 = (bf16[256,896]{1,0:T(8,128)(2,1)S(1)}, bf16[256,896]{1,0:T(8,128)(2,1)S(1)}, u32[]{:S(2)}, u32[]{:S(2)}) collective-permute-start(bf16[256,896]{1,0:T(8,128)(2,1)S(1)} %add_convert_fusion.1), channel_id=1, source_target_pairs={{0,2},{1,3},{2,0},{3,1},{4,6},{5,7},{6,4},{7,5},{8,10},{9,11},{10,... | collective-permute-start | bytes 1376264 | tf_op jit(solution)/shard_map/ppermute | solution.py:251
  51.5 5.7 %backward.1 = (bf16[128,256]{1,0:T(8,128)(2,1)S(1)}, bf16[128,256]{1,0:T(8,128)(2,1)S(1)}, bf16[128,256]{1,0:T(8,128)(2,1)S(1)}, bf16[128,256]{1,0:T(8,128)(2,1)...) custom-call(s32[1]{0:T(128)} %bitcast.me_ref, ...), custom_call_target="tpu_custom_call" | custom-call | flops 7000000000 | bytes 10000000 | tf_op jit(solution)/shard_map/backward/pallas_call | solution.py:386
  57.8 1.2 %collective-permute-start.18 = (bf16[128,256]{1,0:T(8,128)(2,1)S(1)}, bf16[128,256]{1,0:T(8,128)(2,1)S(1)}, u32[]{:S(2)}, u32[]{:S(2)}) collective-permute-start(bf16[128,256]{1,0:T(8,128)(2,1)S(1)} %get-tuple-element.59), channel_id=1, source_target_pairs={{0,8},{4,12},{8,0},{12,4},{16,24},{20,28},{24,16},{28,20},{1,9},{5... | collective-permute-start | bytes 196616 | tf_op jit(solution)/shard_map/ppermute | solution.py:251
  59.1 1.7 %collective-permute-start.19 = (bf16[128,256]{1,0:T(8,128)(2,1)S(1)}, bf16[128,256]{1,0:T(8,128)(2,1)S(1)}, u32[]{:S(2)}, u32[]{:S(2)}) collective-permute-start(bf16[128,256]{1,0:T(8,128)(2,1)S(1)} %get-tuple-element.60), channel_id=1, source_target_pairs={{0,12},{4,8},{8,4},{12,0},{16,28},{20,24},{24,20},{28,16},{1,13},{... | collective-permute-start | bytes 196616 | tf_op jit(solution)/shard_map/ppermute | solution.py:251
  61.6 3.3 %collective-permute-start.20 = (bf16[128,256]{1,0:T(8,128)(2,1)S(1)}, bf16[128,256]{1,0:T(8,128)(2,1)S(1)}, u32[]{:S(2)}, u32[]{:S(2)}) collective-permute-start(bf16[128,256]{1,0:T(8,128)(2,1)S(1)} %get-tuple-element.61), channel_id=1, source_target_pairs={{0,16},{4,20},{8,24},{12,28},{16,0},{20,4},{24,8},{28,12},{1,17},{... | collective-permute-start | bytes 196616 | tf_op jit(solution)/shard_map/ppermute | solution.py:251
  64.8 2.1 %collective-permute-start.21 = (bf16[128,256]{1,0:T(8,128)(2,1)S(1)}, bf16[128,256]{1,0:T(8,128)(2,1)S(1)}, u32[]{:S(2)}, u32[]{:S(2)}) collective-permute-start(bf16[128,256]{1,0:T(8,128)(2,1)S(1)} %get-tuple-element.62), channel_id=1, source_target_pairs={{0,20},{4,16},{8,28},{12,24},{16,4},{20,0},{24,12},{28,8},{1,21},{... | collective-permute-start | bytes 196616 | tf_op jit(solution)/shard_map/ppermute | solution.py:251
  66.9 1.5 %collective-permute-start.22 = (bf16[128,256]{1,0:T(8,128)(2,1)S(1)}, bf16[128,256]{1,0:T(8,128)(2,1)S(1)}, u32[]{:S(2)}, u32[]{:S(2)}) collective-permute-start(bf16[128,256]{1,0:T(8,128)(2,1)S(1)} %get-tuple-element.63), channel_id=1, source_target_pairs={{0,24},{4,28},{8,16},{12,20},{16,8},{20,12},{24,0},{28,4},{1,25},{... | collective-permute-start | bytes 196616 | tf_op jit(solution)/shard_map/ppermute | solution.py:251
  68.7 4.9 %collective-permute-start.23 = (bf16[128,256]{1,0:T(8,128)(2,1)S(1)}, bf16[128,256]{1,0:T(8,128)(2,1)S(1)}, u32[]{:S(2)}, u32[]{:S(2)}) collective-permute-start(bf16[128,256]{1,0:T(8,128)(2,1)S(1)} %get-tuple-element.64), channel_id=1, source_target_pairs={{0,28},{4,24},{8,20},{12,16},{16,12},{20,8},{24,4},{28,0},{1,29},{... | collective-permute-start | bytes 196616 | tf_op jit(solution)/shard_map/ppermute | solution.py:251
  73.7 2.1 %collective-permute-done.23.refs_7_ = bf16[128,256]{1,0:T(8,128)(2,1)S(1)} collective-permute-done((bf16[128,256]{1,0:T(8,128)(2,1)S(1)}, bf16[128,256]{1,0:T(8,128)(2,1)S(1)}, u32[]{:S(2)}, u32[]{:S(2)}) %collective-permute-start.23) | collective-permute-done | bytes 65568 | tf_op jit(solution)/shard_map/ppermute | solution.py:251
  75.8 1.4 %place.1 = (f32[256,128]{1,0:T(8,128)}, f32[256,128]{1,0:T(8,128)}) custom-call(s32[1]{0:T(128)} %bitcast.1.me_ref, s32[8,16]{1,0:T(8,128)S(1)} %get-tuple-element.44.reads_ref, bf16[128,256]{1,0:T(8,128)(2,1)S(1)} %get-tuple-element.57.refs_0_, bf16[128,256]{1,0:T(8,128)(2,1)S(1)} %collective-permute-done.17.refs_1_, ...), custom_call_target="tpu_custom_call" | custom-call | bytes 1048576 | tf_op jit(solution)/shard_map/place/pallas_call | solution.py:406
  (42 shorter events, 9.1 us)
Async XLA Ops:
  0.6 13.8 %collective-permute-start.1 = (bf16[256,896]{1,0:T(8,128)(2,1)}, bf16[256,896]{1,0:T(8,128)(2,1)S(1)}, u32[]{:S(2)}, u32[]{:S(2)}) collective-permute-start(bf16[256,896]{1,0:T(8,128)(2,1)} %own_hbm.1), channel_id=1, source_target_pairs={{0,2},{1,3},{2,0},{3,1},{4,6},{5,7},{6,4},{7,5},{8,10},{9,11},{10,... | collective-permute-start | bytes 1376264 | tf_op jit(solution)/shard_map/ppermute | solution.py:251
  3.7 25.0 %collective-permute-start = (bf16[256,896]{1,0:T(8,128)(2,1)}, bf16[256,896]{1,0:T(8,128)(2,1)S(1)}, u32[]{:S(2)}, u32[]{:S(2)}) collective-permute-start(bf16[256,896]{1,0:T(8,128)(2,1)} %own_hbm.1), channel_id=1, source_target_pairs={{0,1},{1,0},{2,3},{3,2},{4,5},{5,4},{6,7},{7,6},{8,9},{9,8},{10,11... | collective-permute-start | bytes 1376264 | tf_op jit(solution)/shard_map/ppermute | solution.py:251
  14.4 20.4 %collective-permute-start.2 = (bf16[256,896]{1,0:T(8,128)(2,1)S(1)}, bf16[256,896]{1,0:T(8,128)(2,1)S(1)}, u32[]{:S(2)}, u32[]{:S(2)}) collective-permute-start(bf16[256,896]{1,0:T(8,128)(2,1)S(1)} %collective-permute-done.1.refs_1_), channel_id=1, source_target_pairs={{0,1},{1,0},{2,3},{3,2},{4,5},{5,4},{6,7},{7,6},{8,9},{9,8},{10,11... | collective-permute-start | bytes 1376264 | tf_op jit(solution)/shard_map/ppermute | solution.py:251
  14.4 7.4 %collective-permute-start.6 = (bf16[256,128]{1,0:T(8,128)(2,1)}, bf16[256,128]{1,0:T(8,128)(2,1)S(1)}, u32[]{:S(2)}, u32[]{:S(2)}) collective-permute-start(bf16[256,128]{1,0:T(8,128)(2,1)} %keys_hbm.1), channel_id=1, source_target_pairs={{0,16},{4,20},{8,24},{12,28},{16,0},{20,4},{24,8},{28,12},{1,17},{... | collective-permute-start | bytes 196616 | tf_op jit(solution)/shard_map/ppermute | solution.py:251
  17.2 7.2 %collective-permute-start.7 = (bf16[256,128]{1,0:T(8,128)(2,1)}, bf16[256,128]{1,0:T(8,128)(2,1)S(1)}, u32[]{:S(2)}, u32[]{:S(2)}) collective-permute-start(bf16[256,128]{1,0:T(8,128)(2,1)} %values_hbm.1), channel_id=1, source_target_pairs={{0,16},{4,20},{8,24},{12,28},{16,0},{20,4},{24,8},{28,12},{1,17},{... | collective-permute-start | bytes 196616 | tf_op jit(solution)/shard_map/ppermute | solution.py:251
  18.3 8.5 %collective-permute-start.3 = (bf16[128,256]{1,0:T(8,128)(2,1)S(1)}, bf16[128,256]{1,0:T(8,128)(2,1)S(1)}, u32[]{:S(2)}, u32[]{:S(2)}) collective-permute-start(bf16[128,256]{1,0:T(8,128)(2,1)S(1)} %get-tuple-element.41), channel_id=1, source_target_pairs={{0,4},{4,0},{8,12},{12,8},{16,20},{20,16},{24,28},{28,24},{1,5},{5... | collective-permute-start | bytes 196616 | tf_op jit(solution)/shard_map/ppermute | solution.py:251
  21.8 5.6 %collective-permute-start.4 = (bf16[128,256]{1,0:T(8,128)(2,1)S(1)}, bf16[128,256]{1,0:T(8,128)(2,1)S(1)}, u32[]{:S(2)}, u32[]{:S(2)}) collective-permute-start(bf16[128,256]{1,0:T(8,128)(2,1)S(1)} %get-tuple-element.42), channel_id=1, source_target_pairs={{0,8},{4,12},{8,0},{12,4},{16,24},{20,28},{24,16},{28,20},{1,9},{5... | collective-permute-start | bytes 196616 | tf_op jit(solution)/shard_map/ppermute | solution.py:251
  24.4 8.7 %collective-permute-start.5 = (bf16[128,256]{1,0:T(8,128)(2,1)S(1)}, bf16[128,256]{1,0:T(8,128)(2,1)S(1)}, u32[]{:S(2)}, u32[]{:S(2)}) collective-permute-start(bf16[128,256]{1,0:T(8,128)(2,1)S(1)} %get-tuple-element.43), channel_id=1, source_target_pairs={{0,12},{4,8},{8,4},{12,0},{16,28},{20,24},{24,20},{28,16},{1,13},{... | collective-permute-start | bytes 196616 | tf_op jit(solution)/shard_map/ppermute | solution.py:251
  26.9 6.3 %collective-permute-start.8 = (bf16[128,256]{1,0:T(8,128)(2,1)S(1)}, bf16[128,256]{1,0:T(8,128)(2,1)S(1)}, u32[]{:S(2)}, u32[]{:S(2)}) collective-permute-start(bf16[128,256]{1,0:T(8,128)(2,1)S(1)} %get-tuple-element.46), channel_id=1, source_target_pairs={{0,4},{4,0},{8,12},{12,8},{16,20},{20,16},{24,28},{28,24},{1,5},{5... | collective-permute-start | bytes 196616 | tf_op jit(solution)/shard_map/ppermute | solution.py:251
  27.5 7.3 %collective-permute-start.9 = (bf16[128,256]{1,0:T(8,128)(2,1)S(1)}, bf16[128,256]{1,0:T(8,128)(2,1)S(1)}, u32[]{:S(2)}, u32[]{:S(2)}) collective-permute-start(bf16[128,256]{1,0:T(8,128)(2,1)S(1)} %get-tuple-element.47), channel_id=1, source_target_pairs={{0,8},{4,12},{8,0},{12,4},{16,24},{20,28},{24,16},{28,20},{1,9},{5... | collective-permute-start | bytes 196616 | tf_op jit(solution)/shard_map/ppermute | solution.py:251
  28.7 6.1 %collective-permute-start.10 = (bf16[128,256]{1,0:T(8,128)(2,1)S(1)}, bf16[128,256]{1,0:T(8,128)(2,1)S(1)}, u32[]{:S(2)}, u32[]{:S(2)}) collective-permute-start(bf16[128,256]{1,0:T(8,128)(2,1)S(1)} %get-tuple-element.48), channel_id=1, source_target_pairs={{0,12},{4,8},{8,4},{12,0},{16,28},{20,24},{24,20},{28,16},{1,13},{... | collective-permute-start | bytes 196616 | tf_op jit(solution)/shard_map/ppermute | solution.py:251
  33.1 13.2 %collective-permute-start.14 = (bf16[256,896]{1,0:T(8,128)(2,1)}, bf16[256,896]{1,0:T(8,128)(2,1)S(1)}, u32[]{:S(2)}, u32[]{:S(2)}) collective-permute-start(bf16[256,896]{1,0:T(8,128)(2,1)} %refs_0_.1), channel_id=1, source_target_pairs={{0,1},{1,0},{2,3},{3,2},{4,5},{5,4},{6,7},{7,6},{8,9},{9,8},{10,11... | collective-permute-start | bytes 1376264 | tf_op jit(solution)/shard_map/ppermute | solution.py:251
  33.2 13.1 %collective-permute-start.15 = (bf16[256,896]{1,0:T(8,128)(2,1)}, bf16[256,896]{1,0:T(8,128)(2,1)S(1)}, u32[]{:S(2)}, u32[]{:S(2)}) collective-permute-start(bf16[256,896]{1,0:T(8,128)(2,1)} %refs_0_.1), channel_id=1, source_target_pairs={{0,2},{1,3},{2,0},{3,1},{4,6},{5,7},{6,4},{7,5},{8,10},{9,11},{10,... | collective-permute-start | bytes 1376264 | tf_op jit(solution)/shard_map/ppermute | solution.py:251
  40.2 9.6 %collective-permute-start.12 = (bf16[256,896]{1,0:T(8,128)(2,1)S(1)}, bf16[256,896]{1,0:T(8,128)(2,1)S(1)}, u32[]{:S(2)}, u32[]{:S(2)}) collective-permute-start(bf16[256,896]{1,0:T(8,128)(2,1)S(1)} %get-tuple-element.53), channel_id=1, source_target_pairs={{0,1},{1,0},{2,3},{3,2},{4,5},{5,4},{6,7},{7,6},{8,9},{9,8},{10,11... | collective-permute-start | bytes 1376264 | tf_op jit(solution)/shard_map/ppermute | solution.py:251
  46.3 5.2 %collective-permute-start.16 = (bf16[256,896]{1,0:T(8,128)(2,1)S(1)}, bf16[256,896]{1,0:T(8,128)(2,1)S(1)}, u32[]{:S(2)}, u32[]{:S(2)}) collective-permute-start(bf16[256,896]{1,0:T(8,128)(2,1)S(1)} %collective-permute-done.15.refs_2_), channel_id=1, source_target_pairs={{0,1},{1,0},{2,3},{3,2},{4,5},{5,4},{6,7},{7,6},{8,9},{9,8},{10,11... | collective-permute-start | bytes 1376264 | tf_op jit(solution)/shard_map/ppermute | solution.py:251
  49.2 28.0 %collective-permute-start.11 = (bf16[256,896]{1,0:T(8,128)(2,1)S(1)}, bf16[256,896]{1,0:T(8,128)(2,1)S(1)}, u32[]{:S(2)}, u32[]{:S(2)}) collective-permute-start(bf16[256,896]{1,0:T(8,128)(2,1)S(1)} %get-tuple-element.51), channel_id=1, source_target_pairs={{0,1},{1,0},{2,3},{3,2},{4,5},{5,4},{6,7},{7,6},{8,9},{9,8},{10,11... | collective-permute-start | bytes 1376264 | tf_op jit(solution)/shard_map/ppermute | solution.py:251
  49.9 27.3 %collective-permute-start.13 = (bf16[256,896]{1,0:T(8,128)(2,1)S(1)}, bf16[256,896]{1,0:T(8,128)(2,1)S(1)}, u32[]{:S(2)}, u32[]{:S(2)}) collective-permute-start(bf16[256,896]{1,0:T(8,128)(2,1)S(1)} %add_convert_fusion.1), channel_id=1, source_target_pairs={{0,2},{1,3},{2,0},{3,1},{4,6},{5,7},{6,4},{7,5},{8,10},{9,11},{10,... | collective-permute-start | bytes 1376264 | tf_op jit(solution)/shard_map/ppermute | solution.py:251
  57.2 4.3 %collective-permute-start.17 = (bf16[128,256]{1,0:T(8,128)(2,1)S(1)}, bf16[128,256]{1,0:T(8,128)(2,1)S(1)}, u32[]{:S(2)}, u32[]{:S(2)}) collective-permute-start(bf16[128,256]{1,0:T(8,128)(2,1)S(1)} %get-tuple-element.58), channel_id=1, source_target_pairs={{0,4},{4,0},{8,12},{12,8},{16,20},{20,16},{24,28},{28,24},{1,5},{5... | collective-permute-start | bytes 196616 | tf_op jit(solution)/shard_map/ppermute | solution.py:251
  57.8 7.0 %collective-permute-start.18 = (bf16[128,256]{1,0:T(8,128)(2,1)S(1)}, bf16[128,256]{1,0:T(8,128)(2,1)S(1)}, u32[]{:S(2)}, u32[]{:S(2)}) collective-permute-start(bf16[128,256]{1,0:T(8,128)(2,1)S(1)} %get-tuple-element.59), channel_id=1, source_target_pairs={{0,8},{4,12},{8,0},{12,4},{16,24},{20,28},{24,16},{28,20},{1,9},{5... | collective-permute-start | bytes 196616 | tf_op jit(solution)/shard_map/ppermute | solution.py:251
  59.1 7.8 %collective-permute-start.19 = (bf16[128,256]{1,0:T(8,128)(2,1)S(1)}, bf16[128,256]{1,0:T(8,128)(2,1)S(1)}, u32[]{:S(2)}, u32[]{:S(2)}) collective-permute-start(bf16[128,256]{1,0:T(8,128)(2,1)S(1)} %get-tuple-element.60), channel_id=1, source_target_pairs={{0,12},{4,8},{8,4},{12,0},{16,28},{20,24},{24,20},{28,16},{1,13},{... | collective-permute-start | bytes 196616 | tf_op jit(solution)/shard_map/ppermute | solution.py:251
  61.6 7.2 %collective-permute-start.20 = (bf16[128,256]{1,0:T(8,128)(2,1)S(1)}, bf16[128,256]{1,0:T(8,128)(2,1)S(1)}, u32[]{:S(2)}, u32[]{:S(2)}) collective-permute-start(bf16[128,256]{1,0:T(8,128)(2,1)S(1)} %get-tuple-element.61), channel_id=1, source_target_pairs={{0,16},{4,20},{8,24},{12,28},{16,0},{20,4},{24,8},{28,12},{1,17},{... | collective-permute-start | bytes 196616 | tf_op jit(solution)/shard_map/ppermute | solution.py:251
  64.8 8.9 %collective-permute-start.21 = (bf16[128,256]{1,0:T(8,128)(2,1)S(1)}, bf16[128,256]{1,0:T(8,128)(2,1)S(1)}, u32[]{:S(2)}, u32[]{:S(2)}) collective-permute-start(bf16[128,256]{1,0:T(8,128)(2,1)S(1)} %get-tuple-element.62), channel_id=1, source_target_pairs={{0,20},{4,16},{8,28},{12,24},{16,4},{20,0},{24,12},{28,8},{1,21},{... | collective-permute-start | bytes 196616 | tf_op jit(solution)/shard_map/ppermute | solution.py:251
  66.9 6.8 %collective-permute-start.22 = (bf16[128,256]{1,0:T(8,128)(2,1)S(1)}, bf16[128,256]{1,0:T(8,128)(2,1)S(1)}, u32[]{:S(2)}, u32[]{:S(2)}) collective-permute-start(bf16[128,256]{1,0:T(8,128)(2,1)S(1)} %get-tuple-element.63), channel_id=1, source_target_pairs={{0,24},{4,28},{8,16},{12,20},{16,8},{20,12},{24,0},{28,4},{1,25},{... | collective-permute-start | bytes 196616 | tf_op jit(solution)/shard_map/ppermute | solution.py:251
  68.7 7.1 %collective-permute-start.23 = (bf16[128,256]{1,0:T(8,128)(2,1)S(1)}, bf16[128,256]{1,0:T(8,128)(2,1)S(1)}, u32[]{:S(2)}, u32[]{:S(2)}) collective-permute-start(bf16[128,256]{1,0:T(8,128)(2,1)S(1)} %get-tuple-element.64), channel_id=1, source_target_pairs={{0,28},{4,24},{8,20},{12,16},{16,12},{20,8},{24,4},{28,0},{1,29},{... | collective-permute-start | bytes 196616 | tf_op jit(solution)/shard_map/ppermute | solution.py:251
  (3 other events, 20.1 us)

commit v6 on v3

--- a/solution.py
+++ b/solution.py
@@ -176,9 +176,24 @@
     out[...] = total
 
 
+def give(outs, start, probs_ref, slopes_ref, gt_ref, q_ref, scaling):
+    stop = start + sum(out.shape[0] for out in outs)
+    value_grad = dot(probs_ref[start:stop, :], gt_ref[...], ((1,), (1,)))
+    key_grad = dot(slopes_ref[start:stop, :], q_ref[...], ((1,), (0,))) * scaling
+    at = 0
+    for out in outs:
+        size = out.shape[0]
+        out[:, HD:] = value_grad[at:at + size].astype(out.dtype)
+        out[:, :HD] = key_grad[at:at + size].astype(out.dtype)
+        at += size
+
+
+def near_kernel(scaling, exps_ref, dbuf, gt_all, q_all, *outs):
+    give(outs, 0, exps_ref, dbuf, gt_all, q_all, scaling)
+
+
 def backward_kernel(last, n_pre, scaling, me_ref, w_ref, part_ref, grad_ref, q_ref, v_all, exps_ref, row_ref, *refs):
-    outs = refs[:n_pre]
-    gt_all, q_all, dbuf, slopes = refs[n_pre:]
+    outs, (gt_all, q_all, dbuf, slopes) = refs[:n_pre], refs[n_pre:]
     me = me_ref[0]
     length, width = grad_ref.shape
     heads = q_ref.shape[1] // HD
@@ -209,14 +224,7 @@
         later = slope(h + 1) if h + 1 < heads else None
         finish(h, delta)
         delta = later
-    value_grad = dot(exps_ref[:n_rows, :], gt_all[...], ((1,), (1,)))
-    key_grad = dot(dbuf[...], q_all[...], ((1,), (0,))) * scaling
-    at = 0
-    for out in outs:
-        size = out.shape[0]
-        out[:, HD:] = value_grad[at:at + size].astype(out.dtype)
-        out[:, :HD] = key_grad[at:at + size].astype(out.dtype)
-        at += size
+    give(outs, n_rows - sum(out.shape[0] for out in outs), exps_ref, dbuf, gt_all, q_all, scaling)
 
 
 def local(hidden_states, queries, key_weight, value_weight, output_weight, prefix_keys, prefix_values, reads, out_grad):
@@ -357,21 +365,35 @@
     layer_output = (share0.astype(F32) + near1.astype(F32) + across.astype(F32)).astype(BF16)
 
     grad_type = BF16 if dense else F32
-    parts = pl.pallas_call(
-        functools.partial(backward_kernel, n_tp - 1, n_pre, scaling),
-        out_shape=[jax.ShapeDtypeStruct(x.shape, grad_type) for x in prefix],
+    types = [jax.ShapeDtypeStruct(x.shape, grad_type) for x in prefix]
+    n_near = n_pre // 2
+    n_far = n_pre - n_near
+    *far_parts, gt, q_rows, slopes = pl.pallas_call(
+        functools.partial(backward_kernel, n_tp - 1, n_far, scaling),
+        out_shape=types[n_near:] + [
+            jax.ShapeDtypeStruct((HD, heads * length), BF16),
+            jax.ShapeDtypeStruct((heads * length, HD), BF16),
+            jax.ShapeDtypeStruct((n_rows, heads * length), BF16),
+        ],
         in_specs=[SMEM] + [VMEM] * 7,
-        out_specs=[VMEM] * n_pre,
-        scratch_shapes=[
-            pltpu.VMEM((HD, heads * length), BF16),
-            pltpu.VMEM((heads * length, HD), BF16),
-            pltpu.VMEM((n_rows, heads * length), BF16),
-            pltpu.VMEM((2, n_rows, length), F32),
-        ],
-        compiler_params=grant(32),
-        cost_estimate=cost(7e9, 1e7),
+        out_specs=[VMEM] * (n_far + 3),
+        scratch_shapes=[pltpu.VMEM((2, n_rows, length), F32)],
+        compiler_params=grant(28),
+        cost_estimate=cost(6e9, 1e7),
         name="backward",
     )(me_tp, output_weight, part_grad, last_grad, q, v_all, exps, row)
+    near_parts = []
+    if n_near:
+        near_parts = pl.pallas_call(
+            functools.partial(near_kernel, scaling),
+            out_shape=types[:n_near],
+            in_specs=[VMEM] * 4,
+            out_specs=[VMEM] * n_near,
+            compiler_params=grant(16),
+            cost_estimate=cost(1e9, 5e6),
+            name="near_half",
+        )(exps, slopes, gt, q_rows)
+    parts = [*near_parts, *far_parts]
 
     if dense:
         back = {k: hop(parts[k], "seq", k) for k in far_first}

time: 78.3 us -> 79 us (level)
    pallas_call x1 -> x2, Pallas kernels: 5.73 us -> 6.4 us  [the longest x1 5.28 us: local(): pl.pallas_call(functools.partial(backward_kernel, n_tp - 1, n_far, scalin...]
  transfers between devices with their start and end apart: 23 -> 23, of which waited for: 9 -> 9; matrix products, arithmetic and copies ran while one was open for 0% -> 0% of each run, Pallas kernels for 24% -> 25%
where the time goes in v6:
time: 79 us; the launch traced here: 78.8 us
  starting transfers between devices  31 us (39%)
  waiting for transfers between devices  26.2 us (33%)
  Pallas kernels  19.7 us (25%)
  other arithmetic  1.06 us (1%)
    ppermute x23, starting transfers between devices, hop(): return lax.ppermute(x, axis, [(i, i ^ k) for i in range(n)])  31 us
    ppermute x23, waiting for transfers between devices, hop(): return lax.ppermute(x, axis, [(i, i ^ k) for i in range(n)])  26.2 us
    pallas_call x1, Pallas kernels, local(): pl.pallas_call(functools.partial(backward_kernel, n_tp - 1, n_far, scalin...  5.28 us
    pallas_call x1, Pallas kernels, local(): pl.pallas_call(functools.partial(forward_kernel, n_pre, scaling), out_sha...  4.08 us
    pallas_call x1, Pallas kernels, local(): pl.pallas_call(functools.partial(kv_kernel, (1, 0, 2), n_tp - 1), out_sha...  2.67 us
    pallas_call x2, Pallas kernels, project(): pl.pallas_call(functools.partial(project_kernel, order), out_shape=[jax.S...  2.49 us
    pallas_call x1, Pallas kernels, local(): pl.pallas_call(functools.partial(grad_kernel, (0, 1, 2)), out_shape=jax.S...  1.62 us
  transfers between devices with their start and end apart: 23, of which 9 were waited for; matrix products, arithmetic and copies ran while one was open for 0% of the time, Pallas kernels for 25%

profile of v6, /device:TPU:0, one launch (start us, length us, event | category | flops | bytes accessed | tf_op | source)
XLA Modules:
  0.0 78.8 jit_solution(8449806915235785268)
XLA Ops:
  0.6 3.1 %collective-permute-start.1 = (bf16[256,896]{1,0:T(8,128)(2,1)}, bf16[256,896]{1,0:T(8,128)(2,1)S(1)}, u32[]{:S(2)}, u32[]{:S(2)}) collective-permute-start(bf16[256,896]{1,0:T(8,128)(2,1)} %own_hbm.1), channel_id=1, source_target_pairs={{0,2},{1,3},{2,0},{3,1},{4,6},{5,7},{6,4},{7,5},{8,10},{9,11},{10,... | collective-permute-start | bytes 1376264 | tf_op jit(solution)/shard_map/ppermute | solution.py:247
  3.7 10.7 %collective-permute-done.1.refs_1_ = bf16[256,896]{1,0:T(8,128)(2,1)S(1)} collective-permute-done((bf16[256,896]{1,0:T(8,128)(2,1)}, bf16[256,896]{1,0:T(8,128)(2,1)S(1)}, u32[]{:S(2)}, u32[]{:S(2)}) %collective-permute-start.1) | collective-permute-done | bytes 458784 | tf_op jit(solution)/shard_map/ppermute | solution.py:247
  15.4 1.8 %collective-permute-start.3 = (bf16[128,256]{1,0:T(8,128)(2,1)S(1)}, bf16[128,256]{1,0:T(8,128)(2,1)S(1)}, u32[]{:S(2)}, u32[]{:S(2)}) collective-permute-start(bf16[128,256]{1,0:T(8,128)(2,1)S(1)} %get-tuple-element.43), channel_id=1, source_target_pairs={{0,4},{4,0},{8,12},{12,8},{16,20},{20,16},{24,28},{28,24},{1,5},{5... | collective-permute-start | bytes 196616 | tf_op jit(solution)/shard_map/ppermute | solution.py:247
  17.2 1.6 %collective-permute-start.4 = (bf16[128,256]{1,0:T(8,128)(2,1)S(1)}, bf16[128,256]{1,0:T(8,128)(2,1)S(1)}, u32[]{:S(2)}, u32[]{:S(2)}) collective-permute-start(bf16[128,256]{1,0:T(8,128)(2,1)S(1)} %get-tuple-element.44), channel_id=1, source_target_pairs={{0,8},{4,12},{8,0},{12,4},{16,24},{20,28},{24,16},{28,20},{1,9},{5... | collective-permute-start | bytes 196616 | tf_op jit(solution)/shard_map/ppermute | solution.py:247
  20.0 2.8 %collective-permute-start.6 = (bf16[128,256]{1,0:T(8,128)(2,1)S(1)}, bf16[128,256]{1,0:T(8,128)(2,1)S(1)}, u32[]{:S(2)}, u32[]{:S(2)}) collective-permute-start(bf16[128,256]{1,0:T(8,128)(2,1)S(1)} %get-tuple-element.46), channel_id=1, source_target_pairs={{0,16},{4,20},{8,24},{12,28},{16,0},{20,4},{24,8},{28,12},{1,17},{... | collective-permute-start | bytes 196616 | tf_op jit(solution)/shard_map/ppermute | solution.py:247
  24.1 3.6 %collective-permute-start.8 = (bf16[128,256]{1,0:T(8,128)(2,1)S(1)}, bf16[128,256]{1,0:T(8,128)(2,1)S(1)}, u32[]{:S(2)}, u32[]{:S(2)}) collective-permute-start(bf16[128,256]{1,0:T(8,128)(2,1)S(1)} %get-tuple-element.48), channel_id=1, source_target_pairs={{0,24},{4,28},{8,16},{12,20},{16,8},{20,12},{24,0},{28,4},{1,25},{... | collective-permute-start | bytes 196616 | tf_op jit(solution)/shard_map/ppermute | solution.py:247
  27.7 1.3 %collective-permute-start.9 = (bf16[128,256]{1,0:T(8,128)(2,1)S(1)}, bf16[128,256]{1,0:T(8,128)(2,1)S(1)}, u32[]{:S(2)}, u32[]{:S(2)}) collective-permute-start(bf16[128,256]{1,0:T(8,128)(2,1)S(1)} %get-tuple-element.49), channel_id=1, source_target_pairs={{0,28},{4,24},{8,20},{12,16},{16,12},{20,8},{24,4},{28,0},{1,29},{... | collective-permute-start | bytes 196616 | tf_op jit(solution)/shard_map/ppermute | solution.py:247
  29.0 2.7 %kv.1 = (f32[256,128]{1,0:T(8,128)S(1)}, f32[256,128]{1,0:T(8,128)S(1)}, bf16[256,896]{1,0:T(8,128)(2,1)S(1)}, bf16[896,128]{1,0:T(8,128)(2,1)S(1)}, bf16[896,128]{1,0:T(8,128)(2,1)S(1)}) custom-call(s32[1]{0:T(128)} %bitcast.me_ref, bf16[256,896]{1,0:T(8,128)(2,1)} %own_hbm.1, bf16[256,896]{1,0:T(8,128)(2,1)S(1)} %collective-permute-done.refs_0_, ...), custom_call_target="tpu_custom_call" | custom-call | flops 400000000 | bytes 3000000 | tf_op jit(solution)/shard_map/kv/pallas_call | solution.py:301
  32.7 1.5 %collective-permute-start.14 = (bf16[256,896]{1,0:T(8,128)(2,1)}, bf16[256,896]{1,0:T(8,128)(2,1)S(1)}, u32[]{:S(2)}, u32[]{:S(2)}) collective-permute-start(bf16[256,896]{1,0:T(8,128)(2,1)} %refs_0_.1), channel_id=1, source_target_pairs={{0,2},{1,3},{2,0},{3,1},{4,6},{5,7},{6,4},{7,5},{8,10},{9,11},{10,... | collective-permute-start | bytes 1376264 | tf_op jit(solution)/shard_map/ppermute | solution.py:247
  34.8 4.1 %forward.1 = (bf16[256,896]{1,0:T(8,128)(2,1)S(1)}, bf16[1280,1792]{1,0:T(8,128)(2,1)S(1)}, f32[8,256]{1,0:T(8,128)S(1)}, bf16[1280,128]{1,0:T(8,128)(2,1)S(1)}) custom-call(bf16[896,128]{1,0:T(8,128)(2,1)S(1)} %get-tuple-element.37.wk_ref, bf16[896,128]{1,0:T(8,128)(2,1)S(1)} %get-tuple-element.38.wv_ref, ...), custom_call_target="tpu_custom_call" | custom-call | flops 5000000000 | bytes 10000000 | tf_op jit(solution)/shard_map/forward/pallas_call | solution.py:318
  40.2 4.7 %collective-permute-done.14.refs_2_ = bf16[256,896]{1,0:T(8,128)(2,1)S(1)} collective-permute-done((bf16[256,896]{1,0:T(8,128)(2,1)}, bf16[256,896]{1,0:T(8,128)(2,1)S(1)}, u32[]{:S(2)}, u32[]{:S(2)}) %collective-permute-start.14) | collective-permute-done | bytes 458784 | tf_op jit(solution)/shard_map/ppermute | solution.py:247
  44.9 1.6 %grad.1.part_ref = f32[896,256]{1,0:T(8,128)S(1)} custom-call(s32[1]{0:T(128)} %bitcast.me_ref, bf16[896,3584]{1,0:T(8,128)(2,1)S(1)} %bitcast.3, bf16[256,896]{1,0:T(8,128)(2,1)S(1)} %copy-done, bf16[256,896]{1,0:T(8,128)(2,1)S(1)} %collective-permute-done.13.refs_1_, bf16[256,896]{1,0:T(8,128)(2,1)S(1)} %collective-permute-done.14.refs_2_), custom_call_target="tpu_custom_call" | custom-call | flops 1500000000 | bytes 8000000 | tf_op jit(solution)/shard_map/grad/pallas_call | solution.py:339
  48.5 1.6 %collective-permute-start.12 = (bf16[256,896]{1,0:T(8,128)(2,1)S(1)}, bf16[256,896]{1,0:T(8,128)(2,1)S(1)}, u32[]{:S(2)}, u32[]{:S(2)}) collective-permute-start(bf16[256,896]{1,0:T(8,128)(2,1)S(1)} %add_convert_fusion.1), channel_id=1, source_target_pairs={{0,2},{1,3},{2,0},{3,1},{4,6},{5,7},{6,4},{7,5},{8,10},{9,11},{10,... | collective-permute-start | bytes 1376264 | tf_op jit(solution)/shard_map/ppermute | solution.py:247
  50.1 5.3 %backward.1 = (bf16[128,256]{1,0:T(8,128)(2,1)S(1)}, bf16[128,256]{1,0:T(8,128)(2,1)S(1)}, bf16[128,256]{1,0:T(8,128)(2,1)S(1)}, bf16[128,256]{1,0:T(8,128)(2,1)...) custom-call(s32[1]{0:T(128)} %bitcast.me_ref, ...), custom_call_target="tpu_custom_call" | custom-call | flops 6000000000 | bytes 10000000 | tf_op jit(solution)/shard_map/backward/pallas_call | solution.py:371
  56.9 1.3 %collective-permute-start.17 = (bf16[128,256]{1,0:T(8,128)(2,1)S(1)}, bf16[128,256]{1,0:T(8,128)(2,1)S(1)}, u32[]{:S(2)}, u32[]{:S(2)}) collective-permute-start(bf16[128,256]{1,0:T(8,128)(2,1)S(1)} %get-tuple-element.63), channel_id=1, source_target_pairs={{0,8},{4,12},{8,0},{12,4},{16,24},{20,28},{24,16},{28,20},{1,9},{5... | collective-permute-start | bytes 196616 | tf_op jit(solution)/shard_map/ppermute | solution.py:247
  58.3 1.8 %collective-permute-start.18 = (bf16[128,256]{1,0:T(8,128)(2,1)S(1)}, bf16[128,256]{1,0:T(8,128)(2,1)S(1)}, u32[]{:S(2)}, u32[]{:S(2)}) collective-permute-start(bf16[128,256]{1,0:T(8,128)(2,1)S(1)} %get-tuple-element.64), channel_id=1, source_target_pairs={{0,12},{4,8},{8,4},{12,0},{16,28},{20,24},{24,20},{28,16},{1,13},{... | collective-permute-start | bytes 196616 | tf_op jit(solution)/shard_map/ppermute | solution.py:247
  60.8 1.8 %collective-permute-start.19 = (bf16[128,256]{1,0:T(8,128)(2,1)S(1)}, bf16[128,256]{1,0:T(8,128)(2,1)S(1)}, u32[]{:S(2)}, u32[]{:S(2)}) collective-permute-start(bf16[128,256]{1,0:T(8,128)(2,1)S(1)} %get-tuple-element.65), channel_id=1, source_target_pairs={{0,16},{4,20},{8,24},{12,28},{16,0},{20,4},{24,8},{28,12},{1,17},{... | collective-permute-start | bytes 196616 | tf_op jit(solution)/shard_map/ppermute | solution.py:247
  62.6 2.9 %collective-permute-start.20 = (bf16[128,256]{1,0:T(8,128)(2,1)S(1)}, bf16[128,256]{1,0:T(8,128)(2,1)S(1)}, u32[]{:S(2)}, u32[]{:S(2)}) collective-permute-start(bf16[128,256]{1,0:T(8,128)(2,1)S(1)} %get-tuple-element.66), channel_id=1, source_target_pairs={{0,20},{4,16},{8,28},{12,24},{16,4},{20,0},{24,12},{28,8},{1,21},{... | collective-permute-start | bytes 196616 | tf_op jit(solution)/shard_map/ppermute | solution.py:247
  65.5 1.7 %collective-permute-start.21 = (bf16[128,256]{1,0:T(8,128)(2,1)S(1)}, bf16[128,256]{1,0:T(8,128)(2,1)S(1)}, u32[]{:S(2)}, u32[]{:S(2)}) collective-permute-start(bf16[128,256]{1,0:T(8,128)(2,1)S(1)} %get-tuple-element.67), channel_id=1, source_target_pairs={{0,24},{4,28},{8,16},{12,20},{16,8},{20,12},{24,0},{28,4},{1,25},{... | collective-permute-start | bytes 196616 | tf_op jit(solution)/shard_map/ppermute | solution.py:247
  67.2 2.3 %collective-permute-done.19.refs_4_ = bf16[128,256]{1,0:T(8,128)(2,1)S(1)} collective-permute-done((bf16[128,256]{1,0:T(8,128)(2,1)S(1)}, bf16[128,256]{1,0:T(8,128)(2,1)S(1)}, u32[]{:S(2)}, u32[]{:S(2)}) %collective-permute-start.19) | collective-permute-done | bytes 65568 | tf_op jit(solution)/shard_map/ppermute | solution.py:247
  69.5 1.7 %collective-permute-start.22 = (bf16[128,256]{1,0:T(8,128)(2,1)S(1)}, bf16[128,256]{1,0:T(8,128)(2,1)S(1)}, u32[]{:S(2)}, u32[]{:S(2)}) collective-permute-start(bf16[128,256]{1,0:T(8,128)(2,1)S(1)} %get-tuple-element.68), channel_id=1, source_target_pairs={{0,28},{4,24},{8,20},{12,16},{16,12},{20,8},{24,4},{28,0},{1,29},{... | collective-permute-start | bytes 196616 | tf_op jit(solution)/shard_map/ppermute | solution.py:247
  71.2 1.6 %collective-permute-done.20.refs_5_ = bf16[128,256]{1,0:T(8,128)(2,1)S(1)} collective-permute-done((bf16[128,256]{1,0:T(8,128)(2,1)S(1)}, bf16[128,256]{1,0:T(8,128)(2,1)S(1)}, u32[]{:S(2)}, u32[]{:S(2)}) %collective-permute-start.20) | collective-permute-done | bytes 65568 | tf_op jit(solution)/shard_map/ppermute | solution.py:247
  72.8 3.6 %collective-permute-done.22.refs_7_ = bf16[128,256]{1,0:T(8,128)(2,1)S(1)} collective-permute-done((bf16[128,256]{1,0:T(8,128)(2,1)S(1)}, bf16[128,256]{1,0:T(8,128)(2,1)S(1)}, u32[]{:S(2)}, u32[]{:S(2)}) %collective-permute-start.22) | collective-permute-done | bytes 65568 | tf_op jit(solution)/shard_map/ppermute | solution.py:247
  76.4 1.4 %place.1 = (f32[256,128]{1,0:T(8,128)}, f32[256,128]{1,0:T(8,128)}) custom-call(s32[1]{0:T(128)} %bitcast.1.me_ref, s32[8,16]{1,0:T(8,128)S(1)} %copy-done.1, bf16[128,256]{1,0:T(8,128)(2,1)S(1)} %get-tuple-element.61.refs_0_, bf16[128,256]{1,0:T(8,128)(2,1)S(1)} %collective-permute-done.16.refs_1_, bf16[128,256]{1,0:T(8,128)(2,1)S(1)} %collective-permute-done.17.refs_2_, ...), custom_call_target="tpu_custom_call" | custom-call | bytes 1048576 | tf_op jit(solution)/shard_map/place/pallas_call | solution.py:402
  (42 shorter events, 11.7 us)
Async XLA Ops:
  0.6 13.8 %collective-permute-start.1 = (bf16[256,896]{1,0:T(8,128)(2,1)}, bf16[256,896]{1,0:T(8,128)(2,1)S(1)}, u32[]{:S(2)}, u32[]{:S(2)}) collective-permute-start(bf16[256,896]{1,0:T(8,128)(2,1)} %own_hbm.1), channel_id=1, source_target_pairs={{0,2},{1,3},{2,0},{3,1},{4,6},{5,7},{6,4},{7,5},{8,10},{9,11},{10,... | collective-permute-start | bytes 1376264 | tf_op jit(solution)/shard_map/ppermute | solution.py:247
  3.7 24.0 %collective-permute-start = (bf16[256,896]{1,0:T(8,128)(2,1)}, bf16[256,896]{1,0:T(8,128)(2,1)S(1)}, u32[]{:S(2)}, u32[]{:S(2)}) collective-permute-start(bf16[256,896]{1,0:T(8,128)(2,1)} %own_hbm.1), channel_id=1, source_target_pairs={{0,1},{1,0},{2,3},{3,2},{4,5},{5,4},{6,7},{7,6},{8,9},{9,8},{10,11... | collective-permute-start | bytes 1376264 | tf_op jit(solution)/shard_map/ppermute | solution.py:247
  14.4 20.3 %collective-permute-start.2 = (bf16[256,896]{1,0:T(8,128)(2,1)S(1)}, bf16[256,896]{1,0:T(8,128)(2,1)S(1)}, u32[]{:S(2)}, u32[]{:S(2)}) collective-permute-start(bf16[256,896]{1,0:T(8,128)(2,1)S(1)} %collective-permute-done.1.refs_1_), channel_id=1, source_target_pairs={{0,1},{1,0},{2,3},{3,2},{4,5},{5,4},{6,7},{7,6},{8,9},{9,8},{10,11... | collective-permute-start | bytes 1376264 | tf_op jit(solution)/shard_map/ppermute | solution.py:247
  15.4 4.6 %collective-permute-start.3 = (bf16[128,256]{1,0:T(8,128)(2,1)S(1)}, bf16[128,256]{1,0:T(8,128)(2,1)S(1)}, u32[]{:S(2)}, u32[]{:S(2)}) collective-permute-start(bf16[128,256]{1,0:T(8,128)(2,1)S(1)} %get-tuple-element.43), channel_id=1, source_target_pairs={{0,4},{4,0},{8,12},{12,8},{16,20},{20,16},{24,28},{28,24},{1,5},{5... | collective-permute-start | bytes 196616 | tf_op jit(solution)/shard_map/ppermute | solution.py:247
  17.2 5.6 %collective-permute-start.4 = (bf16[128,256]{1,0:T(8,128)(2,1)S(1)}, bf16[128,256]{1,0:T(8,128)(2,1)S(1)}, u32[]{:S(2)}, u32[]{:S(2)}) collective-permute-start(bf16[128,256]{1,0:T(8,128)(2,1)S(1)} %get-tuple-element.44), channel_id=1, source_target_pairs={{0,8},{4,12},{8,0},{12,4},{16,24},{20,28},{24,16},{28,20},{1,9},{5... | collective-permute-start | bytes 196616 | tf_op jit(solution)/shard_map/ppermute | solution.py:247
  18.8 5.3 %collective-permute-start.5 = (bf16[128,256]{1,0:T(8,128)(2,1)S(1)}, bf16[128,256]{1,0:T(8,128)(2,1)S(1)}, u32[]{:S(2)}, u32[]{:S(2)}) collective-permute-start(bf16[128,256]{1,0:T(8,128)(2,1)S(1)} %get-tuple-element.45), channel_id=1, source_target_pairs={{0,12},{4,8},{8,4},{12,0},{16,28},{20,24},{24,20},{28,16},{1,13},{... | collective-permute-start | bytes 196616 | tf_op jit(solution)/shard_map/ppermute | solution.py:247
  20.0 11.6 %collective-permute-start.6 = (bf16[128,256]{1,0:T(8,128)(2,1)S(1)}, bf16[128,256]{1,0:T(8,128)(2,1)S(1)}, u32[]{:S(2)}, u32[]{:S(2)}) collective-permute-start(bf16[128,256]{1,0:T(8,128)(2,1)S(1)} %get-tuple-element.46), channel_id=1, source_target_pairs={{0,16},{4,20},{8,24},{12,28},{16,0},{20,4},{24,8},{28,12},{1,17},{... | collective-permute-start | bytes 196616 | tf_op jit(solution)/shard_map/ppermute | solution.py:247
  22.8 9.9 %collective-permute-start.7 = (bf16[128,256]{1,0:T(8,128)(2,1)S(1)}, bf16[128,256]{1,0:T(8,128)(2,1)S(1)}, u32[]{:S(2)}, u32[]{:S(2)}) collective-permute-start(bf16[128,256]{1,0:T(8,128)(2,1)S(1)} %get-tuple-element.47), channel_id=1, source_target_pairs={{0,20},{4,16},{8,28},{12,24},{16,4},{20,0},{24,12},{28,8},{1,21},{... | collective-permute-start | bytes 196616 | tf_op jit(solution)/shard_map/ppermute | solution.py:247
  24.1 10.1 %collective-permute-start.8 = (bf16[128,256]{1,0:T(8,128)(2,1)S(1)}, bf16[128,256]{1,0:T(8,128)(2,1)S(1)}, u32[]{:S(2)}, u32[]{:S(2)}) collective-permute-start(bf16[128,256]{1,0:T(8,128)(2,1)S(1)} %get-tuple-element.48), channel_id=1, source_target_pairs={{0,24},{4,28},{8,16},{12,20},{16,8},{20,12},{24,0},{28,4},{1,25},{... | collective-permute-start | bytes 196616 | tf_op jit(solution)/shard_map/ppermute | solution.py:247
  27.7 7.1 %collective-permute-start.9 = (bf16[128,256]{1,0:T(8,128)(2,1)S(1)}, bf16[128,256]{1,0:T(8,128)(2,1)S(1)}, u32[]{:S(2)}, u32[]{:S(2)}) collective-permute-start(bf16[128,256]{1,0:T(8,128)(2,1)S(1)} %get-tuple-element.49), channel_id=1, source_target_pairs={{0,28},{4,24},{8,20},{12,16},{16,12},{20,8},{24,4},{28,0},{1,29},{... | collective-permute-start | bytes 196616 | tf_op jit(solution)/shard_map/ppermute | solution.py:247
  31.7 13.2 %collective-permute-start.13 = (bf16[256,896]{1,0:T(8,128)(2,1)}, bf16[256,896]{1,0:T(8,128)(2,1)S(1)}, u32[]{:S(2)}, u32[]{:S(2)}) collective-permute-start(bf16[256,896]{1,0:T(8,128)(2,1)} %refs_0_.1), channel_id=1, source_target_pairs={{0,1},{1,0},{2,3},{3,2},{4,5},{5,4},{6,7},{7,6},{8,9},{9,8},{10,11... | collective-permute-start | bytes 1376264 | tf_op jit(solution)/shard_map/ppermute | solution.py:247
  32.7 12.2 %collective-permute-start.14 = (bf16[256,896]{1,0:T(8,128)(2,1)}, bf16[256,896]{1,0:T(8,128)(2,1)S(1)}, u32[]{:S(2)}, u32[]{:S(2)}) collective-permute-start(bf16[256,896]{1,0:T(8,128)(2,1)} %refs_0_.1), channel_id=1, source_target_pairs={{0,2},{1,3},{2,0},{3,1},{4,6},{5,7},{6,4},{7,5},{8,10},{9,11},{10,... | collective-permute-start | bytes 1376264 | tf_op jit(solution)/shard_map/ppermute | solution.py:247
  40.1 8.2 %collective-permute-start.11 = (bf16[256,896]{1,0:T(8,128)(2,1)S(1)}, bf16[256,896]{1,0:T(8,128)(2,1)S(1)}, u32[]{:S(2)}, u32[]{:S(2)}) collective-permute-start(bf16[256,896]{1,0:T(8,128)(2,1)S(1)} %get-tuple-element.54), channel_id=1, source_target_pairs={{0,1},{1,0},{2,3},{3,2},{4,5},{5,4},{6,7},{7,6},{8,9},{9,8},{10,11... | collective-permute-start | bytes 1376264 | tf_op jit(solution)/shard_map/ppermute | solution.py:247
  44.9 5.2 %collective-permute-start.15 = (bf16[256,896]{1,0:T(8,128)(2,1)S(1)}, bf16[256,896]{1,0:T(8,128)(2,1)S(1)}, u32[]{:S(2)}, u32[]{:S(2)}) collective-permute-start(bf16[256,896]{1,0:T(8,128)(2,1)S(1)} %collective-permute-done.14.refs_2_), channel_id=1, source_target_pairs={{0,1},{1,0},{2,3},{3,2},{4,5},{5,4},{6,7},{7,6},{8,9},{9,8},{10,11... | collective-permute-start | bytes 1376264 | tf_op jit(solution)/shard_map/ppermute | solution.py:247
  47.8 30.1 %collective-permute-start.10 = (bf16[256,896]{1,0:T(8,128)(2,1)S(1)}, bf16[256,896]{1,0:T(8,128)(2,1)S(1)}, u32[]{:S(2)}, u32[]{:S(2)}) collective-permute-start(bf16[256,896]{1,0:T(8,128)(2,1)S(1)} %get-tuple-element.52), channel_id=1, source_target_pairs={{0,1},{1,0},{2,3},{3,2},{4,5},{5,4},{6,7},{7,6},{8,9},{9,8},{10,11... | collective-permute-start | bytes 1376264 | tf_op jit(solution)/shard_map/ppermute | solution.py:247
  48.5 29.4 %collective-permute-start.12 = (bf16[256,896]{1,0:T(8,128)(2,1)S(1)}, bf16[256,896]{1,0:T(8,128)(2,1)S(1)}, u32[]{:S(2)}, u32[]{:S(2)}) collective-permute-start(bf16[256,896]{1,0:T(8,128)(2,1)S(1)} %add_convert_fusion.1), channel_id=1, source_target_pairs={{0,2},{1,3},{2,0},{3,1},{4,6},{5,7},{6,4},{7,5},{8,10},{9,11},{10,... | collective-permute-start | bytes 1376264 | tf_op jit(solution)/shard_map/ppermute | solution.py:247
  55.3 21.1 %copy-start.1 = (s32[8,16]{1,0:T(8,128)S(1)}, s32[8,16]{1,0:T(8,128)}, u32[]{:S(2)}) copy-start(s32[8,16]{1,0:T(8,128)} %reads_ref.1) | copy-start | bytes 1540
  56.5 4.3 %collective-permute-start.16 = (bf16[128,256]{1,0:T(8,128)(2,1)S(1)}, bf16[128,256]{1,0:T(8,128)(2,1)S(1)}, u32[]{:S(2)}, u32[]{:S(2)}) collective-permute-start(bf16[128,256]{1,0:T(8,128)(2,1)S(1)} %get-tuple-element.62), channel_id=1, source_target_pairs={{0,4},{4,0},{8,12},{12,8},{16,20},{20,16},{24,28},{28,24},{1,5},{5... | collective-permute-start | bytes 196616 | tf_op jit(solution)/shard_map/ppermute | solution.py:247
  56.9 5.6 %collective-permute-start.17 = (bf16[128,256]{1,0:T(8,128)(2,1)S(1)}, bf16[128,256]{1,0:T(8,128)(2,1)S(1)}, u32[]{:S(2)}, u32[]{:S(2)}) collective-permute-start(bf16[128,256]{1,0:T(8,128)(2,1)S(1)} %get-tuple-element.63), channel_id=1, source_target_pairs={{0,8},{4,12},{8,0},{12,4},{16,24},{20,28},{24,16},{28,20},{1,9},{5... | collective-permute-start | bytes 196616 | tf_op jit(solution)/shard_map/ppermute | solution.py:247
  58.3 7.2 %collective-permute-start.18 = (bf16[128,256]{1,0:T(8,128)(2,1)S(1)}, bf16[128,256]{1,0:T(8,128)(2,1)S(1)}, u32[]{:S(2)}, u32[]{:S(2)}) collective-permute-start(bf16[128,256]{1,0:T(8,128)(2,1)S(1)} %get-tuple-element.64), channel_id=1, source_target_pairs={{0,12},{4,8},{8,4},{12,0},{16,28},{20,24},{24,20},{28,16},{1,13},{... | collective-permute-start | bytes 196616 | tf_op jit(solution)/shard_map/ppermute | solution.py:247
  60.8 8.7 %collective-permute-start.19 = (bf16[128,256]{1,0:T(8,128)(2,1)S(1)}, bf16[128,256]{1,0:T(8,128)(2,1)S(1)}, u32[]{:S(2)}, u32[]{:S(2)}) collective-permute-start(bf16[128,256]{1,0:T(8,128)(2,1)S(1)} %get-tuple-element.65), channel_id=1, source_target_pairs={{0,16},{4,20},{8,24},{12,28},{16,0},{20,4},{24,8},{28,12},{1,17},{... | collective-permute-start | bytes 196616 | tf_op jit(solution)/shard_map/ppermute | solution.py:247
  62.6 10.2 %collective-permute-start.20 = (bf16[128,256]{1,0:T(8,128)(2,1)S(1)}, bf16[128,256]{1,0:T(8,128)(2,1)S(1)}, u32[]{:S(2)}, u32[]{:S(2)}) collective-permute-start(bf16[128,256]{1,0:T(8,128)(2,1)S(1)} %get-tuple-element.66), channel_id=1, source_target_pairs={{0,20},{4,16},{8,28},{12,24},{16,4},{20,0},{24,12},{28,8},{1,21},{... | collective-permute-start | bytes 196616 | tf_op jit(solution)/shard_map/ppermute | solution.py:247
  65.5 7.3 %collective-permute-start.21 = (bf16[128,256]{1,0:T(8,128)(2,1)S(1)}, bf16[128,256]{1,0:T(8,128)(2,1)S(1)}, u32[]{:S(2)}, u32[]{:S(2)}) collective-permute-start(bf16[128,256]{1,0:T(8,128)(2,1)S(1)} %get-tuple-element.67), channel_id=1, source_target_pairs={{0,24},{4,28},{8,16},{12,20},{16,8},{20,12},{24,0},{28,4},{1,25},{... | collective-permute-start | bytes 196616 | tf_op jit(solution)/shard_map/ppermute | solution.py:247
  69.5 7.0 %collective-permute-start.22 = (bf16[128,256]{1,0:T(8,128)(2,1)S(1)}, bf16[128,256]{1,0:T(8,128)(2,1)S(1)}, u32[]{:S(2)}, u32[]{:S(2)}) collective-permute-start(bf16[128,256]{1,0:T(8,128)(2,1)S(1)} %get-tuple-element.68), channel_id=1, source_target_pairs={{0,28},{4,24},{8,20},{12,16},{16,12},{20,8},{24,4},{28,0},{1,29},{... | collective-permute-start | bytes 196616 | tf_op jit(solution)/shard_map/ppermute | solution.py:247
  (3 other events, 20.0 us)

commit v7 on v3

--- a/solution.py
+++ b/solution.py
@@ -51,17 +51,27 @@
 
 
 def place_kernel(n, cap, here, me_ref, reads_ref, *refs):
-    parts, keys_ref, values_ref = refs[:n], refs[n], refs[n + 1]
-    me = me_ref[0]
-    keys_ref[...] = jnp.zeros_like(keys_ref)
-    values_ref[...] = jnp.zeros_like(values_ref)
-    for k in range(n):
-        for r in range(cap):
-            block = reads_ref[me ^ k, cap * me + r] - here * me
-            rows = pl.ds(pl.multiple_of(block * PBLK, PBLK), PBLK)
-            piece = parts[k][r * PBLK:(r + 1) * PBLK, :].astype(F32)
-            keys_ref[rows, :] += piece[:, :HD]
-            values_ref[rows, :] += piece[:, HD:]
+    parts, (keys_out, values_out, keys_buf, values_buf, sems) = refs[:n], refs[n:]
+    me = me_ref[0]
+    level = here // cap
+    copies = []
+    for r in range(cap):
+        picked = [reads_ref[me ^ k, cap * me + r] - here * me for k in range(n)]
+        for c in range(level):
+            rows = slice((r * level + c) * PBLK, (r * level + c + 1) * PBLK)
+            total = jnp.zeros((PBLK, 2 * HD), F32)
+            for k in range(n):
+                piece = parts[k][r * PBLK:(r + 1) * PBLK, :].astype(F32)
+                total += jnp.where(picked[k] == r * level + c, piece, 0.0)
+            keys_buf[rows, :] = total[:, :HD]
+            values_buf[rows, :] = total[:, HD:]
+        done = pl.ds(r * level * PBLK, level * PBLK)
+        copies.append(pltpu.make_async_copy(keys_buf.at[done], keys_out.at[done], sems.at[r, 0]))
+        copies.append(pltpu.make_async_copy(values_buf.at[done], values_out.at[done], sems.at[r, 1]))
+        for copy in copies[-2:]:
+            copy.start()
+    for copy in copies:
+        copy.wait()
 
 
 def weight_copies(i, me, width, hbms, bufs, slot, sems):
@@ -228,7 +238,7 @@
     here = prefix_keys.shape[0] // PBLK
     read_count = reads.shape[1]
     cap = max(1, read_count // n_seq)
-    dense = cap * n_seq == read_count and n_seq & (n_seq - 1) == 0 and here * n_seq % read_count == 0
+    dense = cap * n_seq == read_count and here % cap == 0 and n_seq & (n_seq - 1) == 0 and here * n_seq % read_count == 0
     me_tp = lax.axis_index("tp").astype(jnp.int32).reshape(1)
     me_seq = lax.axis_index("seq").astype(jnp.int32).reshape(1)
     n_rows = read_count * PBLK
@@ -381,7 +391,12 @@
             functools.partial(place_kernel, n_seq, cap, here),
             out_shape=[shape] * 2,
             in_specs=[SMEM, SMEM] + [VMEM] * n_seq,
-            out_specs=[VMEM] * 2,
+            out_specs=[HBM] * 2,
+            scratch_shapes=[
+                pltpu.VMEM(prefix_keys.shape, F32),
+                pltpu.VMEM(prefix_keys.shape, F32),
+                pltpu.SemaphoreType.DMA((cap, 2)),
+            ],
             cost_estimate=cost(0, 2 ** 20),
             compiler_params=grant(4),
             name="place",

time: 78.3 us -> 78.4 us (level)
  no operation moved by 1% of the time
where the time goes in v7:
time: 78.4 us; the launch traced here: 78.2 us
  starting transfers between devices  31 us (40%)
  waiting for transfers between devices  26.3 us (34%)
  Pallas kernels  19.1 us (24%)
  other arithmetic  1.07 us (1%)
  between operations  0.79 us (1%)
    ppermute x23, starting transfers between devices, hop(): return lax.ppermute(x, axis, [(i, i ^ k) for i in range(n)])  31 us
    ppermute x23, waiting for transfers between devices, hop(): return lax.ppermute(x, axis, [(i, i ^ k) for i in range(n)])  26.3 us
    pallas_call x1, Pallas kernels, local(): pl.pallas_call(functools.partial(backward_kernel, n_tp - 1, n_pre, scalin...  5.73 us
    pallas_call x1, Pallas kernels, local(): pl.pallas_call(functools.partial(forward_kernel, n_pre, scaling), out_sha...  4.07 us
    pallas_call x1, Pallas kernels, local(): pl.pallas_call(functools.partial(kv_kernel, (1, 0, 2), n_tp - 1), out_sha...  2.67 us
    pallas_call x2, Pallas kernels, project(): pl.pallas_call(functools.partial(project_kernel, order), out_shape=[jax.S...  2.49 us
    pallas_call x1, Pallas kernels, local(): pl.pallas_call(functools.partial(grad_kernel, (0, 1, 2)), out_shape=jax.S...  1.62 us
  transfers between devices with their start and end apart: 23, of which 9 were waited for; matrix products, arithmetic and copies ran while one was open for 0% of the time, Pallas kernels for 24%

profile of v7, /device:TPU:0, one launch (start us, length us, event | category | flops | bytes accessed | tf_op | source)
XLA Modules:
  0.0 78.2 jit_solution(10886107696396120998)
XLA Ops:
  0.6 3.1 %collective-permute-start.1 = (bf16[256,896]{1,0:T(8,128)(2,1)}, bf16[256,896]{1,0:T(8,128)(2,1)S(1)}, u32[]{:S(2)}, u32[]{:S(2)}) collective-permute-start(bf16[256,896]{1,0:T(8,128)(2,1)} %own_hbm.1), channel_id=1, source_target_pairs={{0,2},{1,3},{2,0},{3,1},{4,6},{5,7},{6,4},{7,5},{8,10},{9,11},{10,... | collective-permute-start | bytes 1376264 | tf_op jit(solution)/shard_map/ppermute | solution.py:249
  3.7 10.7 %collective-permute-done.1.refs_1_ = bf16[256,896]{1,0:T(8,128)(2,1)S(1)} collective-permute-done((bf16[256,896]{1,0:T(8,128)(2,1)}, bf16[256,896]{1,0:T(8,128)(2,1)S(1)}, u32[]{:S(2)}, u32[]{:S(2)}) %collective-permute-start.1) | collective-permute-done | bytes 458784 | tf_op jit(solution)/shard_map/ppermute | solution.py:249
  15.4 1.8 %collective-permute-start.3 = (bf16[128,256]{1,0:T(8,128)(2,1)S(1)}, bf16[128,256]{1,0:T(8,128)(2,1)S(1)}, u32[]{:S(2)}, u32[]{:S(2)}) collective-permute-start(bf16[128,256]{1,0:T(8,128)(2,1)S(1)} %get-tuple-element.40), channel_id=1, source_target_pairs={{0,4},{4,0},{8,12},{12,8},{16,20},{20,16},{24,28},{28,24},{1,5},{5... | collective-permute-start | bytes 196616 | tf_op jit(solution)/shard_map/ppermute | solution.py:249
  17.2 1.6 %collective-permute-start.4 = (bf16[128,256]{1,0:T(8,128)(2,1)S(1)}, bf16[128,256]{1,0:T(8,128)(2,1)S(1)}, u32[]{:S(2)}, u32[]{:S(2)}) collective-permute-start(bf16[128,256]{1,0:T(8,128)(2,1)S(1)} %get-tuple-element.41), channel_id=1, source_target_pairs={{0,8},{4,12},{8,0},{12,4},{16,24},{20,28},{24,16},{28,20},{1,9},{5... | collective-permute-start | bytes 196616 | tf_op jit(solution)/shard_map/ppermute | solution.py:249
  20.0 2.8 %collective-permute-start.6 = (bf16[128,256]{1,0:T(8,128)(2,1)S(1)}, bf16[128,256]{1,0:T(8,128)(2,1)S(1)}, u32[]{:S(2)}, u32[]{:S(2)}) collective-permute-start(bf16[128,256]{1,0:T(8,128)(2,1)S(1)} %get-tuple-element.43), channel_id=1, source_target_pairs={{0,16},{4,20},{8,24},{12,28},{16,0},{20,4},{24,8},{28,12},{1,17},{... | collective-permute-start | bytes 196616 | tf_op jit(solution)/shard_map/ppermute | solution.py:249
  24.1 3.6 %collective-permute-start.8 = (bf16[128,256]{1,0:T(8,128)(2,1)S(1)}, bf16[128,256]{1,0:T(8,128)(2,1)S(1)}, u32[]{:S(2)}, u32[]{:S(2)}) collective-permute-start(bf16[128,256]{1,0:T(8,128)(2,1)S(1)} %get-tuple-element.45), channel_id=1, source_target_pairs={{0,24},{4,28},{8,16},{12,20},{16,8},{20,12},{24,0},{28,4},{1,25},{... | collective-permute-start | bytes 196616 | tf_op jit(solution)/shard_map/ppermute | solution.py:249
  27.7 1.3 %collective-permute-start.9 = (bf16[128,256]{1,0:T(8,128)(2,1)S(1)}, bf16[128,256]{1,0:T(8,128)(2,1)S(1)}, u32[]{:S(2)}, u32[]{:S(2)}) collective-permute-start(bf16[128,256]{1,0:T(8,128)(2,1)S(1)} %get-tuple-element.46), channel_id=1, source_target_pairs={{0,28},{4,24},{8,20},{12,16},{16,12},{20,8},{24,4},{28,0},{1,29},{... | collective-permute-start | bytes 196616 | tf_op jit(solution)/shard_map/ppermute | solution.py:249
  29.0 2.7 %kv.1 = (f32[256,128]{1,0:T(8,128)S(1)}, f32[256,128]{1,0:T(8,128)S(1)}, bf16[256,896]{1,0:T(8,128)(2,1)S(1)}, bf16[896,128]{1,0:T(8,128)(2,1)S(1)}, bf16[896,128]{1,0:T(8,128)(2,1)S(1)}) custom-call(s32[1]{0:T(128)} %bitcast.me_ref, bf16[256,896]{1,0:T(8,128)(2,1)} %own_hbm.1, bf16[256,896]{1,0:T(8,128)(2,1)S(1)} %collective-permute-done.refs_0_, ...), custom_call_target="tpu_custom_call" | custom-call | flops 400000000 | bytes 3000000 | tf_op jit(solution)/shard_map/kv/pallas_call | solution.py:303
  32.7 1.5 %collective-permute-start.14 = (bf16[256,896]{1,0:T(8,128)(2,1)}, bf16[256,896]{1,0:T(8,128)(2,1)S(1)}, u32[]{:S(2)}, u32[]{:S(2)}) collective-permute-start(bf16[256,896]{1,0:T(8,128)(2,1)} %refs_0_.1), channel_id=1, source_target_pairs={{0,2},{1,3},{2,0},{3,1},{4,6},{5,7},{6,4},{7,5},{8,10},{9,11},{10,... | collective-permute-start | bytes 1376264 | tf_op jit(solution)/shard_map/ppermute | solution.py:249
  34.8 4.1 %forward.1 = (bf16[256,896]{1,0:T(8,128)(2,1)S(1)}, bf16[1280,1792]{1,0:T(8,128)(2,1)S(1)}, f32[8,256]{1,0:T(8,128)S(1)}, bf16[1280,128]{1,0:T(8,128)(2,1)S(1)}) custom-call(bf16[896,128]{1,0:T(8,128)(2,1)S(1)} %get-tuple-element.34.wk_ref, bf16[896,128]{1,0:T(8,128)(2,1)S(1)} %get-tuple-element.35.wv_ref, ...), custom_call_target="tpu_custom_call" | custom-call | flops 5000000000 | bytes 10000000 | tf_op jit(solution)/shard_map/forward/pallas_call | solution.py:320
  40.2 4.7 %collective-permute-done.14.refs_2_ = bf16[256,896]{1,0:T(8,128)(2,1)S(1)} collective-permute-done((bf16[256,896]{1,0:T(8,128)(2,1)}, bf16[256,896]{1,0:T(8,128)(2,1)S(1)}, u32[]{:S(2)}, u32[]{:S(2)}) %collective-permute-start.14) | collective-permute-done | bytes 458784 | tf_op jit(solution)/shard_map/ppermute | solution.py:249
  44.9 1.6 %grad.1.part_ref = f32[896,256]{1,0:T(8,128)S(1)} custom-call(s32[1]{0:T(128)} %bitcast.me_ref, bf16[896,3584]{1,0:T(8,128)(2,1)S(1)} %bitcast.3, bf16[256,896]{1,0:T(8,128)(2,1)S(1)} %copy-done, bf16[256,896]{1,0:T(8,128)(2,1)S(1)} %collective-permute-done.13.refs_1_, bf16[256,896]{1,0:T(8,128)(2,1)S(1)} %collective-permute-done.14.refs_2_), custom_call_target="tpu_custom_call" | custom-call | flops 1500000000 | bytes 8000000 | tf_op jit(solution)/shard_map/grad/pallas_call | solution.py:341
  48.5 1.6 %collective-permute-start.12 = (bf16[256,896]{1,0:T(8,128)(2,1)S(1)}, bf16[256,896]{1,0:T(8,128)(2,1)S(1)}, u32[]{:S(2)}, u32[]{:S(2)}) collective-permute-start(bf16[256,896]{1,0:T(8,128)(2,1)S(1)} %add_convert_fusion.1), channel_id=1, source_target_pairs={{0,2},{1,3},{2,0},{3,1},{4,6},{5,7},{6,4},{7,5},{8,10},{9,11},{10,... | collective-permute-start | bytes 1376264 | tf_op jit(solution)/shard_map/ppermute | solution.py:249
  50.1 5.7 %backward.1 = (bf16[128,256]{1,0:T(8,128)(2,1)S(1)}, bf16[128,256]{1,0:T(8,128)(2,1)S(1)}, bf16[128,256]{1,0:T(8,128)(2,1)S(1)}, bf16[128,256]{1,0:T(8,128)(2,1)...) custom-call(s32[1]{0:T(128)} %bitcast.me_ref, ...), custom_call_target="tpu_custom_call" | custom-call | flops 7000000000 | bytes 10000000 | tf_op jit(solution)/shard_map/backward/pallas_call | solution.py:370
  56.3 1.3 %collective-permute-start.17 = (bf16[128,256]{1,0:T(8,128)(2,1)S(1)}, bf16[128,256]{1,0:T(8,128)(2,1)S(1)}, u32[]{:S(2)}, u32[]{:S(2)}) collective-permute-start(bf16[128,256]{1,0:T(8,128)(2,1)S(1)} %get-tuple-element.57), channel_id=1, source_target_pairs={{0,8},{4,12},{8,0},{12,4},{16,24},{20,28},{24,16},{28,20},{1,9},{5... | collective-permute-start | bytes 196616 | tf_op jit(solution)/shard_map/ppermute | solution.py:249
  57.6 1.8 %collective-permute-start.18 = (bf16[128,256]{1,0:T(8,128)(2,1)S(1)}, bf16[128,256]{1,0:T(8,128)(2,1)S(1)}, u32[]{:S(2)}, u32[]{:S(2)}) collective-permute-start(bf16[128,256]{1,0:T(8,128)(2,1)S(1)} %get-tuple-element.58), channel_id=1, source_target_pairs={{0,12},{4,8},{8,4},{12,0},{16,28},{20,24},{24,20},{28,16},{1,13},{... | collective-permute-start | bytes 196616 | tf_op jit(solution)/shard_map/ppermute | solution.py:249
  60.1 1.8 %collective-permute-start.19 = (bf16[128,256]{1,0:T(8,128)(2,1)S(1)}, bf16[128,256]{1,0:T(8,128)(2,1)S(1)}, u32[]{:S(2)}, u32[]{:S(2)}) collective-permute-start(bf16[128,256]{1,0:T(8,128)(2,1)S(1)} %get-tuple-element.59), channel_id=1, source_target_pairs={{0,16},{4,20},{8,24},{12,28},{16,0},{20,4},{24,8},{28,12},{1,17},{... | collective-permute-start | bytes 196616 | tf_op jit(solution)/shard_map/ppermute | solution.py:249
  61.9 2.9 %collective-permute-start.20 = (bf16[128,256]{1,0:T(8,128)(2,1)S(1)}, bf16[128,256]{1,0:T(8,128)(2,1)S(1)}, u32[]{:S(2)}, u32[]{:S(2)}) collective-permute-start(bf16[128,256]{1,0:T(8,128)(2,1)S(1)} %get-tuple-element.60), channel_id=1, source_target_pairs={{0,20},{4,16},{8,28},{12,24},{16,4},{20,0},{24,12},{28,8},{1,21},{... | collective-permute-start | bytes 196616 | tf_op jit(solution)/shard_map/ppermute | solution.py:249
  64.8 1.7 %collective-permute-start.21 = (bf16[128,256]{1,0:T(8,128)(2,1)S(1)}, bf16[128,256]{1,0:T(8,128)(2,1)S(1)}, u32[]{:S(2)}, u32[]{:S(2)}) collective-permute-start(bf16[128,256]{1,0:T(8,128)(2,1)S(1)} %get-tuple-element.61), channel_id=1, source_target_pairs={{0,24},{4,28},{8,16},{12,20},{16,8},{20,12},{24,0},{28,4},{1,25},{... | collective-permute-start | bytes 196616 | tf_op jit(solution)/shard_map/ppermute | solution.py:249
  66.5 2.3 %collective-permute-done.19.refs_4_ = bf16[128,256]{1,0:T(8,128)(2,1)S(1)} collective-permute-done((bf16[128,256]{1,0:T(8,128)(2,1)S(1)}, bf16[128,256]{1,0:T(8,128)(2,1)S(1)}, u32[]{:S(2)}, u32[]{:S(2)}) %collective-permute-start.19) | collective-permute-done | bytes 65568 | tf_op jit(solution)/shard_map/ppermute | solution.py:249
  68.8 1.7 %collective-permute-start.22 = (bf16[128,256]{1,0:T(8,128)(2,1)S(1)}, bf16[128,256]{1,0:T(8,128)(2,1)S(1)}, u32[]{:S(2)}, u32[]{:S(2)}) collective-permute-start(bf16[128,256]{1,0:T(8,128)(2,1)S(1)} %get-tuple-element.62), channel_id=1, source_target_pairs={{0,28},{4,24},{8,20},{12,16},{16,12},{20,8},{24,4},{28,0},{1,29},{... | collective-permute-start | bytes 196616 | tf_op jit(solution)/shard_map/ppermute | solution.py:249
  70.5 1.6 %collective-permute-done.20.refs_5_ = bf16[128,256]{1,0:T(8,128)(2,1)S(1)} collective-permute-done((bf16[128,256]{1,0:T(8,128)(2,1)S(1)}, bf16[128,256]{1,0:T(8,128)(2,1)S(1)}, u32[]{:S(2)}, u32[]{:S(2)}) %collective-permute-start.20) | collective-permute-done | bytes 65568 | tf_op jit(solution)/shard_map/ppermute | solution.py:249
  72.1 3.6 %collective-permute-done.22.refs_7_ = bf16[128,256]{1,0:T(8,128)(2,1)S(1)} collective-permute-done((bf16[128,256]{1,0:T(8,128)(2,1)S(1)}, bf16[128,256]{1,0:T(8,128)(2,1)S(1)}, u32[]{:S(2)}, u32[]{:S(2)}) %collective-permute-start.22) | collective-permute-done | bytes 65568 | tf_op jit(solution)/shard_map/ppermute | solution.py:249
  75.8 1.5 %place.1 = (f32[256,128]{1,0:T(8,128)}, f32[256,128]{1,0:T(8,128)}) custom-call(s32[1]{0:T(128)} %bitcast.1.me_ref, s32[8,16]{1,0:T(8,128)S(1)} %copy-done.1, bf16[128,256]{1,0:T(8,128)(2,1)S(1)} %get-tuple-element.55.refs_0_, bf16[128,256]{1,0:T(8,128)(2,1)S(1)} %collective-permute-done.16.refs_1_, bf16[128,256]{1,0:T(8,128)(2,1)S(1)} %collective-permute-done.17.refs_2_, ...), custom_call_target="tpu_custom_call" | custom-call | bytes 1048576 | tf_op jit(solution)/shard_map/place/pallas_call | solution.py:390
  (41 shorter events, 10.6 us)
Async XLA Ops:
  0.6 13.8 %collective-permute-start.1 = (bf16[256,896]{1,0:T(8,128)(2,1)}, bf16[256,896]{1,0:T(8,128)(2,1)S(1)}, u32[]{:S(2)}, u32[]{:S(2)}) collective-permute-start(bf16[256,896]{1,0:T(8,128)(2,1)} %own_hbm.1), channel_id=1, source_target_pairs={{0,2},{1,3},{2,0},{3,1},{4,6},{5,7},{6,4},{7,5},{8,10},{9,11},{10,... | collective-permute-start | bytes 1376264 | tf_op jit(solution)/shard_map/ppermute | solution.py:249
  3.7 24.0 %collective-permute-start = (bf16[256,896]{1,0:T(8,128)(2,1)}, bf16[256,896]{1,0:T(8,128)(2,1)S(1)}, u32[]{:S(2)}, u32[]{:S(2)}) collective-permute-start(bf16[256,896]{1,0:T(8,128)(2,1)} %own_hbm.1), channel_id=1, source_target_pairs={{0,1},{1,0},{2,3},{3,2},{4,5},{5,4},{6,7},{7,6},{8,9},{9,8},{10,11... | collective-permute-start | bytes 1376264 | tf_op jit(solution)/shard_map/ppermute | solution.py:249
  14.4 20.3 %collective-permute-start.2 = (bf16[256,896]{1,0:T(8,128)(2,1)S(1)}, bf16[256,896]{1,0:T(8,128)(2,1)S(1)}, u32[]{:S(2)}, u32[]{:S(2)}) collective-permute-start(bf16[256,896]{1,0:T(8,128)(2,1)S(1)} %collective-permute-done.1.refs_1_), channel_id=1, source_target_pairs={{0,1},{1,0},{2,3},{3,2},{4,5},{5,4},{6,7},{7,6},{8,9},{9,8},{10,11... | collective-permute-start | bytes 1376264 | tf_op jit(solution)/shard_map/ppermute | solution.py:249
  15.4 4.6 %collective-permute-start.3 = (bf16[128,256]{1,0:T(8,128)(2,1)S(1)}, bf16[128,256]{1,0:T(8,128)(2,1)S(1)}, u32[]{:S(2)}, u32[]{:S(2)}) collective-permute-start(bf16[128,256]{1,0:T(8,128)(2,1)S(1)} %get-tuple-element.40), channel_id=1, source_target_pairs={{0,4},{4,0},{8,12},{12,8},{16,20},{20,16},{24,28},{28,24},{1,5},{5... | collective-permute-start | bytes 196616 | tf_op jit(solution)/shard_map/ppermute | solution.py:249
  17.2 5.6 %collective-permute-start.4 = (bf16[128,256]{1,0:T(8,128)(2,1)S(1)}, bf16[128,256]{1,0:T(8,128)(2,1)S(1)}, u32[]{:S(2)}, u32[]{:S(2)}) collective-permute-start(bf16[128,256]{1,0:T(8,128)(2,1)S(1)} %get-tuple-element.41), channel_id=1, source_target_pairs={{0,8},{4,12},{8,0},{12,4},{16,24},{20,28},{24,16},{28,20},{1,9},{5... | collective-permute-start | bytes 196616 | tf_op jit(solution)/shard_map/ppermute | solution.py:249
  18.8 5.3 %collective-permute-start.5 = (bf16[128,256]{1,0:T(8,128)(2,1)S(1)}, bf16[128,256]{1,0:T(8,128)(2,1)S(1)}, u32[]{:S(2)}, u32[]{:S(2)}) collective-permute-start(bf16[128,256]{1,0:T(8,128)(2,1)S(1)} %get-tuple-element.42), channel_id=1, source_target_pairs={{0,12},{4,8},{8,4},{12,0},{16,28},{20,24},{24,20},{28,16},{1,13},{... | collective-permute-start | bytes 196616 | tf_op jit(solution)/shard_map/ppermute | solution.py:249
  20.0 11.6 %collective-permute-start.6 = (bf16[128,256]{1,0:T(8,128)(2,1)S(1)}, bf16[128,256]{1,0:T(8,128)(2,1)S(1)}, u32[]{:S(2)}, u32[]{:S(2)}) collective-permute-start(bf16[128,256]{1,0:T(8,128)(2,1)S(1)} %get-tuple-element.43), channel_id=1, source_target_pairs={{0,16},{4,20},{8,24},{12,28},{16,0},{20,4},{24,8},{28,12},{1,17},{... | collective-permute-start | bytes 196616 | tf_op jit(solution)/shard_map/ppermute | solution.py:249
  22.8 9.9 %collective-permute-start.7 = (bf16[128,256]{1,0:T(8,128)(2,1)S(1)}, bf16[128,256]{1,0:T(8,128)(2,1)S(1)}, u32[]{:S(2)}, u32[]{:S(2)}) collective-permute-start(bf16[128,256]{1,0:T(8,128)(2,1)S(1)} %get-tuple-element.44), channel_id=1, source_target_pairs={{0,20},{4,16},{8,28},{12,24},{16,4},{20,0},{24,12},{28,8},{1,21},{... | collective-permute-start | bytes 196616 | tf_op jit(solution)/shard_map/ppermute | solution.py:249
  24.1 10.1 %collective-permute-start.8 = (bf16[128,256]{1,0:T(8,128)(2,1)S(1)}, bf16[128,256]{1,0:T(8,128)(2,1)S(1)}, u32[]{:S(2)}, u32[]{:S(2)}) collective-permute-start(bf16[128,256]{1,0:T(8,128)(2,1)S(1)} %get-tuple-element.45), channel_id=1, source_target_pairs={{0,24},{4,28},{8,16},{12,20},{16,8},{20,12},{24,0},{28,4},{1,25},{... | collective-permute-start | bytes 196616 | tf_op jit(solution)/shard_map/ppermute | solution.py:249
  27.7 7.1 %collective-permute-start.9 = (bf16[128,256]{1,0:T(8,128)(2,1)S(1)}, bf16[128,256]{1,0:T(8,128)(2,1)S(1)}, u32[]{:S(2)}, u32[]{:S(2)}) collective-permute-start(bf16[128,256]{1,0:T(8,128)(2,1)S(1)} %get-tuple-element.46), channel_id=1, source_target_pairs={{0,28},{4,24},{8,20},{12,16},{16,12},{20,8},{24,4},{28,0},{1,29},{... | collective-permute-start | bytes 196616 | tf_op jit(solution)/shard_map/ppermute | solution.py:249
  31.7 13.2 %collective-permute-start.13 = (bf16[256,896]{1,0:T(8,128)(2,1)}, bf16[256,896]{1,0:T(8,128)(2,1)S(1)}, u32[]{:S(2)}, u32[]{:S(2)}) collective-permute-start(bf16[256,896]{1,0:T(8,128)(2,1)} %refs_0_.1), channel_id=1, source_target_pairs={{0,1},{1,0},{2,3},{3,2},{4,5},{5,4},{6,7},{7,6},{8,9},{9,8},{10,11... | collective-permute-start | bytes 1376264 | tf_op jit(solution)/shard_map/ppermute | solution.py:249
  32.7 12.2 %collective-permute-start.14 = (bf16[256,896]{1,0:T(8,128)(2,1)}, bf16[256,896]{1,0:T(8,128)(2,1)S(1)}, u32[]{:S(2)}, u32[]{:S(2)}) collective-permute-start(bf16[256,896]{1,0:T(8,128)(2,1)} %refs_0_.1), channel_id=1, source_target_pairs={{0,2},{1,3},{2,0},{3,1},{4,6},{5,7},{6,4},{7,5},{8,10},{9,11},{10,... | collective-permute-start | bytes 1376264 | tf_op jit(solution)/shard_map/ppermute | solution.py:249
  40.1 8.2 %collective-permute-start.11 = (bf16[256,896]{1,0:T(8,128)(2,1)S(1)}, bf16[256,896]{1,0:T(8,128)(2,1)S(1)}, u32[]{:S(2)}, u32[]{:S(2)}) collective-permute-start(bf16[256,896]{1,0:T(8,128)(2,1)S(1)} %get-tuple-element.51), channel_id=1, source_target_pairs={{0,1},{1,0},{2,3},{3,2},{4,5},{5,4},{6,7},{7,6},{8,9},{9,8},{10,11... | collective-permute-start | bytes 1376264 | tf_op jit(solution)/shard_map/ppermute | solution.py:249
  44.9 5.2 %collective-permute-start.15 = (bf16[256,896]{1,0:T(8,128)(2,1)S(1)}, bf16[256,896]{1,0:T(8,128)(2,1)S(1)}, u32[]{:S(2)}, u32[]{:S(2)}) collective-permute-start(bf16[256,896]{1,0:T(8,128)(2,1)S(1)} %collective-permute-done.14.refs_2_), channel_id=1, source_target_pairs={{0,1},{1,0},{2,3},{3,2},{4,5},{5,4},{6,7},{7,6},{8,9},{9,8},{10,11... | collective-permute-start | bytes 1376264 | tf_op jit(solution)/shard_map/ppermute | solution.py:249
  47.8 29.5 %collective-permute-start.10 = (bf16[256,896]{1,0:T(8,128)(2,1)S(1)}, bf16[256,896]{1,0:T(8,128)(2,1)S(1)}, u32[]{:S(2)}, u32[]{:S(2)}) collective-permute-start(bf16[256,896]{1,0:T(8,128)(2,1)S(1)} %get-tuple-element.49), channel_id=1, source_target_pairs={{0,1},{1,0},{2,3},{3,2},{4,5},{5,4},{6,7},{7,6},{8,9},{9,8},{10,11... | collective-permute-start | bytes 1376264 | tf_op jit(solution)/shard_map/ppermute | solution.py:249
  48.5 28.8 %collective-permute-start.12 = (bf16[256,896]{1,0:T(8,128)(2,1)S(1)}, bf16[256,896]{1,0:T(8,128)(2,1)S(1)}, u32[]{:S(2)}, u32[]{:S(2)}) collective-permute-start(bf16[256,896]{1,0:T(8,128)(2,1)S(1)} %add_convert_fusion.1), channel_id=1, source_target_pairs={{0,2},{1,3},{2,0},{3,1},{4,6},{5,7},{6,4},{7,5},{8,10},{9,11},{10,... | collective-permute-start | bytes 1376264 | tf_op jit(solution)/shard_map/ppermute | solution.py:249
  50.1 25.7 %copy-start.1 = (s32[8,16]{1,0:T(8,128)S(1)}, s32[8,16]{1,0:T(8,128)}, u32[]{:S(2)}) copy-start(s32[8,16]{1,0:T(8,128)} %reads_ref.1) | copy-start | bytes 1540
  55.8 4.3 %collective-permute-start.16 = (bf16[128,256]{1,0:T(8,128)(2,1)S(1)}, bf16[128,256]{1,0:T(8,128)(2,1)S(1)}, u32[]{:S(2)}, u32[]{:S(2)}) collective-permute-start(bf16[128,256]{1,0:T(8,128)(2,1)S(1)} %get-tuple-element.56), channel_id=1, source_target_pairs={{0,4},{4,0},{8,12},{12,8},{16,20},{20,16},{24,28},{28,24},{1,5},{5... | collective-permute-start | bytes 196616 | tf_op jit(solution)/shard_map/ppermute | solution.py:249
  56.3 5.6 %collective-permute-start.17 = (bf16[128,256]{1,0:T(8,128)(2,1)S(1)}, bf16[128,256]{1,0:T(8,128)(2,1)S(1)}, u32[]{:S(2)}, u32[]{:S(2)}) collective-permute-start(bf16[128,256]{1,0:T(8,128)(2,1)S(1)} %get-tuple-element.57), channel_id=1, source_target_pairs={{0,8},{4,12},{8,0},{12,4},{16,24},{20,28},{24,16},{28,20},{1,9},{5... | collective-permute-start | bytes 196616 | tf_op jit(solution)/shard_map/ppermute | solution.py:249
  57.6 7.2 %collective-permute-start.18 = (bf16[128,256]{1,0:T(8,128)(2,1)S(1)}, bf16[128,256]{1,0:T(8,128)(2,1)S(1)}, u32[]{:S(2)}, u32[]{:S(2)}) collective-permute-start(bf16[128,256]{1,0:T(8,128)(2,1)S(1)} %get-tuple-element.58), channel_id=1, source_target_pairs={{0,12},{4,8},{8,4},{12,0},{16,28},{20,24},{24,20},{28,16},{1,13},{... | collective-permute-start | bytes 196616 | tf_op jit(solution)/shard_map/ppermute | solution.py:249
  60.1 8.7 %collective-permute-start.19 = (bf16[128,256]{1,0:T(8,128)(2,1)S(1)}, bf16[128,256]{1,0:T(8,128)(2,1)S(1)}, u32[]{:S(2)}, u32[]{:S(2)}) collective-permute-start(bf16[128,256]{1,0:T(8,128)(2,1)S(1)} %get-tuple-element.59), channel_id=1, source_target_pairs={{0,16},{4,20},{8,24},{12,28},{16,0},{20,4},{24,8},{28,12},{1,17},{... | collective-permute-start | bytes 196616 | tf_op jit(solution)/shard_map/ppermute | solution.py:249
  61.9 10.3 %collective-permute-start.20 = (bf16[128,256]{1,0:T(8,128)(2,1)S(1)}, bf16[128,256]{1,0:T(8,128)(2,1)S(1)}, u32[]{:S(2)}, u32[]{:S(2)}) collective-permute-start(bf16[128,256]{1,0:T(8,128)(2,1)S(1)} %get-tuple-element.60), channel_id=1, source_target_pairs={{0,20},{4,16},{8,28},{12,24},{16,4},{20,0},{24,12},{28,8},{1,21},{... | collective-permute-start | bytes 196616 | tf_op jit(solution)/shard_map/ppermute | solution.py:249
  64.8 7.4 %collective-permute-start.21 = (bf16[128,256]{1,0:T(8,128)(2,1)S(1)}, bf16[128,256]{1,0:T(8,128)(2,1)S(1)}, u32[]{:S(2)}, u32[]{:S(2)}) collective-permute-start(bf16[128,256]{1,0:T(8,128)(2,1)S(1)} %get-tuple-element.61), channel_id=1, source_target_pairs={{0,24},{4,28},{8,16},{12,20},{16,8},{20,12},{24,0},{28,4},{1,25},{... | collective-permute-start | bytes 196616 | tf_op jit(solution)/shard_map/ppermute | solution.py:249
  68.8 7.0 %collective-permute-start.22 = (bf16[128,256]{1,0:T(8,128)(2,1)S(1)}, bf16[128,256]{1,0:T(8,128)(2,1)S(1)}, u32[]{:S(2)}, u32[]{:S(2)}) collective-permute-start(bf16[128,256]{1,0:T(8,128)(2,1)S(1)} %get-tuple-element.62), channel_id=1, source_target_pairs={{0,28},{4,24},{8,20},{12,16},{16,12},{20,8},{24,4},{28,0},{1,29},{... | collective-permute-start | bytes 196616 | tf_op jit(solution)/shard_map/ppermute | solution.py:249
  (3 other events, 20.0 us)

commit v8 on v3

--- a/solution.py
+++ b/solution.py
@@ -69,8 +69,8 @@
     return [pltpu.make_async_copy(w.at[rows], buf.at[slot], sems.at[j, slot]) for j, (w, buf) in enumerate(zip(hbms, bufs))]
 
 
-def kv_kernel(order, last, me_ref, own_hbm, *refs):
-    hidden, (wk_hbm, wv_hbm, q_hbm, k_ref, v_ref, q_ref, lastk_ref, lastv_ref) = refs[:-13], refs[-13:-5]
+def kv_kernel(order, rest, me_ref, own_hbm, *refs):
+    hidden, (wk_hbm, wv_hbm, q_hbm, k_ref, v_ref, q_ref, restk_ref, restv_ref) = refs[:-13], refs[-13:-5]
     own_ref, wk_ref, wv_ref, sems, far_sems = refs[-5:]
     me = me_ref[0]
     width = own_ref.shape[1]
@@ -83,22 +83,22 @@
             copy.start()
     own = pltpu.make_async_copy(own_hbm, own_ref, far_sems.at[0])
     own.start()
-    rows = pl.ds(pl.multiple_of((me ^ last) * width, width), width)
-    later = [
-        pltpu.make_async_copy(q_hbm, q_ref, far_sems.at[1]),
-        pltpu.make_async_copy(wk_hbm.at[rows], lastk_ref, far_sems.at[2]),
-        pltpu.make_async_copy(wv_hbm.at[rows], lastv_ref, far_sems.at[3]),
-    ]
+    later = [pltpu.make_async_copy(q_hbm, q_ref, far_sems.at[1])]
+    for slot, i in enumerate(rest):
+        rows = pl.ds(pl.multiple_of((me ^ i) * width, width), width)
+        later.append(pltpu.make_async_copy(wk_hbm.at[rows], restk_ref.at[slot], far_sems.at[2 + 2 * slot]))
+        later.append(pltpu.make_async_copy(wv_hbm.at[rows], restv_ref.at[slot], far_sems.at[3 + 2 * slot]))
     for copy in later:
         copy.start()
     new_k = jnp.zeros(k_ref.shape, F32)
     new_v = jnp.zeros(k_ref.shape, F32)
+    pieces = iter(hidden)
     for slot, i in enumerate(order):
         for copy in fetch(slot, i):
             copy.wait()
         if i == 0:
             own.wait()
-        piece = hidden[i - 1][...] if i else own_ref[...]
+        piece = next(pieces)[...] if i else own_ref[...]
         new_k += dot(piece, wk_ref[slot], ((1,), (0,)))
         new_v += dot(piece, wv_ref[slot], ((1,), (0,)))
     k_ref[...] = new_k
@@ -107,10 +107,11 @@
         copy.wait()
 
 
-def forward_kernel(n_pre, scaling, wk_ref, wv_ref, hidden_ref, q_ref, partk_ref, partv_ref, *refs):
+def forward_kernel(n_rest, n_pre, scaling, wk_ref, wv_ref, *refs):
+    hidden, (q_ref, partk_ref, partv_ref), refs = refs[:n_rest], refs[n_rest:n_rest + 3], refs[n_rest + 3:]
     prefix = refs[:n_pre]
     ctx_ref, exps_ref, row_ref, v_all, k_all, vt_all, s_buf, sums = refs[n_pre:]
-    length = hidden_ref.shape[0]
+    length = q_ref.shape[0]
     heads = q_ref.shape[1] // HD
     factor = scaling * LOG2E
     at = 0
@@ -119,9 +120,12 @@
         k_all[at:at + size, :] = ref[:, :HD]
         v_all[at:at + size, :] = ref[:, HD:]
         at += size
-    piece = hidden_ref[...]
-    k_all[at:, :] = (partk_ref[...] + dot(piece, wk_ref[...], ((1,), (0,)))).astype(BF16)
-    v_all[at:, :] = (partv_ref[...] + dot(piece, wv_ref[...], ((1,), (0,)))).astype(BF16)
+    new_k, new_v = partk_ref[...], partv_ref[...]
+    for slot, ref in enumerate(hidden):
+        new_k += dot(ref[...], wk_ref[slot], ((1,), (0,)))
+        new_v += dot(ref[...], wv_ref[slot], ((1,), (0,)))
+    k_all[at:, :] = new_k.astype(BF16)
+    v_all[at:, :] = new_v.astype(BF16)
     vt_all[...] = v_all[...].astype(F32).T.astype(BF16)
     visible = lax.broadcasted_iota(jnp.int32, (length, length), 0) <= lax.broadcasted_iota(
         jnp.int32, (length, length), 1)
@@ -289,33 +293,34 @@
     n_pre = len(prefix)
 
     part = jax.ShapeDtypeStruct((length, HD), F32)
-    weight = jax.ShapeDtypeStruct((width, HD), BF16)
-    part_k, part_v, q, last_k, last_v = pl.pallas_call(
-        functools.partial(kv_kernel, (1, 0, 2), n_tp - 1),
+    n_rest = n_tp - 2
+    weight = jax.ShapeDtypeStruct((n_rest, width, HD), BF16)
+    part_k, part_v, q, rest_k, rest_v = pl.pallas_call(
+        functools.partial(kv_kernel, (2, 0), (1, 3)),
         out_shape=[part, part, jax.ShapeDtypeStruct(queries.shape, BF16), weight, weight],
-        in_specs=[SMEM, HBM] + [VMEM] * (n_tp - 2) + [HBM] * 3,
+        in_specs=[SMEM, HBM, VMEM] + [HBM] * 3,
         out_specs=[VMEM] * 5,
         scratch_shapes=[
             pltpu.VMEM((length, width), BF16),
-            pltpu.VMEM((n_tp - 1, width, HD), BF16),
-            pltpu.VMEM((n_tp - 1, width, HD), BF16),
-            pltpu.SemaphoreType.DMA((2, n_tp - 1)),
-            pltpu.SemaphoreType.DMA((4,)),
+            pltpu.VMEM((2, width, HD), BF16),
+            pltpu.VMEM((2, width, HD), BF16),
+            pltpu.SemaphoreType.DMA((2, 2)),
+            pltpu.SemaphoreType.DMA((2 + 2 * n_rest,)),
         ],
         compiler_params=grant(8),
         cost_estimate=cost(4e8, 3e6),
         name="kv",
-    )(me_tp, hbm(hidden_states), near_hidden, far_hidden, hbm(key_weight), hbm(value_weight), hbm(queries))
+    )(me_tp, hbm(hidden_states), far_hidden, hbm(key_weight), hbm(value_weight), hbm(queries))
 
     ctx, exps, row, v_all = pl.pallas_call(
-        functools.partial(forward_kernel, n_pre, scaling),
+        functools.partial(forward_kernel, n_rest, n_pre, scaling),
         out_shape=[
             jax.ShapeDtypeStruct((length, heads * HD), BF16),
             jax.ShapeDtypeStruct((keys, heads * length), BF16),
             jax.ShapeDtypeStruct((heads + (-heads) % 8, length), F32),
             jax.ShapeDtypeStruct((keys, HD), BF16),
         ],
-        in_specs=[VMEM] * (6 + n_pre),
+        in_specs=[VMEM] * (5 + n_rest + n_pre),
         out_specs=[VMEM] * 4,
         scratch_shapes=[
             pltpu.VMEM((keys, HD), BF16),
@@ -326,7 +331,7 @@
         compiler_params=grant(20),
         cost_estimate=cost(5e9, 1e7, 3e6),
         name="forward",
-    )(last_k, last_v, last_hidden, q, part_k, part_v, *prefix)
+    )(rest_k, rest_v, near_hidden, last_hidden, q, part_k, part_v, *prefix)
 
     part_grad = pl.pallas_call(
         functools.partial(grad_kernel, (0, 1, 2)),

time: 78.3 us -> 79.7 us (1.018)
  starting transfers between devices: 31 us -> 32.2 us
    ppermute x23, starting transfers between devices: 31 us -> 32.2 us  [hop(): return lax.ppermute(x, axis, [(i, i ^ k) for i in range(n)])]
  transfers between devices with their start and end apart: 23 -> 23, of which waited for: 9 -> 8; matrix products, arithmetic and copies ran while one was open for 0% -> 0% of each run, Pallas kernels for 24% -> 24%
where the time goes in v8:
time: 79.7 us; the launch traced here: 79.6 us
  starting transfers between devices  32.2 us (40%)
  waiting for transfers between devices  26.4 us (33%)
  Pallas kernels  19.1 us (24%)
  other arithmetic  1.06 us (1%)
    ppermute x23, starting transfers between devices, hop(): return lax.ppermute(x, axis, [(i, i ^ k) for i in range(n)])  32.2 us
    ppermute x23, waiting for transfers between devices, hop(): return lax.ppermute(x, axis, [(i, i ^ k) for i in range(n)])  26.4 us
    pallas_call x1, Pallas kernels, local(): pl.pallas_call(functools.partial(backward_kernel, n_tp - 1, n_pre, scalin...  5.73 us
    pallas_call x1, Pallas kernels, local(): pl.pallas_call(functools.partial(forward_kernel, n_rest, n_pre, scaling),...  4.34 us
    pallas_call x1, Pallas kernels, local(): pl.pallas_call(functools.partial(kv_kernel, (2, 0), (1, 3)), out_shape=[p...  2.51 us
    pallas_call x2, Pallas kernels, project(): pl.pallas_call(functools.partial(project_kernel, order), out_shape=[jax.S...  2.49 us
    pallas_call x1, Pallas kernels, local(): pl.pallas_call(functools.partial(grad_kernel, (0, 1, 2)), out_shape=jax.S...  1.62 us
  transfers between devices with their start and end apart: 23, of which 8 were waited for; matrix products, arithmetic and copies ran while one was open for 0% of the time, Pallas kernels for 24%

profile of v8, /device:TPU:0, one launch (start us, length us, event | category | flops | bytes accessed | tf_op | source)
XLA Modules:
  0.0 79.6 jit_solution(13925855719761102285)
XLA Ops:
  0.6 3.1 %collective-permute-start = (bf16[256,896]{1,0:T(8,128)(2,1)}, bf16[256,896]{1,0:T(8,128)(2,1)S(1)}, u32[]{:S(2)}, u32[]{:S(2)}) collective-permute-start(bf16[256,896]{1,0:T(8,128)(2,1)} %own_hbm.1), channel_id=1, source_target_pairs={{0,2},{1,3},{2,0},{3,1},{4,6},{5,7},{6,4},{7,5},{8,10},{9,11},{10,... | collective-permute-start | bytes 1376264 | tf_op jit(solution)/shard_map/ppermute | solution.py:243
  3.7 10.7 %collective-permute-done.refs_0_ = bf16[256,896]{1,0:T(8,128)(2,1)S(1)} collective-permute-done((bf16[256,896]{1,0:T(8,128)(2,1)}, bf16[256,896]{1,0:T(8,128)(2,1)S(1)}, u32[]{:S(2)}, u32[]{:S(2)}) %collective-permute-start) | collective-permute-done | bytes 458784 | tf_op jit(solution)/shard_map/ppermute | solution.py:243
  15.4 1.8 %collective-permute-start.3 = (bf16[128,256]{1,0:T(8,128)(2,1)S(1)}, bf16[128,256]{1,0:T(8,128)(2,1)S(1)}, u32[]{:S(2)}, u32[]{:S(2)}) collective-permute-start(bf16[128,256]{1,0:T(8,128)(2,1)S(1)} %get-tuple-element.40), channel_id=1, source_target_pairs={{0,4},{4,0},{8,12},{12,8},{16,20},{20,16},{24,28},{28,24},{1,5},{5... | collective-permute-start | bytes 196616 | tf_op jit(solution)/shard_map/ppermute | solution.py:243
  17.2 1.6 %collective-permute-start.4 = (bf16[128,256]{1,0:T(8,128)(2,1)S(1)}, bf16[128,256]{1,0:T(8,128)(2,1)S(1)}, u32[]{:S(2)}, u32[]{:S(2)}) collective-permute-start(bf16[128,256]{1,0:T(8,128)(2,1)S(1)} %get-tuple-element.41), channel_id=1, source_target_pairs={{0,8},{4,12},{8,0},{12,4},{16,24},{20,28},{24,16},{28,20},{1,9},{5... | collective-permute-start | bytes 196616 | tf_op jit(solution)/shard_map/ppermute | solution.py:243
  20.0 2.8 %collective-permute-start.6 = (bf16[128,256]{1,0:T(8,128)(2,1)S(1)}, bf16[128,256]{1,0:T(8,128)(2,1)S(1)}, u32[]{:S(2)}, u32[]{:S(2)}) collective-permute-start(bf16[128,256]{1,0:T(8,128)(2,1)S(1)} %get-tuple-element.43), channel_id=1, source_target_pairs={{0,16},{4,20},{8,24},{12,28},{16,0},{20,4},{24,8},{28,12},{1,17},{... | collective-permute-start | bytes 196616 | tf_op jit(solution)/shard_map/ppermute | solution.py:243
  22.8 1.3 %collective-permute-start.7 = (bf16[128,256]{1,0:T(8,128)(2,1)S(1)}, bf16[128,256]{1,0:T(8,128)(2,1)S(1)}, u32[]{:S(2)}, u32[]{:S(2)}) collective-permute-start(bf16[128,256]{1,0:T(8,128)(2,1)S(1)} %get-tuple-element.44), channel_id=1, source_target_pairs={{0,20},{4,16},{8,28},{12,24},{16,4},{20,0},{24,12},{28,8},{1,21},{... | collective-permute-start | bytes 196616 | tf_op jit(solution)/shard_map/ppermute | solution.py:243
  24.1 3.6 %collective-permute-start.8 = (bf16[128,256]{1,0:T(8,128)(2,1)S(1)}, bf16[128,256]{1,0:T(8,128)(2,1)S(1)}, u32[]{:S(2)}, u32[]{:S(2)}) collective-permute-start(bf16[128,256]{1,0:T(8,128)(2,1)S(1)} %get-tuple-element.45), channel_id=1, source_target_pairs={{0,24},{4,28},{8,16},{12,20},{16,8},{20,12},{24,0},{28,4},{1,25},{... | collective-permute-start | bytes 196616 | tf_op jit(solution)/shard_map/ppermute | solution.py:243
  27.7 5.1 %collective-permute-start.9 = (bf16[128,256]{1,0:T(8,128)(2,1)S(1)}, bf16[128,256]{1,0:T(8,128)(2,1)S(1)}, u32[]{:S(2)}, u32[]{:S(2)}) collective-permute-start(bf16[128,256]{1,0:T(8,128)(2,1)S(1)} %get-tuple-element.46), channel_id=1, source_target_pairs={{0,28},{4,24},{8,20},{12,16},{16,12},{20,8},{24,4},{28,0},{1,29},{... | collective-permute-start | bytes 196616 | tf_op jit(solution)/shard_map/ppermute | solution.py:243
  32.8 2.5 %kv.1 = (f32[256,128]{1,0:T(8,128)S(1)}, f32[256,128]{1,0:T(8,128)S(1)}, bf16[256,896]{1,0:T(8,128)(2,1)S(1)}, bf16[2,896,128]{2,1,0:T(8,128)(2,1)S(1)}, bf16[2,896,128]{2,1,0:T(8,128)(2,1)S(1)}) custom-call(s32[1]{0:T(128)} %bitcast.me_ref, bf16[256,896]{1,0:T(8,128)(2,1)} %own_hbm.1, bf16[256,896]{1,0:T(8,128)(2,1)S(1)} %collective-permute-done.refs_0_, ...), custom_call_target="tpu_custom_call" | custom-call | flops 400000000 | bytes 3000000 | tf_op jit(solution)/shard_map/kv/pallas_call | solution.py:298
  35.3 1.6 %collective-permute-start.14 = (bf16[256,896]{1,0:T(8,128)(2,1)}, bf16[256,896]{1,0:T(8,128)(2,1)S(1)}, u32[]{:S(2)}, u32[]{:S(2)}) collective-permute-start(bf16[256,896]{1,0:T(8,128)(2,1)} %refs_0_.1), channel_id=1, source_target_pairs={{0,2},{1,3},{2,0},{3,1},{4,6},{5,7},{6,4},{7,5},{8,10},{9,11},{10,... | collective-permute-start | bytes 1376264 | tf_op jit(solution)/shard_map/ppermute | solution.py:243
  37.0 4.3 %forward.1 = (bf16[256,896]{1,0:T(8,128)(2,1)S(1)}, bf16[1280,1792]{1,0:T(8,128)(2,1)S(1)}, f32[8,256]{1,0:T(8,128)S(1)}, bf16[1280,128]{1,0:T(8,128)(2,1)S(1)}) custom-call(bf16[2,896,128]{2,1,0:T(8,128)(2,1)S(1)} %get-tuple-element.34.wk_ref, bf16[2,896,128]{2,1,0:T(8,128)(2,1)S(1)} %get-tuple-element.35.wv_ref, ...), custom_call_target="tpu_custom_call" | custom-call | flops 5000000000 | bytes 10000000 | tf_op jit(solution)/shard_map/forward/pallas_call | solution.py:315
  41.3 1.2 %shard_map.113 = (bf16[256,896]{1,0:T(8,128)(2,1)S(1)}, bf16[256,896]{1,0:T(8,128)(2,1)S(1)}) custom-call(s32[1]{0:T(128)} %bitcast.me_ref, bf16[256,896]{1,0:T(8,128)(2,1)S(1)} %get-tuple-element.47.ctx_ref, bf16[896,3584]{1,0:T(8,128)(2,1)S(1)} %bitcast.3), custom_call_target="tpu_custom_call" | custom-call | flops 1000000000 | bytes 4000000 | tf_op jit(solution)/shard_map/pallas_call | solution.py:347
  43.1 4.5 %collective-permute-done.14.refs_2_ = bf16[256,896]{1,0:T(8,128)(2,1)S(1)} collective-permute-done((bf16[256,896]{1,0:T(8,128)(2,1)}, bf16[256,896]{1,0:T(8,128)(2,1)S(1)}, u32[]{:S(2)}, u32[]{:S(2)}) %collective-permute-start.14) | collective-permute-done | bytes 458784 | tf_op jit(solution)/shard_map/ppermute | solution.py:243
  47.7 1.6 %grad.1.part_ref = f32[896,256]{1,0:T(8,128)S(1)} custom-call(s32[1]{0:T(128)} %bitcast.me_ref, bf16[896,3584]{1,0:T(8,128)(2,1)S(1)} %bitcast.3, bf16[256,896]{1,0:T(8,128)(2,1)S(1)} %copy-done, bf16[256,896]{1,0:T(8,128)(2,1)S(1)} %collective-permute-done.13.refs_1_, bf16[256,896]{1,0:T(8,128)(2,1)S(1)} %collective-permute-done.14.refs_2_), custom_call_target="tpu_custom_call" | custom-call | flops 1500000000 | bytes 8000000 | tf_op jit(solution)/shard_map/grad/pallas_call | solution.py:336
  49.3 1.3 %shard_map.112 = (bf16[256,896]{1,0:T(8,128)(2,1)S(1)}, bf16[256,896]{1,0:T(8,128)(2,1)S(1)}) custom-call(s32[1]{0:T(128)} %bitcast.me_ref, bf16[256,896]{1,0:T(8,128)(2,1)S(1)} %get-tuple-element.47.ctx_ref, bf16[896,3584]{1,0:T(8,128)(2,1)S(1)} %bitcast.3), custom_call_target="tpu_custom_call" | custom-call | flops 1000000000 | bytes 4000000 | tf_op jit(solution)/shard_map/pallas_call | solution.py:347
  51.3 1.6 %collective-permute-start.12 = (bf16[256,896]{1,0:T(8,128)(2,1)S(1)}, bf16[256,896]{1,0:T(8,128)(2,1)S(1)}, u32[]{:S(2)}, u32[]{:S(2)}) collective-permute-start(bf16[256,896]{1,0:T(8,128)(2,1)S(1)} %add_convert_fusion.1), channel_id=1, source_target_pairs={{0,2},{1,3},{2,0},{3,1},{4,6},{5,7},{6,4},{7,5},{8,10},{9,11},{10,... | collective-permute-start | bytes 1376264 | tf_op jit(solution)/shard_map/ppermute | solution.py:243
  52.8 5.7 %backward.1 = (bf16[128,256]{1,0:T(8,128)(2,1)S(1)}, bf16[128,256]{1,0:T(8,128)(2,1)S(1)}, bf16[128,256]{1,0:T(8,128)(2,1)S(1)}, bf16[128,256]{1,0:T(8,128)(2,1)...) custom-call(s32[1]{0:T(128)} %bitcast.me_ref, ...), custom_call_target="tpu_custom_call" | custom-call | flops 7000000000 | bytes 10000000 | tf_op jit(solution)/shard_map/backward/pallas_call | solution.py:365
  58.7 3.4 %collective-permute-start.18 = (bf16[128,256]{1,0:T(8,128)(2,1)S(1)}, bf16[128,256]{1,0:T(8,128)(2,1)S(1)}, u32[]{:S(2)}, u32[]{:S(2)}) collective-permute-start(bf16[128,256]{1,0:T(8,128)(2,1)S(1)} %get-tuple-element.58), channel_id=1, source_target_pairs={{0,12},{4,8},{8,4},{12,0},{16,28},{20,24},{24,20},{28,16},{1,13},{... | collective-permute-start | bytes 196616 | tf_op jit(solution)/shard_map/ppermute | solution.py:243
  63.6 1.7 %collective-permute-start.20 = (bf16[128,256]{1,0:T(8,128)(2,1)S(1)}, bf16[128,256]{1,0:T(8,128)(2,1)S(1)}, u32[]{:S(2)}, u32[]{:S(2)}) collective-permute-start(bf16[128,256]{1,0:T(8,128)(2,1)S(1)} %get-tuple-element.60), channel_id=1, source_target_pairs={{0,20},{4,16},{8,28},{12,24},{16,4},{20,0},{24,12},{28,8},{1,21},{... | collective-permute-start | bytes 196616 | tf_op jit(solution)/shard_map/ppermute | solution.py:243
  65.3 2.1 %collective-permute-start.21 = (bf16[128,256]{1,0:T(8,128)(2,1)S(1)}, bf16[128,256]{1,0:T(8,128)(2,1)S(1)}, u32[]{:S(2)}, u32[]{:S(2)}) collective-permute-start(bf16[128,256]{1,0:T(8,128)(2,1)S(1)} %get-tuple-element.61), channel_id=1, source_target_pairs={{0,24},{4,28},{8,16},{12,20},{16,8},{20,12},{24,0},{28,4},{1,25},{... | collective-permute-start | bytes 196616 | tf_op jit(solution)/shard_map/ppermute | solution.py:243
  67.4 2.8 %collective-permute-done.19.refs_4_ = bf16[128,256]{1,0:T(8,128)(2,1)S(1)} collective-permute-done((bf16[128,256]{1,0:T(8,128)(2,1)S(1)}, bf16[128,256]{1,0:T(8,128)(2,1)S(1)}, u32[]{:S(2)}, u32[]{:S(2)}) %collective-permute-start.19) | collective-permute-done | bytes 65568 | tf_op jit(solution)/shard_map/ppermute | solution.py:243
  70.2 1.1 %collective-permute-start.22 = (bf16[128,256]{1,0:T(8,128)(2,1)S(1)}, bf16[128,256]{1,0:T(8,128)(2,1)S(1)}, u32[]{:S(2)}, u32[]{:S(2)}) collective-permute-start(bf16[128,256]{1,0:T(8,128)(2,1)S(1)} %get-tuple-element.62), channel_id=1, source_target_pairs={{0,28},{4,24},{8,20},{12,16},{16,12},{20,8},{24,4},{28,0},{1,29},{... | collective-permute-start | bytes 196616 | tf_op jit(solution)/shard_map/ppermute | solution.py:243
  72.0 5.1 %collective-permute-done.22.refs_7_ = bf16[128,256]{1,0:T(8,128)(2,1)S(1)} collective-permute-done((bf16[128,256]{1,0:T(8,128)(2,1)S(1)}, bf16[128,256]{1,0:T(8,128)(2,1)S(1)}, u32[]{:S(2)}, u32[]{:S(2)}) %collective-permute-start.22) | collective-permute-done | bytes 65568 | tf_op jit(solution)/shard_map/ppermute | solution.py:243
  77.2 1.4 %place.1 = (f32[256,128]{1,0:T(8,128)}, f32[256,128]{1,0:T(8,128)}) custom-call(s32[1]{0:T(128)} %bitcast.1.me_ref, s32[8,16]{1,0:T(8,128)S(1)} %copy-done.1, bf16[128,256]{1,0:T(8,128)(2,1)S(1)} %get-tuple-element.55.refs_0_, bf16[128,256]{1,0:T(8,128)(2,1)S(1)} %collective-permute-done.16.refs_1_, bf16[128,256]{1,0:T(8,128)(2,1)S(1)} %collective-permute-done.17.refs_2_, ...), custom_call_target="tpu_custom_call" | custom-call | bytes 1048576 | tf_op jit(solution)/shard_map/place/pallas_call | solution.py:385
  (41 shorter events, 6.8 us)
Async XLA Ops:
  0.6 13.8 %collective-permute-start = (bf16[256,896]{1,0:T(8,128)(2,1)}, bf16[256,896]{1,0:T(8,128)(2,1)S(1)}, u32[]{:S(2)}, u32[]{:S(2)}) collective-permute-start(bf16[256,896]{1,0:T(8,128)(2,1)} %own_hbm.1), channel_id=1, source_target_pairs={{0,2},{1,3},{2,0},{3,1},{4,6},{5,7},{6,4},{7,5},{8,10},{9,11},{10,... | collective-permute-start | bytes 1376264 | tf_op jit(solution)/shard_map/ppermute | solution.py:243
  3.7 33.2 %collective-permute-start.1 = (bf16[256,896]{1,0:T(8,128)(2,1)}, bf16[256,896]{1,0:T(8,128)(2,1)S(1)}, u32[]{:S(2)}, u32[]{:S(2)}) collective-permute-start(bf16[256,896]{1,0:T(8,128)(2,1)} %own_hbm.1), channel_id=1, source_target_pairs={{0,1},{1,0},{2,3},{3,2},{4,5},{5,4},{6,7},{7,6},{8,9},{9,8},{10,11... | collective-permute-start | bytes 1376264 | tf_op jit(solution)/shard_map/ppermute | solution.py:243
  14.4 22.5 %collective-permute-start.2 = (bf16[256,896]{1,0:T(8,128)(2,1)S(1)}, bf16[256,896]{1,0:T(8,128)(2,1)S(1)}, u32[]{:S(2)}, u32[]{:S(2)}) collective-permute-start(bf16[256,896]{1,0:T(8,128)(2,1)S(1)} %collective-permute-done.refs_0_), channel_id=1, source_target_pairs={{0,1},{1,0},{2,3},{3,2},{4,5},{5,4},{6,7},{7,6},{8,9},{9,8},{10,11... | collective-permute-start | bytes 1376264 | tf_op jit(solution)/shard_map/ppermute | solution.py:243
  15.4 4.6 %collective-permute-start.3 = (bf16[128,256]{1,0:T(8,128)(2,1)S(1)}, bf16[128,256]{1,0:T(8,128)(2,1)S(1)}, u32[]{:S(2)}, u32[]{:S(2)}) collective-permute-start(bf16[128,256]{1,0:T(8,128)(2,1)S(1)} %get-tuple-element.40), channel_id=1, source_target_pairs={{0,4},{4,0},{8,12},{12,8},{16,20},{20,16},{24,28},{28,24},{1,5},{5... | collective-permute-start | bytes 196616 | tf_op jit(solution)/shard_map/ppermute | solution.py:243
  17.2 5.6 %collective-permute-start.4 = (bf16[128,256]{1,0:T(8,128)(2,1)S(1)}, bf16[128,256]{1,0:T(8,128)(2,1)S(1)}, u32[]{:S(2)}, u32[]{:S(2)}) collective-permute-start(bf16[128,256]{1,0:T(8,128)(2,1)S(1)} %get-tuple-element.41), channel_id=1, source_target_pairs={{0,8},{4,12},{8,0},{12,4},{16,24},{20,28},{24,16},{28,20},{1,9},{5... | collective-permute-start | bytes 196616 | tf_op jit(solution)/shard_map/ppermute | solution.py:243
  18.8 5.3 %collective-permute-start.5 = (bf16[128,256]{1,0:T(8,128)(2,1)S(1)}, bf16[128,256]{1,0:T(8,128)(2,1)S(1)}, u32[]{:S(2)}, u32[]{:S(2)}) collective-permute-start(bf16[128,256]{1,0:T(8,128)(2,1)S(1)} %get-tuple-element.42), channel_id=1, source_target_pairs={{0,12},{4,8},{8,4},{12,0},{16,28},{20,24},{24,20},{28,16},{1,13},{... | collective-permute-start | bytes 196616 | tf_op jit(solution)/shard_map/ppermute | solution.py:243
  20.0 7.7 %collective-permute-start.6 = (bf16[128,256]{1,0:T(8,128)(2,1)S(1)}, bf16[128,256]{1,0:T(8,128)(2,1)S(1)}, u32[]{:S(2)}, u32[]{:S(2)}) collective-permute-start(bf16[128,256]{1,0:T(8,128)(2,1)S(1)} %get-tuple-element.43), channel_id=1, source_target_pairs={{0,16},{4,20},{8,24},{12,28},{16,0},{20,4},{24,8},{28,12},{1,17},{... | collective-permute-start | bytes 196616 | tf_op jit(solution)/shard_map/ppermute | solution.py:243
  22.8 12.5 %collective-permute-start.7 = (bf16[128,256]{1,0:T(8,128)(2,1)S(1)}, bf16[128,256]{1,0:T(8,128)(2,1)S(1)}, u32[]{:S(2)}, u32[]{:S(2)}) collective-permute-start(bf16[128,256]{1,0:T(8,128)(2,1)S(1)} %get-tuple-element.44), channel_id=1, source_target_pairs={{0,20},{4,16},{8,28},{12,24},{16,4},{20,0},{24,12},{28,8},{1,21},{... | collective-permute-start | bytes 196616 | tf_op jit(solution)/shard_map/ppermute | solution.py:243
  24.1 12.8 %collective-permute-start.8 = (bf16[128,256]{1,0:T(8,128)(2,1)S(1)}, bf16[128,256]{1,0:T(8,128)(2,1)S(1)}, u32[]{:S(2)}, u32[]{:S(2)}) collective-permute-start(bf16[128,256]{1,0:T(8,128)(2,1)S(1)} %get-tuple-element.45), channel_id=1, source_target_pairs={{0,24},{4,28},{8,16},{12,20},{16,8},{20,12},{24,0},{28,4},{1,25},{... | collective-permute-start | bytes 196616 | tf_op jit(solution)/shard_map/ppermute | solution.py:243
  27.7 9.2 %collective-permute-start.9 = (bf16[128,256]{1,0:T(8,128)(2,1)S(1)}, bf16[128,256]{1,0:T(8,128)(2,1)S(1)}, u32[]{:S(2)}, u32[]{:S(2)}) collective-permute-start(bf16[128,256]{1,0:T(8,128)(2,1)S(1)} %get-tuple-element.46), channel_id=1, source_target_pairs={{0,28},{4,24},{8,20},{12,16},{16,12},{20,8},{24,4},{28,0},{1,29},{... | collective-permute-start | bytes 196616 | tf_op jit(solution)/shard_map/ppermute | solution.py:243
  35.3 12.3 %collective-permute-start.14 = (bf16[256,896]{1,0:T(8,128)(2,1)}, bf16[256,896]{1,0:T(8,128)(2,1)S(1)}, u32[]{:S(2)}, u32[]{:S(2)}) collective-permute-start(bf16[256,896]{1,0:T(8,128)(2,1)} %refs_0_.1), channel_id=1, source_target_pairs={{0,2},{1,3},{2,0},{3,1},{4,6},{5,7},{6,4},{7,5},{8,10},{9,11},{10,... | collective-permute-start | bytes 1376264 | tf_op jit(solution)/shard_map/ppermute | solution.py:243
  36.9 10.8 %collective-permute-start.13 = (bf16[256,896]{1,0:T(8,128)(2,1)}, bf16[256,896]{1,0:T(8,128)(2,1)S(1)}, u32[]{:S(2)}, u32[]{:S(2)}) collective-permute-start(bf16[256,896]{1,0:T(8,128)(2,1)} %refs_0_.1), channel_id=1, source_target_pairs={{0,1},{1,0},{2,3},{3,2},{4,5},{5,4},{6,7},{7,6},{8,9},{9,8},{10,11... | collective-permute-start | bytes 1376264 | tf_op jit(solution)/shard_map/ppermute | solution.py:243
  42.6 8.6 %collective-permute-start.11 = (bf16[256,896]{1,0:T(8,128)(2,1)S(1)}, bf16[256,896]{1,0:T(8,128)(2,1)S(1)}, u32[]{:S(2)}, u32[]{:S(2)}) collective-permute-start(bf16[256,896]{1,0:T(8,128)(2,1)S(1)} %get-tuple-element.51), channel_id=1, source_target_pairs={{0,1},{1,0},{2,3},{3,2},{4,5},{5,4},{6,7},{7,6},{8,9},{9,8},{10,11... | collective-permute-start | bytes 1376264 | tf_op jit(solution)/shard_map/ppermute | solution.py:243
  47.7 5.2 %collective-permute-start.15 = (bf16[256,896]{1,0:T(8,128)(2,1)S(1)}, bf16[256,896]{1,0:T(8,128)(2,1)S(1)}, u32[]{:S(2)}, u32[]{:S(2)}) collective-permute-start(bf16[256,896]{1,0:T(8,128)(2,1)S(1)} %collective-permute-done.14.refs_2_), channel_id=1, source_target_pairs={{0,1},{1,0},{2,3},{3,2},{4,5},{5,4},{6,7},{7,6},{8,9},{9,8},{10,11... | collective-permute-start | bytes 1376264 | tf_op jit(solution)/shard_map/ppermute | solution.py:243
  50.6 28.0 %collective-permute-start.10 = (bf16[256,896]{1,0:T(8,128)(2,1)S(1)}, bf16[256,896]{1,0:T(8,128)(2,1)S(1)}, u32[]{:S(2)}, u32[]{:S(2)}) collective-permute-start(bf16[256,896]{1,0:T(8,128)(2,1)S(1)} %get-tuple-element.49), channel_id=1, source_target_pairs={{0,1},{1,0},{2,3},{3,2},{4,5},{5,4},{6,7},{7,6},{8,9},{9,8},{10,11... | collective-permute-start | bytes 1376264 | tf_op jit(solution)/shard_map/ppermute | solution.py:243
  51.3 27.4 %collective-permute-start.12 = (bf16[256,896]{1,0:T(8,128)(2,1)S(1)}, bf16[256,896]{1,0:T(8,128)(2,1)S(1)}, u32[]{:S(2)}, u32[]{:S(2)}) collective-permute-start(bf16[256,896]{1,0:T(8,128)(2,1)S(1)} %add_convert_fusion.1), channel_id=1, source_target_pairs={{0,2},{1,3},{2,0},{3,1},{4,6},{5,7},{6,4},{7,5},{8,10},{9,11},{10,... | collective-permute-start | bytes 1376264 | tf_op jit(solution)/shard_map/ppermute | solution.py:243
  52.8 24.3 %copy-start.1 = (s32[8,16]{1,0:T(8,128)S(1)}, s32[8,16]{1,0:T(8,128)}, u32[]{:S(2)}) copy-start(s32[8,16]{1,0:T(8,128)} %reads_ref.1) | copy-start | bytes 1540
  58.6 4.3 %collective-permute-start.16 = (bf16[128,256]{1,0:T(8,128)(2,1)S(1)}, bf16[128,256]{1,0:T(8,128)(2,1)S(1)}, u32[]{:S(2)}, u32[]{:S(2)}) collective-permute-start(bf16[128,256]{1,0:T(8,128)(2,1)S(1)} %get-tuple-element.56), channel_id=1, source_target_pairs={{0,4},{4,0},{8,12},{12,8},{16,20},{20,16},{24,28},{28,24},{1,5},{5... | collective-permute-start | bytes 196616 | tf_op jit(solution)/shard_map/ppermute | solution.py:243
  58.7 4.9 %collective-permute-start.17 = (bf16[128,256]{1,0:T(8,128)(2,1)S(1)}, bf16[128,256]{1,0:T(8,128)(2,1)S(1)}, u32[]{:S(2)}, u32[]{:S(2)}) collective-permute-start(bf16[128,256]{1,0:T(8,128)(2,1)S(1)} %get-tuple-element.57), channel_id=1, source_target_pairs={{0,8},{4,12},{8,0},{12,4},{16,24},{20,28},{24,16},{28,20},{1,9},{5... | collective-permute-start | bytes 196616 | tf_op jit(solution)/shard_map/ppermute | solution.py:243
  58.7 6.5 %collective-permute-start.18 = (bf16[128,256]{1,0:T(8,128)(2,1)S(1)}, bf16[128,256]{1,0:T(8,128)(2,1)S(1)}, u32[]{:S(2)}, u32[]{:S(2)}) collective-permute-start(bf16[128,256]{1,0:T(8,128)(2,1)S(1)} %get-tuple-element.58), channel_id=1, source_target_pairs={{0,12},{4,8},{8,4},{12,0},{16,28},{20,24},{24,20},{28,16},{1,13},{... | collective-permute-start | bytes 196616 | tf_op jit(solution)/shard_map/ppermute | solution.py:243
  62.9 7.3 %collective-permute-start.19 = (bf16[128,256]{1,0:T(8,128)(2,1)S(1)}, bf16[128,256]{1,0:T(8,128)(2,1)S(1)}, u32[]{:S(2)}, u32[]{:S(2)}) collective-permute-start(bf16[128,256]{1,0:T(8,128)(2,1)S(1)} %get-tuple-element.59), channel_id=1, source_target_pairs={{0,16},{4,20},{8,24},{12,28},{16,0},{20,4},{24,8},{28,12},{1,17},{... | collective-permute-start | bytes 196616 | tf_op jit(solution)/shard_map/ppermute | solution.py:243
  63.6 8.5 %collective-permute-start.20 = (bf16[128,256]{1,0:T(8,128)(2,1)S(1)}, bf16[128,256]{1,0:T(8,128)(2,1)S(1)}, u32[]{:S(2)}, u32[]{:S(2)}) collective-permute-start(bf16[128,256]{1,0:T(8,128)(2,1)S(1)} %get-tuple-element.60), channel_id=1, source_target_pairs={{0,20},{4,16},{8,28},{12,24},{16,4},{20,0},{24,12},{28,8},{1,21},{... | collective-permute-start | bytes 196616 | tf_op jit(solution)/shard_map/ppermute | solution.py:243
  65.3 6.8 %collective-permute-start.21 = (bf16[128,256]{1,0:T(8,128)(2,1)S(1)}, bf16[128,256]{1,0:T(8,128)(2,1)S(1)}, u32[]{:S(2)}, u32[]{:S(2)}) collective-permute-start(bf16[128,256]{1,0:T(8,128)(2,1)S(1)} %get-tuple-element.61), channel_id=1, source_target_pairs={{0,24},{4,28},{8,16},{12,20},{16,8},{20,12},{24,0},{28,4},{1,25},{... | collective-permute-start | bytes 196616 | tf_op jit(solution)/shard_map/ppermute | solution.py:243
  70.2 7.0 %collective-permute-start.22 = (bf16[128,256]{1,0:T(8,128)(2,1)S(1)}, bf16[128,256]{1,0:T(8,128)(2,1)S(1)}, u32[]{:S(2)}, u32[]{:S(2)}) collective-permute-start(bf16[128,256]{1,0:T(8,128)(2,1)S(1)} %get-tuple-element.62), channel_id=1, source_target_pairs={{0,28},{4,24},{8,20},{12,16},{16,12},{20,8},{24,4},{28,0},{1,29},{... | collective-permute-start | bytes 196616 | tf_op jit(solution)/shard_map/ppermute | solution.py:243
  (3 other events, 19.3 us)
